TPU v7x, 128 devices: a whole 4x4x4 slice. The times are simulated.
128 devices in a mesh: row: 4 (over z), col: 32 (over x, y, core).
Axes of the slice: x: 4, y: 4, z: 4, core: 2. Of those that a mesh axis runs over, the one named last changes fastest.
Arguments:
- star_pos: float32 [512, 3, 128], P(('row', 'col')), may hold values from -5 to 5
- star_vel: float32 [512, 3, 128], P(('row', 'col')), may hold values from -5 to 5
- star_acc: float32 [512, 3, 128], P(('row', 'col')), may hold values from -5 to 5
- star_jerk: float32 [512, 3, 128], P(('row', 'col')), may hold values from -5 to 5
- star_mass: float32 [512, 128], P(('row', 'col')), may hold values from 3.0517578e-05 to 0.00024414062
- active_index: int32 [128, 128], P(('row', 'col')), may hold values from 0 to 511, as said below
- send_block: int32 [128, 128, 4], P(('row', 'col')), may hold values from -1 to 3, as said below
- send_leaf: int32 [128, 128, 4], P(('row', 'col')), may hold values from -1 to 127
- galaxy_pos: float32 [16384, 3, 128], P(('row', 'col')), may hold values from -5 to 5
- galaxy_mass: float32 [16384, 128], P(('row', 'col')), may hold values from 0.0001 to 0.001
Outputs:
- star_pos_new: float32 [512, 3, 128], P(('row', 'col'))
- star_vel_new: float32 [512, 3, 128], P(('row', 'col'))
- galaxy_accel: float32 [16384, 3, 128], P(('row', 'col'))
Inputs may be any that keep to these rules, and one draw needn't show every extreme that they name: `active_index`: the entries of one device's row are distinct. `send_block`: an entry is -1 exactly where the same entry of send_leaf is -1. Every device fills all 4 slots to itself, and one device receives 4 filled slots from every device.
All inputs are finite; a program needn't handle non-finite values.
Results may differ from a plain program's by a relative error of at most 0.0003.
Values sent between devices are 32-bit elements; how exact they have to be, the bound alone decides.
No kernel may reach another device: no remote copies, remote signals or barrier semaphores. Data moves between devices by JAX's collectives and lax.ppermute only.
A program may use at most 64 MiB of HBM per device.

v0:
```python
import math

import jax
import jax.numpy as jnp
from jax import lax
from jax.sharding import PartitionSpec as P

STAR_DEV = 512
BLOCK = 128


step_length = 1.0
soft_star = 0.01
soft_galaxy = 0.04


def gather_turned(arrays, axis, dims):
    turned = [jnp.moveaxis(a, dim, 0) for a, dim in zip(arrays, dims)]
    widths = [t[0].size for t in turned]
    both = jnp.concatenate([t.reshape(-1, w) for t, w in zip(turned, widths)], axis=1)
    out = lax.all_gather(both, axis, axis=0, tiled=True)
    parts = jnp.split(out, [sum(widths[:k]) for k in range(1, len(widths))], axis=1)
    return tuple(
        (
            jnp.moveaxis(b.reshape(-1, *t.shape[1:]), 0, dim)
            for b, t, dim in zip(parts, turned, dims)
        )
    )


def joined_along(parts, dim):
    shape = list(parts.shape[1:])
    shape[dim] *= parts.shape[0]
    return jnp.moveaxis(parts, 0, dim).reshape(shape)


def copy_for_each(x, axis):
    peers = lax.axis_size(axis)
    return lax.all_to_all(jnp.broadcast_to(x[None], (peers, *x.shape)), axis, 0, 0, tiled=True)


def gathered_copies(x, axis, dim):
    return joined_along(copy_for_each(x, axis), dim)


def cut_along(x, dim, peers):
    shape = x.shape
    parts = x.reshape(*shape[:dim], peers, shape[dim] // peers, *shape[dim + 1 :])
    return jnp.moveaxis(parts, dim, 0)


def sent_and_summed(x, axis, dim):
    parts = cut_along(x, dim, lax.axis_size(axis))
    arrived = lax.all_to_all(parts, axis, split_axis=0, concat_axis=0, tiled=True)
    return arrived.sum(axis=0)


def exchange_both(x, axis, axes, splits, concats):
    sizes = [lax.axis_size(a) for a in axes]
    parts = cut_along(x, splits[0], sizes[0])
    parts = jnp.moveaxis(cut_along(parts, splits[1] + 1, sizes[1]), 0, 1)
    inside = parts.shape[2:]
    parts = parts.reshape(-1, *inside)
    parts = lax.all_to_all(parts, axis, split_axis=0, concat_axis=0, tiled=True)
    parts = joined_along(parts.reshape(*sizes, *inside), concats[0] + 1)
    return joined_along(parts, concats[1])


def pair_block(apos, avel, rpos, rvel, rmass):
    delta = rpos[:, None, :] - apos[:, :, None]
    dvel = rvel[:, None, :] - avel[:, :, None]
    radius = jnp.sum(delta * delta, 0) + soft_star
    inverse = lax.rsqrt(radius)
    weight = rmass[None, :] * inverse * inverse * inverse
    along = jnp.sum(delta * dvel, 0) * inverse * inverse
    accel = jnp.sum(delta * weight[None], -1)
    jerks = jnp.sum((dvel - 3.0 * along[None] * delta) * weight[None], -1)
    return (accel, jerks)


def pair_terms(piece, rpos, rvel, rmass):
    count = piece.shape[1]
    size = math.gcd(count, 512)
    grouped = piece.reshape(6, count // size, size).transpose(1, 0, 2)

    def pair_one(item):
        accel, jerks = pair_block(item[:3], item[3:], rpos, rvel, rmass)
        return jnp.concatenate([accel, jerks], 0)

    result = lax.map(pair_one, grouped)
    return result.transpose(1, 0, 2).reshape(6, count)


def entry_terms(stars4, leaves4):
    count = stars4.shape[0]
    group = math.gcd(count, 16)

    def entry_one(item):
        spos = item[0][:, :3]
        smass = item[0][:, 3]
        gpos = item[1][:, :3]
        gmass = item[1][:, 3]
        delta = gpos[:, :, None, :] - spos[:, :, :, None]
        radius = jnp.sum(delta * delta, 1) + soft_galaxy
        inverse = lax.rsqrt(radius)
        cube = inverse * inverse * inverse
        kick = jnp.sum(delta * (gmass[:, None, :] * cube)[:, None], -1)
        pull = -jnp.sum(delta * (smass[:, :, None] * cube)[:, None], 2)
        return (pull, kick)

    shaped = (
        stars4.reshape((count // group, group) + stars4.shape[1:]),
        leaves4.reshape((count // group, group) + leaves4.shape[1:]),
    )
    pull, kick = lax.map(entry_one, shaped)
    return (pull.reshape((count,) + pull.shape[2:]), kick.reshape((count,) + kick.shape[2:]))


def flatten(blocks):
    return blocks.transpose(1, 0, 2).reshape(3, -1)


def local(
    star_pos,
    star_vel,
    star_acc,
    star_jerk,
    star_mass,
    active_index,
    send_block,
    send_leaf,
    galaxy_pos,
    galaxy_mass,
):
    nblock = star_pos.shape[0]
    width = star_pos.shape[2]
    half = 0.5 * step_length**2
    sixth = step_length**3 / 6.0
    pred_pos = star_pos + step_length * star_vel + half * star_acc + sixth * star_jerk
    pred_vel = star_vel + step_length * star_acc + half * star_jerk
    pos_flat = flatten(pred_pos)
    vel_flat = flatten(pred_vel)
    mass_flat = star_mass.reshape(-1)
    chosen = active_index[0]
    active = jnp.concatenate([pos_flat[:, chosen], vel_flat[:, chosen]], 0)
    res_pos, res_vel, res_mass = gather_turned((pos_flat, vel_flat, mass_flat), "row", (1, 1, 0))
    terms = pair_terms(gathered_copies(active, "col", 1), res_pos, res_vel, res_mass)
    forces = sent_and_summed(terms, "col", 1)
    acc_new = forces[:3]
    jerk_new = forces[3:]
    start_acc = flatten(star_acc)[:, chosen]
    start_jerk = flatten(star_jerk)[:, chosen]
    start_pos = flatten(star_pos)[:, chosen]
    start_vel = flatten(star_vel)[:, chosen]
    vel_one = (
        start_vel
        + (start_acc + acc_new) * (0.5 * step_length)
        + (start_jerk - jerk_new) * (step_length**2 / 12.0)
    )
    pos_one = (
        start_pos
        + (start_vel + vel_one) * (0.5 * step_length)
        + (start_acc - acc_new) * (step_length**2 / 12.0)
    )
    pos_new = pos_flat.at[:, chosen].set(pos_one).reshape(3, nblock, width).transpose(1, 0, 2)
    vel_mid = vel_flat.at[:, chosen].set(vel_one).reshape(3, nblock, width).transpose(1, 0, 2)
    table = send_block[0]
    targets = table.shape[0]
    slots = table.shape[1]
    entries = targets * slots
    pick = (
        (table[:, :, None] == jnp.arange(nblock, dtype=jnp.int32))
        .astype(jnp.float32)
        .reshape(entries, nblock)
    )
    packed = jnp.concatenate([pos_new, star_mass[:, None, :]], 1).reshape(nblock, -1)
    outgoing = jnp.dot(
        pick, packed, precision=lax.Precision.HIGHEST, preferred_element_type=jnp.float32
    )
    outgoing = outgoing.reshape(targets, slots, 4, width)
    rows = lax.axis_size("row")
    cols = lax.axis_size("col")
    arrived, arrived_leaf = (
        exchange_both(
            outgoing.reshape(rows, cols, slots, 4, width),
            ("row", "col"),
            ("row", "col"),
            (0, 1),
            (0, 1),
        ),
        exchange_both(
            send_leaf[0].reshape(rows, cols, slots), ("row", "col"), ("row", "col"), (0, 1), (0, 1)
        ),
    )
    leaves = galaxy_pos.shape[0]
    depth = galaxy_pos.shape[2]
    grab = (arrived_leaf.reshape(entries)[:, None] == jnp.arange(leaves, dtype=jnp.int32)).astype(
        jnp.float32
    )
    packed_gal = jnp.concatenate([galaxy_pos, galaxy_mass[:, None, :]], 1).reshape(leaves, -1)
    local_leaves = jnp.dot(
        grab, packed_gal, precision=lax.Precision.HIGHEST, preferred_element_type=jnp.float32
    )
    pull, kick = entry_terms(
        arrived.reshape(entries, 4, width), local_leaves.reshape(entries, 4, depth)
    )
    pull_total = lax.dot_general(
        grab,
        pull.reshape(entries, -1),
        (((0,), (0,)), ((), ())),
        precision=lax.Precision.HIGHEST,
        preferred_element_type=jnp.float32,
    )
    galaxy_accel = pull_total.reshape(leaves, 3, depth) * (STAR_DEV * rows * cols / BLOCK)
    returned = exchange_both(
        kick.reshape(rows, cols, slots, 3, width), ("row", "col"), ("row", "col"), (0, 1), (0, 1)
    )
    kick_blocks = lax.dot_general(
        pick,
        returned.reshape(entries, -1),
        (((0,), (0,)), ((), ())),
        precision=lax.Precision.HIGHEST,
        preferred_element_type=jnp.float32,
    )
    star_vel_new = vel_mid + step_length * kick_blocks.reshape(nblock, 3, width)
    return (pos_new, star_vel_new, galaxy_accel)


def solution(mesh):
    return jax.shard_map(
        local,
        mesh=mesh,
        in_specs=(
            P(("row", "col"), None, None),
            P(("row", "col"), None, None),
            P(("row", "col"), None, None),
            P(("row", "col"), None, None),
            P(("row", "col"), None),
            P(("row", "col"), None),
            P(("row", "col"), None, None),
            P(("row", "col"), None, None),
            P(("row", "col"), None, None),
            P(("row", "col"), None),
        ),
        out_specs=(
            P(("row", "col"), None, None),
            P(("row", "col"), None, None),
            P(("row", "col"), None, None),
        ),
        check_vma=False,
    )
```

profile of v0, /device:TPU:1, one launch (start us, length us, event | category | flops | bytes accessed | tf_op | source)
XLA Modules:
  0.0 325.6 jit_solution(6353200224879167708)
XLA Ops:
  4.5 8.6 %all-to-all-start = ((f32[32,6,128]{2,1,0:T(8,128)}), f32[32,6,128]{2,1,0:T(8,128)S(1)}, u32[]{:S(2)}, u32[]{:S(2)}) async-start(f32[32,6,128]{2,1,0:T(8,128)} %broadcast_in_dim.24), calls=%async_computation | async-start | bytes 262144 | tf_op jit(solution)/shard_map/all_to_all | solution.py:39
  14.0 11.0 %all_gather.3 = f32[2048,7]{0,1:T(8,128)S(1)} all-gather(f32[512,7]{0,1:T(8,128)S(1)} %pad_maximum_fusion), channel_id=1, replica_groups=mesh['row'=4,'col'=32] {'row'}, dimensions={0}, use_global_device_ids=true | all-gather | bytes 71680 | tf_op jit(solution)/shard_map/all_gather | solution.py:21
  25.1 85.4 %while.22 = (s32[]{:T(128)}, f32[8,6,512]{2,1,0:T(8,128)S(1)}, f32[3,2048]{1,0:T(4,128)S(1)}, f32[8,6,512]{2,1,0:T(8,128)S(1)}, f32[2048,1]{0,1:T(1,128)S(1)}, /...) while((s32[]{:T(128)}, f32[8,6,512]{2,1,0:T(8,128)S(1)}, f32[3,2048]{1,0:T(4,128)S(1)}, ...), condition=%wide.region_5.6_spmd, body=%wide.region_0.5_spmd.sunk | while | flops 49283072 | bytes 33755252 | solution.py:90
  25.1 4.0 %fusion.51 = (f32[512,2048]{1,0:T(8,128)S(1)}, f32[512,2048]{1,0:T(8,128)S(1)}) fusion(f32[3,512]{1,0:T(4,128)S(1)} %get-tuple-element.238, f32[3,2048]{1,0:T(4,128)S(1)} %get-tuple-element.277, f32[3,512]{1,0:T(4,128)S(1)} %get-tuple-element.239, f32[3,2048]{1,0:T(4,128)S(1)} %get-tuple-element.280), kind=kLoop, calls=%fused_computation.15.clone.1 | loop fusion | flops 16777216 | bytes 8450048 | tf_op jit(solution)/shard_map/while/body/eval_jaxpr/reduce_sum | solution.py:72
  29.1 1.9 fusion.52
  31.1 4.7 %fusion.53 = (f32[3,512]{1,0:T(4,128)S(1)}, f32[3,512]{1,0:T(4,128)S(1)}) fusion(f32[512,2048]{1,0:T(8,128)S(1)} %get-tuple-element.242, f32[3,512]{1,0:T(4,128)S(1)} %get-tuple-element.238, f32[3,2048]{1,0:T(4,128)S(1)} %get-tuple-element.277, f32[512,2048]{1,0:T(8,128)S(1)} %get-tuple-element.243, f32[3,512]{1,0:T(4,128)S(1)} %get-tuple-element.239, ...), kind=kLoop, calls=%fused_computation.16.clone.1 | loop fusion | flops 25162752 | bytes 8462336 | tf_op jit(solution)/shard_map/while/body/eval_jaxpr/reduce_sum | solution.py:76
  35.8 4.0 %fusion.51 = (f32[512,2048]{1,0:T(8,128)S(1)}, f32[512,2048]{1,0:T(8,128)S(1)}) fusion(f32[3,512]{1,0:T(4,128)S(1)} %get-tuple-element.238, f32[3,2048]{1,0:T(4,128)S(1)} %get-tuple-element.277, f32[3,512]{1,0:T(4,128)S(1)} %get-tuple-element.239, f32[3,2048]{1,0:T(4,128)S(1)} %get-tuple-element.280), kind=kLoop, calls=%fused_computation.15.clone.1 | loop fusion | flops 16777216 | bytes 8450048 | tf_op jit(solution)/shard_map/while/body/eval_jaxpr/reduce_sum | solution.py:72
  41.7 4.7 %fusion.53 = (f32[3,512]{1,0:T(4,128)S(1)}, f32[3,512]{1,0:T(4,128)S(1)}) fusion(f32[512,2048]{1,0:T(8,128)S(1)} %get-tuple-element.242, f32[3,512]{1,0:T(4,128)S(1)} %get-tuple-element.238, f32[3,2048]{1,0:T(4,128)S(1)} %get-tuple-element.277, f32[512,2048]{1,0:T(8,128)S(1)} %get-tuple-element.243, f32[3,512]{1,0:T(4,128)S(1)} %get-tuple-element.239, ...), kind=kLoop, calls=%fused_computation.16.clone.1 | loop fusion | flops 25162752 | bytes 8462336 | tf_op jit(solution)/shard_map/while/body/eval_jaxpr/reduce_sum | solution.py:76
  46.5 4.0 %fusion.51 = (f32[512,2048]{1,0:T(8,128)S(1)}, f32[512,2048]{1,0:T(8,128)S(1)}) fusion(f32[3,512]{1,0:T(4,128)S(1)} %get-tuple-element.238, f32[3,2048]{1,0:T(4,128)S(1)} %get-tuple-element.277, f32[3,512]{1,0:T(4,128)S(1)} %get-tuple-element.239, f32[3,2048]{1,0:T(4,128)S(1)} %get-tuple-element.280), kind=kLoop, calls=%fused_computation.15.clone.1 | loop fusion | flops 16777216 | bytes 8450048 | tf_op jit(solution)/shard_map/while/body/eval_jaxpr/reduce_sum | solution.py:72
  50.5 1.9 fusion.52
  52.4 4.7 %fusion.53 = (f32[3,512]{1,0:T(4,128)S(1)}, f32[3,512]{1,0:T(4,128)S(1)}) fusion(f32[512,2048]{1,0:T(8,128)S(1)} %get-tuple-element.242, f32[3,512]{1,0:T(4,128)S(1)} %get-tuple-element.238, f32[3,2048]{1,0:T(4,128)S(1)} %get-tuple-element.277, f32[512,2048]{1,0:T(8,128)S(1)} %get-tuple-element.243, f32[3,512]{1,0:T(4,128)S(1)} %get-tuple-element.239, ...), kind=kLoop, calls=%fused_computation.16.clone.1 | loop fusion | flops 25162752 | bytes 8462336 | tf_op jit(solution)/shard_map/while/body/eval_jaxpr/reduce_sum | solution.py:76
  57.2 4.0 %fusion.51 = (f32[512,2048]{1,0:T(8,128)S(1)}, f32[512,2048]{1,0:T(8,128)S(1)}) fusion(f32[3,512]{1,0:T(4,128)S(1)} %get-tuple-element.238, f32[3,2048]{1,0:T(4,128)S(1)} %get-tuple-element.277, f32[3,512]{1,0:T(4,128)S(1)} %get-tuple-element.239, f32[3,2048]{1,0:T(4,128)S(1)} %get-tuple-element.280), kind=kLoop, calls=%fused_computation.15.clone.1 | loop fusion | flops 16777216 | bytes 8450048 | tf_op jit(solution)/shard_map/while/body/eval_jaxpr/reduce_sum | solution.py:72
  63.1 4.7 %fusion.53 = (f32[3,512]{1,0:T(4,128)S(1)}, f32[3,512]{1,0:T(4,128)S(1)}) fusion(f32[512,2048]{1,0:T(8,128)S(1)} %get-tuple-element.242, f32[3,512]{1,0:T(4,128)S(1)} %get-tuple-element.238, f32[3,2048]{1,0:T(4,128)S(1)} %get-tuple-element.277, f32[512,2048]{1,0:T(8,128)S(1)} %get-tuple-element.243, f32[3,512]{1,0:T(4,128)S(1)} %get-tuple-element.239, ...), kind=kLoop, calls=%fused_computation.16.clone.1 | loop fusion | flops 25162752 | bytes 8462336 | tf_op jit(solution)/shard_map/while/body/eval_jaxpr/reduce_sum | solution.py:76
  67.9 4.0 %fusion.51 = (f32[512,2048]{1,0:T(8,128)S(1)}, f32[512,2048]{1,0:T(8,128)S(1)}) fusion(f32[3,512]{1,0:T(4,128)S(1)} %get-tuple-element.238, f32[3,2048]{1,0:T(4,128)S(1)} %get-tuple-element.277, f32[3,512]{1,0:T(4,128)S(1)} %get-tuple-element.239, f32[3,2048]{1,0:T(4,128)S(1)} %get-tuple-element.280), kind=kLoop, calls=%fused_computation.15.clone.1 | loop fusion | flops 16777216 | bytes 8450048 | tf_op jit(solution)/shard_map/while/body/eval_jaxpr/reduce_sum | solution.py:72
  71.8 1.9 fusion.52
  73.8 4.7 %fusion.53 = (f32[3,512]{1,0:T(4,128)S(1)}, f32[3,512]{1,0:T(4,128)S(1)}) fusion(f32[512,2048]{1,0:T(8,128)S(1)} %get-tuple-element.242, f32[3,512]{1,0:T(4,128)S(1)} %get-tuple-element.238, f32[3,2048]{1,0:T(4,128)S(1)} %get-tuple-element.277, f32[512,2048]{1,0:T(8,128)S(1)} %get-tuple-element.243, f32[3,512]{1,0:T(4,128)S(1)} %get-tuple-element.239, ...), kind=kLoop, calls=%fused_computation.16.clone.1 | loop fusion | flops 25162752 | bytes 8462336 | tf_op jit(solution)/shard_map/while/body/eval_jaxpr/reduce_sum | solution.py:76
  78.5 4.0 %fusion.51 = (f32[512,2048]{1,0:T(8,128)S(1)}, f32[512,2048]{1,0:T(8,128)S(1)}) fusion(f32[3,512]{1,0:T(4,128)S(1)} %get-tuple-element.238, f32[3,2048]{1,0:T(4,128)S(1)} %get-tuple-element.277, f32[3,512]{1,0:T(4,128)S(1)} %get-tuple-element.239, f32[3,2048]{1,0:T(4,128)S(1)} %get-tuple-element.280), kind=kLoop, calls=%fused_computation.15.clone.1 | loop fusion | flops 16777216 | bytes 8450048 | tf_op jit(solution)/shard_map/while/body/eval_jaxpr/reduce_sum | solution.py:72
  84.4 4.7 %fusion.53 = (f32[3,512]{1,0:T(4,128)S(1)}, f32[3,512]{1,0:T(4,128)S(1)}) fusion(f32[512,2048]{1,0:T(8,128)S(1)} %get-tuple-element.242, f32[3,512]{1,0:T(4,128)S(1)} %get-tuple-element.238, f32[3,2048]{1,0:T(4,128)S(1)} %get-tuple-element.277, f32[512,2048]{1,0:T(8,128)S(1)} %get-tuple-element.243, f32[3,512]{1,0:T(4,128)S(1)} %get-tuple-element.239, ...), kind=kLoop, calls=%fused_computation.16.clone.1 | loop fusion | flops 25162752 | bytes 8462336 | tf_op jit(solution)/shard_map/while/body/eval_jaxpr/reduce_sum | solution.py:76
  89.2 4.0 %fusion.51 = (f32[512,2048]{1,0:T(8,128)S(1)}, f32[512,2048]{1,0:T(8,128)S(1)}) fusion(f32[3,512]{1,0:T(4,128)S(1)} %get-tuple-element.238, f32[3,2048]{1,0:T(4,128)S(1)} %get-tuple-element.277, f32[3,512]{1,0:T(4,128)S(1)} %get-tuple-element.239, f32[3,2048]{1,0:T(4,128)S(1)} %get-tuple-element.280), kind=kLoop, calls=%fused_computation.15.clone.1 | loop fusion | flops 16777216 | bytes 8450048 | tf_op jit(solution)/shard_map/while/body/eval_jaxpr/reduce_sum | solution.py:72
  95.1 4.7 %fusion.53 = (f32[3,512]{1,0:T(4,128)S(1)}, f32[3,512]{1,0:T(4,128)S(1)}) fusion(f32[512,2048]{1,0:T(8,128)S(1)} %get-tuple-element.242, f32[3,512]{1,0:T(4,128)S(1)} %get-tuple-element.238, f32[3,2048]{1,0:T(4,128)S(1)} %get-tuple-element.277, f32[512,2048]{1,0:T(8,128)S(1)} %get-tuple-element.243, f32[3,512]{1,0:T(4,128)S(1)} %get-tuple-element.239, ...), kind=kLoop, calls=%fused_computation.16.clone.1 | loop fusion | flops 25162752 | bytes 8462336 | tf_op jit(solution)/shard_map/while/body/eval_jaxpr/reduce_sum | solution.py:76
  99.9 4.0 %fusion.51 = (f32[512,2048]{1,0:T(8,128)S(1)}, f32[512,2048]{1,0:T(8,128)S(1)}) fusion(f32[3,512]{1,0:T(4,128)S(1)} %get-tuple-element.238, f32[3,2048]{1,0:T(4,128)S(1)} %get-tuple-element.277, f32[3,512]{1,0:T(4,128)S(1)} %get-tuple-element.239, f32[3,2048]{1,0:T(4,128)S(1)} %get-tuple-element.280), kind=kLoop, calls=%fused_computation.15.clone.1 | loop fusion | flops 16777216 | bytes 8450048 | tf_op jit(solution)/shard_map/while/body/eval_jaxpr/reduce_sum | solution.py:72
  105.8 4.7 %fusion.53 = (f32[3,512]{1,0:T(4,128)S(1)}, f32[3,512]{1,0:T(4,128)S(1)}) fusion(f32[512,2048]{1,0:T(8,128)S(1)} %get-tuple-element.242, f32[3,512]{1,0:T(4,128)S(1)} %get-tuple-element.238, f32[3,2048]{1,0:T(4,128)S(1)} %get-tuple-element.277, f32[512,2048]{1,0:T(8,128)S(1)} %get-tuple-element.243, f32[3,512]{1,0:T(4,128)S(1)} %get-tuple-element.239, ...), kind=kLoop, calls=%fused_computation.16.clone.1 | loop fusion | flops 25162752 | bytes 8462336 | tf_op jit(solution)/shard_map/while/body/eval_jaxpr/reduce_sum | solution.py:76
  111.4 9.5 %all-to-all-start.1 = ((f32[32,6,128]{2,1,0:T(8,128)}), f32[32,6,128]{2,1,0:T(8,128)S(1)}, u32[]{:S(2)}, u32[]{:S(2)}) async-start(f32[32,6,128]{2,1,0:T(8,128)} %copy.206), calls=%async_computation.1 | async-start | bytes 262144 | tf_op jit(solution)/shard_map/all_to_all | solution.py:54
  125.1 3.4 %all-to-all-done.1 = f32[32,6,128]{2,1,0:T(8,128)S(1)} async-done(((f32[32,6,128]{2,1,0:T(8,128)}), f32[32,6,128]{2,1,0:T(8,128)S(1)}, u32[]{:S(2)}, u32[]{:S(2)}) %all-to-all-start.1) | async-done | bytes 98336 | tf_op jit(solution)/shard_map/all_to_all | solution.py:54
  128.5 5.7 %all-to-all-start.2 = ((s32[128,1,1,4]{3,2,1,0:T(1,128)}), s32[128,1,1,4]{3,2,1,0:T(1,128)S(1)}, u32[]{:S(2)}, u32[]{:S(2)}) async-start(s32[128,1,1,4]{3,2,1,0:T(1,128)} %bitcast.47), calls=%async_computation.2 | async-start | bytes 131072 | tf_op jit(solution)/shard_map/all_to_all | solution.py:64
  137.9 6.0 %all-to-all-done.2 = s32[128,1,1,4]{3,2,1,0:T(1,128)S(1)} async-done(((s32[128,1,1,4]{3,2,1,0:T(1,128)}), s32[128,1,1,4]{3,2,1,0:T(1,128)S(1)}, u32[]{:S(2)}, u32[]{:S(2)}) %all-to-all-start.2) | async-done | bytes 2080 | tf_op jit(solution)/shard_map/all_to_all | solution.py:64
  143.9 4.4 %all-to-all-start.3 = ((f32[128,1,1,4,4,128]{5,4,3,2,1,0:T(4,128)}), f32[128,1,1,4,4,128]{5,4,3,2,1,0:T(4,128)S(1)}, u32[]{:S(2)}, u32[]{:S(2)}) async-start(f32[128,1,1,4,4,128]{5,4,3,2,1,0:T(4,128)} %copy.218), calls=%async_computation.3 | async-start | bytes 2097152 | tf_op jit(solution)/shard_map/all_to_all | solution.py:64
  149.3 17.8 %all-to-all-done.3 = f32[128,1,1,4,4,128]{5,4,3,2,1,0:T(4,128)S(1)} async-done(((f32[128,1,1,4,4,128]{5,4,3,2,1,0:T(4,128)}), f32[128,1,1,4,4,128]{5,4,3,2,1,0:T(4,128)S(1)}, u32[]{:S(2)}, u32[]{:S(2)}) %all-to-all-start.3) | async-done | bytes 1048608 | tf_op jit(solution)/shard_map/all_to_all | solution.py:64
  167.4 133.1 %while.23 = (s32[]{:T(128)}, f32[32,16,3,128]{3,2,1,0:T(4,128)}, f32[32,16,3,128]{3,2,1,0:T(4,128)}, f32[32,16,4,128]{3,1,2,0:T(8,128)S(1)}, f32[32,16,4,128]{3,1,0,2:T(8,128)S(1)}, /*index=5*/s32[]{:T(128)}) while((s32[]{:T(128)}, f32[32,16,3,128]{3,2,1,0:T(4,128)}, f32[32,16,3,128]{3,2,1,0:T(4,128)}, f32[32,16,4,128]{3,1,2,0:T(8,128)S(1)}, ...), condition=%wide.region_13.14_spmd, body=%wide.region_9.13_spmd.sunk | while | flops 7333890 | bytes 6931021 | solution.py:115
  168.9 2.0 fusion.57
  173.1 2.0 fusion.57
  177.2 2.0 fusion.57
  181.4 2.0 fusion.57
  185.6 2.0 fusion.57
  189.7 2.0 fusion.57
  193.9 2.0 fusion.57
  198.0 2.0 fusion.57
  202.2 2.0 fusion.57
  206.3 2.0 fusion.57
  210.5 2.0 fusion.57
  214.6 2.0 fusion.57
  218.8 2.0 fusion.57
  223.0 2.0 fusion.57
  227.1 2.0 fusion.57
  231.3 2.0 fusion.57
  235.4 2.0 fusion.57
  239.6 2.0 fusion.57
  243.8 2.0 fusion.57
  247.9 2.0 fusion.57
  252.1 2.0 fusion.57
  256.2 2.0 fusion.57
  260.4 2.0 fusion.57
  264.6 2.0 fusion.57
  268.7 2.0 fusion.57
  272.9 2.0 fusion.57
  277.0 2.0 fusion.57
  281.2 2.0 fusion.57
  285.4 2.0 fusion.57
  289.5 2.0 fusion.57
  293.7 2.0 fusion.57
  297.8 2.0 fusion.57
  300.4 2.3 copy.222
  302.8 4.8 %all-to-all-start.4 = ((f32[128,1,1,4,3,128]{5,3,4,2,1,0:T(4,128)}), f32[128,1,1,4,3,128]{5,3,4,2,1,0:T(4,128)S(1)}, u32[]{:S(2)}, u32[]{:S(2)}) async-start(f32[128,1,1,4,3,128]{5,3,4,2,1,0:T(4,128)} %copy.222), calls=%async_computation.4 | async-start | bytes 1572864 | tf_op jit(solution)/shard_map/all_to_all | solution.py:64
  311.9 11.9 %all-to-all-done.4 = f32[128,1,1,4,3,128]{5,3,4,2,1,0:T(4,128)S(1)} async-done(((f32[128,1,1,4,3,128]{5,3,4,2,1,0:T(4,128)}), f32[128,1,1,4,3,128]{5,3,4,2,1,0:T(4,128)S(1)}, u32[]{:S(2)}, u32[]{:S(2)}) %all-to-all-start.4) | async-done | bytes 786464 | tf_op jit(solution)/shard_map/all_to_all | solution.py:64
  (454 shorter events, 99.0 us)
Async XLA Ops:
  4.5 20.5 %all-to-all-start = ((f32[32,6,128]{2,1,0:T(8,128)}), f32[32,6,128]{2,1,0:T(8,128)S(1)}, u32[]{:S(2)}, u32[]{:S(2)}) async-start(f32[32,6,128]{2,1,0:T(8,128)} %broadcast_in_dim.24), calls=%async_computation | async-start | bytes 262144 | tf_op jit(solution)/shard_map/all_to_all | solution.py:39
  25.0 95.8 %copy-start.3 = (f32[4,3,128]{2,0,1:T(4,128)S(1)}, f32[4,3,128]{2,0,1:T(4,128)}, u32[]{:S(2)}) copy-start(f32[4,3,128]{2,0,1:T(4,128)} %param.14) | copy-start | bytes 18436
  25.0 96.7 %copy-start.4 = (f32[4,3,128]{2,0,1:T(4,128)S(1)}, f32[4,3,128]{2,0,1:T(4,128)}, u32[]{:S(2)}) copy-start(f32[4,3,128]{2,0,1:T(4,128)} %param.15) | copy-start | bytes 18436
  25.1 97.6 %copy-start.5 = (f32[4,3,128]{2,0,1:T(4,128)S(1)}, f32[4,3,128]{2,0,1:T(4,128)}, u32[]{:S(2)}) copy-start(f32[4,3,128]{2,0,1:T(4,128)} %param.16) | copy-start | bytes 18436
  25.1 98.4 %copy-start.6 = (f32[4,3,128]{2,0,1:T(4,128)S(1)}, f32[4,3,128]{2,0,1:T(4,128)}, u32[]{:S(2)}) copy-start(f32[4,3,128]{2,0,1:T(4,128)} %param.17) | copy-start | bytes 18436
  25.1 99.3 %copy-start.9 = (s32[1,128,4]{1,2,0:T(4,128)S(1)}, s32[1,128,4]{1,2,0:T(4,128)}, u32[]{:S(2)}) copy-start(s32[1,128,4]{1,2,0:T(4,128)} %param.21) | copy-start | bytes 6148
  25.1 110.4 %copy-start.7 = (f32[4,128]{1,0:T(4,128)S(1)}, f32[4,128]{1,0:T(4,128)}, u32[]{:S(2)}) copy-start(f32[4,128]{1,0:T(4,128)} %param.18) | copy-start | bytes 6148
  25.1 110.4 %copy-start.8 = (s32[1,128,4]{1,2,0:T(4,128)S(1)}, s32[1,128,4]{1,2,0:T(4,128)}, u32[]{:S(2)}) copy-start(s32[1,128,4]{1,2,0:T(4,128)} %param.20) | copy-start | bytes 6148
  110.5 37.8 %copy-start = (f32[128,3,128]{2,0,1:T(8,128)S(1)}, f32[128,3,128]{2,0,1:T(8,128)}, u32[]{:S(2)}) copy-start(f32[128,3,128]{2,0,1:T(8,128)} %param.22) | copy-start | bytes 589828
  110.6 37.8 %copy-start.1 = (f32[128,128]{1,0:T(8,128)S(1)}, f32[128,128]{1,0:T(8,128)}, u32[]{:S(2)}) copy-start(f32[128,128]{1,0:T(8,128)} %param.23) | copy-start | bytes 196612
  111.4 17.2 %all-to-all-start.1 = ((f32[32,6,128]{2,1,0:T(8,128)}), f32[32,6,128]{2,1,0:T(8,128)S(1)}, u32[]{:S(2)}, u32[]{:S(2)}) async-start(f32[32,6,128]{2,1,0:T(8,128)} %copy.206), calls=%async_computation.1 | async-start | bytes 262144 | tf_op jit(solution)/shard_map/all_to_all | solution.py:54
  128.5 15.3 %all-to-all-start.2 = ((s32[128,1,1,4]{3,2,1,0:T(1,128)}), s32[128,1,1,4]{3,2,1,0:T(1,128)S(1)}, u32[]{:S(2)}, u32[]{:S(2)}) async-start(s32[128,1,1,4]{3,2,1,0:T(1,128)} %bitcast.47), calls=%async_computation.2 | async-start | bytes 131072 | tf_op jit(solution)/shard_map/all_to_all | solution.py:64
  135.5 31.8 %copy-start.2 = (f32[3,4,128]{2,1,0:T(4,128)}, f32[3,4,128]{2,1,0:T(4,128)S(1)}, u32[]{:S(2)}) copy-start(f32[3,4,128]{2,1,0:T(4,128)S(1)} %copy.211) | copy-start | bytes 18436
  143.9 23.2 %all-to-all-start.3 = ((f32[128,1,1,4,4,128]{5,4,3,2,1,0:T(4,128)}), f32[128,1,1,4,4,128]{5,4,3,2,1,0:T(4,128)S(1)}, u32[]{:S(2)}, u32[]{:S(2)}) async-start(f32[128,1,1,4,4,128]{5,4,3,2,1,0:T(4,128)} %copy.218), calls=%async_computation.3 | async-start | bytes 2097152 | tf_op jit(solution)/shard_map/all_to_all | solution.py:64
  302.8 21.1 %all-to-all-start.4 = ((f32[128,1,1,4,3,128]{5,3,4,2,1,0:T(4,128)}), f32[128,1,1,4,3,128]{5,3,4,2,1,0:T(4,128)S(1)}, u32[]{:S(2)}, u32[]{:S(2)}) async-start(f32[128,1,1,4,3,128]{5,3,4,2,1,0:T(4,128)} %copy.222), calls=%async_computation.4 | async-start | bytes 1572864 | tf_op jit(solution)/shard_map/all_to_all | solution.py:64
where the time goes:
time: 326 us
  other arithmetic  216 us (66%)
  waiting for transfers between devices  39.1 us (12%)
  starting transfers between devices  33 us (10%)
  local copies, waits for them, and re-layouts  19.3 us (6%)
  blocking collectives  11 us (3%)
  matrix products  3.58 us (1%)
    reduce_sum x32, other arithmetic, entry_one(): kick = jnp.sum(delta * (gmass[:, None, :] * cube)[:, None], -1)  62.5 us
    reduce_sum x8, other arithmetic, pair_block(): accel = jnp.sum(delta * weight[None], -1)  37.6 us
    all_to_all x3, waiting for transfers between devices, exchange_both(): parts = lax.all_to_all(parts, axis, split_axis=0, concat_axis=0, tiled=True)  35.7 us
    reduce_sum x32, other arithmetic, entry_one(): radius = jnp.sum(delta * delta, 1) + soft_galaxy  33.2 us
    reduce_sum x8, other arithmetic, pair_block(): radius = jnp.sum(delta * delta, 0) + soft_star  31.7 us
    dynamic_update_slice x32, other arithmetic, entry_terms(): pull, kick = lax.map(entry_one, shaped)  20.7 us
    mul x8, other arithmetic, pair_block(): jerks = jnp.sum((dvel - 3.0 * along[None] * delta) * weight[None], -1)  15.5 us
    all_to_all x3, starting transfers between devices, exchange_both(): parts = lax.all_to_all(parts, axis, split_axis=0, concat_axis=0, tiled=True)  14.9 us
  transfers between devices with their start and end apart: 5, of which 4 were waited for; matrix products, arithmetic and copies ran while one was open for 4% of the time, Pallas kernels for 0%

commit v1 on v0

v1 whole, which is shorter than its diff:
```python
import functools

import jax
import jax.numpy as jnp
from jax import lax
from jax.experimental import pallas as pl
from jax.experimental.pallas import tpu as pltpu
from jax.sharding import PartitionSpec as P

F32 = jnp.float32
BF16 = jnp.bfloat16
I32 = jnp.int32

STAR_DEV = 512
BLOCK = 128
STEP = 1.0
SOFT_STAR = 0.01
SOFT_GALAXY = 0.04

NT = (((1,), (1,)), ((), ()))
SMEM = pl.BlockSpec(memory_space=pltpu.SMEM)
VMEM = pl.BlockSpec(memory_space=pltpu.VMEM)


def split3(x):
    a = x.astype(BF16).astype(F32)
    r = x - a
    b = r.astype(BF16).astype(F32)
    c = (r - b).astype(BF16).astype(F32)
    return a, b, c


def predicted(pos, vel, acc, jerk):
    half = 0.5 * STEP**2
    sixth = STEP**3 / 6.0
    return (
        pos + STEP * vel + half * acc + sixth * jerk,
        vel + STEP * acc + half * jerk,
    )


def chosen_hot(active_row, stars):
    row = lax.broadcasted_iota(I32, (stars, active_row.shape[1]), 0)
    return jnp.where(row == active_row, 1.0, 0.0).astype(BF16)


def sum_parts(x):
    n = x.shape[0] // 3
    return x[:n] + x[n : 2 * n] + x[2 * n : 3 * n]


def pre_kernel(pos_ref, vel_ref, acc_ref, jerk_ref, mass_ref, idx_ref, leaf_ref,
               planes_ref, act_ref, start_ref):
    nb = mass_ref.shape[0]
    lanes = lambda ref, q: jnp.concatenate([ref[q, b : b + 1, :] for b in range(nb)], 1)
    rows = lambda ref: jnp.concatenate([lanes(ref, q) for q in range(3)], 0)
    pos, vel, acc, jerk = (rows(r) for r in (pos_ref, vel_ref, acc_ref, jerk_ref))
    mass = jnp.concatenate([mass_ref[b : b + 1, :] for b in range(nb)], 1)
    leaf = jnp.concatenate([leaf_ref[s : s + 1, :] for s in range(leaf_ref.shape[0])], 1)
    x, v = predicted(pos, vel, acc, jerk)
    planes_ref[...] = jnp.concatenate([x, v, mass, leaf.astype(F32)], 0)
    hot = chosen_hot(idx_ref[...], pos.shape[1])
    zero4 = jnp.zeros((4, pos.shape[1]), F32)
    parts = split3(jnp.concatenate([pos, vel, acc, jerk, zero4], 0))
    at = sum_parts(
        jnp.dot(jnp.concatenate(parts, 0).astype(BF16), hot, preferred_element_type=F32)
    )
    start_ref[...] = at
    ax, av = predicted(at[0:3], at[3:6], at[6:9], at[9:12])
    sent = jnp.concatenate([ax, av, jnp.zeros((2, at.shape[1]), F32)], 0)
    for c in range(act_ref.shape[0]):
        act_ref[c] = sent


def prepare(pos, vel, acc, jerk, mass, idx, leaf, cols):
    stars = mass.size
    acts = idx.shape[1]
    return pl.pallas_call(
        pre_kernel,
        out_shape=(
            jax.ShapeDtypeStruct((8, stars), F32),
            jax.ShapeDtypeStruct((cols, 8, acts), F32),
            jax.ShapeDtypeStruct((16, acts), F32),
        ),
    )(pos, vel, acc, jerk, mass, idx, leaf)


def pair_kernel(width, row_ref, act_ref, s0_ref, s1_ref, s2_ref, s3_ref, out_ref,
                rs_ref, b_ref, ws_ref, leaf_ref):
    own = s0_ref.shape[1]
    refs = (s0_ref, s1_ref, s2_ref, s3_ref)
    n = own * len(refs)
    acts = act_ref.shape[2]
    ic = act_ref.shape[0] * acts

    @pl.when(pl.program_id(0) == 0)
    def _():
        for k, ref in enumerate(refs):
            s = ref[...]
            row = lax.broadcasted_iota(I32, s.shape, 0)
            s1, s2, s3 = split3(s)
            x = s[0:3]
            v = s[3:6]
            n1, n2, n3 = split3(jnp.sum(x * x, 0, keepdims=True))
            d1, d2, d3 = split3(jnp.sum(x * v, 0, keepdims=True))
            one = jnp.ones_like(n1)
            zero7 = jnp.zeros((7, own), F32)
            tail = [one, one, one, n1, n2, n3, d1, d2, d3, zero7]
            big = jnp.concatenate([s1, s2, s3, s1, s2, s1] + tail, 0)
            rs_ref[k * own : (k + 1) * own, :] = big.T.astype(BF16)
            m = s[6:7]
            g1, g2, g3 = split3(jnp.where(row == 6, m, s * m))
            b_ref[:, k * own : (k + 1) * own] = jnp.concatenate(
                [g1, g2, g3, jnp.zeros_like(g1)], 0
            ).astype(BF16)
        slots = own // 128
        table = [r[7:8, 128 * s : 128 * s + 128] for r in refs for s in range(slots)]
        table.append(jnp.zeros((128 - len(table), 128), F32))
        turned = pltpu.roll(jnp.concatenate(table, 0), (128 - 32 * row_ref[0]) & 127, 1)
        leaf_ref[...] = turned.T

    a = jnp.concatenate([act_ref[q] for q in range(act_ref.shape[0])], 1)
    x = a[0:3]
    v = a[3:6]
    zero2 = jnp.zeros((2, ic), F32)
    one = jnp.ones((1, ic), F32)
    zero3 = jnp.zeros((3, ic), F32)
    one3 = jnp.ones((3, ic), F32)
    zero7 = jnp.zeros((7, ic), F32)

    def left(p, extra, tail):
        p1, p2, p3 = split3(p)
        return jnp.concatenate(
            [p1, p1, p1, p2, p2, p3] + list(split3(extra)) + tail + [zero7], 0
        )

    lr = left(
        jnp.concatenate([-2.0 * x, zero3, zero2], 0),
        jnp.sum(x * x, 0, keepdims=True) + SOFT_STAR,
        [one3, zero3],
    )
    lv = left(
        jnp.concatenate([-v, -x, zero2], 0),
        jnp.sum(x * v, 0, keepdims=True),
        [zero3, one3],
    )
    L = jnp.concatenate([lr, lv], 1).astype(BF16)
    f = None
    for j0 in range(0, n, width):
        p = jnp.dot(rs_ref[j0 : j0 + width, :], L, preferred_element_type=F32)
        inv = lax.rsqrt(p[:, :ic])
        i2 = inv * inv
        w = i2 * inv
        ws_ref[j0 : j0 + width, :ic] = w.astype(BF16)
        ws_ref[j0 : j0 + width, ic:] = ((w * i2) * p[:, ic:]).astype(BF16)
        d = jnp.dot(
            b_ref[:, j0 : j0 + width],
            ws_ref[j0 : j0 + width, :],
            preferred_element_type=F32,
        )
        f = d if f is None else f + d
    t = sum_parts(f[0:24])
    wt = t[:, :ic]
    st = t[:, ic:]
    mw = wt[6:7]
    ms = st[6:7]
    acc = wt[0:3] - x * mw
    jerk = wt[3:6] - v * mw - 3.0 * (st[0:3] - x * ms)
    for q in range(act_ref.shape[0]):
        cut = slice(q * acts, (q + 1) * acts)
        c = pl.program_id(0) * act_ref.shape[0] + q
        out_ref[q, 0:6, :] = jnp.concatenate([acc[:, cut], jerk[:, cut]], 0)
        out_ref[q, 6:7, :] = leaf_ref[pl.ds(c, 1), :]
        out_ref[q, 7:8, :] = jnp.zeros((1, acts), F32)


def pair_terms(row, active, stars, group=2, width=1024):
    cols, _, acts = active.shape
    own = stars[0].shape[1]
    n = own * len(stars)
    ic = group * acts
    block = pl.BlockSpec((group, 8, acts), lambda i: (i, 0, 0))
    whole = pl.BlockSpec((8, own), lambda i: (0, 0))
    return pl.pallas_call(
        functools.partial(pair_kernel, width),
        grid=(cols // group,),
        in_specs=[SMEM, block] + [whole] * len(stars),
        out_specs=block,
        out_shape=jax.ShapeDtypeStruct((cols, 8, acts), F32),
        scratch_shapes=[
            pltpu.VMEM((n, 64), BF16),
            pltpu.VMEM((32, n), BF16),
            pltpu.VMEM((n, 2 * ic), BF16),
            pltpu.VMEM((128, 128), F32),
        ],
    )(row, active, *stars)


def correct_kernel(block_ref, part_ref, start_ref, planes_ref, idx_ref,
                   pos_ref, mid_ref, send_ref, table_ref, lo_ref, hi_ref):
    nb = pos_ref.shape[1]
    total = part_ref[0]
    for c in range(1, part_ref.shape[0]):
        total = total + part_ref[c]
    table_ref[...] = part_ref[:, 6, :].astype(I32)
    acc = total[0:3]
    jerk = total[3:6]
    x0, v0, a0, j0 = (start_ref[3 * q : 3 * q + 3, :] for q in range(4))
    v1 = v0 + (a0 + acc) * (0.5 * STEP) + (j0 - jerk) * (STEP**2 / 12.0)
    x1 = x0 + (v0 + v1) * (0.5 * STEP) + (a0 - acc) * (STEP**2 / 12.0)
    one = jnp.ones((2, x1.shape[1]), F32)
    parts = split3(jnp.concatenate([x1, v1, one], 0))
    planes = planes_ref[...]
    hot = chosen_hot(idx_ref[...], planes.shape[1])
    put = jnp.concatenate(parts + (jnp.zeros_like(parts[0]),), 0).astype(BF16)
    spread = sum_parts(lax.dot_general(put, hot, NT, preferred_element_type=F32)[0:24])
    new = jnp.where(spread[6:7] > 0.5, spread, planes)
    zero4 = jnp.zeros((4, BLOCK), F32)
    for b in range(nb):
        cut = slice(b * BLOCK, (b + 1) * BLOCK)
        for q in range(3):
            pos_ref[q, b : b + 1, :] = new[q : q + 1, cut]
            mid_ref[q, b : b + 1, :] = new[3 + q : 4 + q, cut]
        packed = jnp.concatenate([new[0:3, cut], planes[6:7, cut]], 0)
        lo_ref[b] = jnp.concatenate([packed, zero4], 0)
        hi_ref[b] = jnp.concatenate([zero4, packed], 0)
    lo_ref[nb] = jnp.concatenate([zero4, zero4], 0)
    hi_ref[nb] = jnp.concatenate([zero4, zero4], 0)

    def body(e, carry):
        for h in range(2):
            a = block_ref[2 * h, e]
            b = block_ref[2 * h + 1, e]
            send_ref[e, 8 * h : 8 * h + 8, :] = (
                lo_ref[jnp.where(a < 0, nb, a)] + hi_ref[jnp.where(b < 0, nb, b)]
            )
        return carry

    lax.fori_loop(0, send_ref.shape[0], body, 0, unroll=8)


def correct(block, part, start, planes, idx, nb):
    targets = block.shape[1]
    return pl.pallas_call(
        correct_kernel,
        in_specs=[SMEM] + [VMEM] * 4,
        out_shape=(
            jax.ShapeDtypeStruct((3, nb, BLOCK), F32),
            jax.ShapeDtypeStruct((3, nb, BLOCK), F32),
            jax.ShapeDtypeStruct((targets, 16, BLOCK), F32),
            jax.ShapeDtypeStruct((part.shape[0], 128), I32),
        ),
        scratch_shapes=[pltpu.VMEM((nb + 1, 8, BLOCK), F32)] * 2,
    )(block, part, start, planes, idx)


def leaf_kernel(pos_ref, mass_ref, g_ref, gm_ref):
    def body(l, carry):
        g = jnp.concatenate([pos_ref[q, pl.ds(l, 1), :] for q in range(3)], 0)
        m = mass_ref[pl.ds(l, 1), :]
        z1 = jnp.zeros_like(m)
        z4 = jnp.zeros((4, m.shape[1]), F32)
        e = jnp.concatenate(split3(jnp.sum(g * g, 0, keepdims=True) + SOFT_GALAXY), 0)
        p1, p2, p3 = split3(-2.0 * g)
        low = []
        high = []
        for t in (p1, p1, p1, p2, p2, p3, jnp.ones_like(g), e):
            low += [t, z1, z4]
            high += [z4, t, z1]
        g_ref[l] = jnp.concatenate(low + high, 0).T.astype(BF16)
        w1, w2, w3 = split3(jnp.concatenate([g * m, m], 0))
        gm_ref[l] = jnp.concatenate([w1, w1, w2, w2, w3, w3, z4, z4], 0).astype(BF16)
        return carry

    lax.fori_loop(0, mass_ref.shape[0], body, 0, unroll=4)


def leaf_prep(pos, mass):
    nl = mass.shape[0]
    return pl.pallas_call(
        leaf_kernel,
        out_shape=(
            jax.ShapeDtypeStruct((nl, 128, 128), BF16),
            jax.ShapeDtypeStruct((nl, 32, 128), BF16),
        ),
        cost_estimate=pl.CostEstimate(
            flops=10**7, transcendentals=0, bytes_accessed=5 * 10**6
        ),
    )(pos, mass)


def entry_kernel(G, scale, row_ref, tab_ref, st_ref, g_ref, gm_ref, gpos_ref,
                 pull_ref, kick_ref, acc_ref, t_ref, s_ref, v_ref):
    nl = g_ref.shape[0]
    ng = 2 * st_ref.shape[0] // G
    acc_ref[...] = jnp.zeros_like(acc_ref)
    t_ref[...] = jnp.zeros_like(t_ref)
    r8 = lax.broadcasted_iota(I32, (8, 128), 0)
    low = r8 < 4
    q4 = r8 & 3
    one = jnp.ones((8, 128), F32)
    zero8 = jnp.zeros((8, 128), F32)
    me = row_ref[0]

    def leaves(g, j):
        d = g * (G // 2) + j // 2
        h = j % 2
        c = d & 31
        k = (me - lax.shift_right_logical(d, 5)) & 3
        la = jnp.maximum(tab_ref[c, k * 4 + 2 * h], 0)
        lb = jnp.maximum(tab_ref[c, k * 4 + 2 * h + 1], 0)
        return la, lb

    def halves(t, a, b):
        return jnp.where(
            low,
            jnp.broadcast_to(t[a : a + 1], (8, 128)),
            jnp.broadcast_to(t[b : b + 1], (8, 128)),
        )

    def stars(g, j):
        h = 8 * (j % 2)
        return st_ref[g * (G // 2) + j // 2, h : h + 8, :]

    def prep(g, b, j):
        s = stars(g, j)
        s1, s2, s3 = split3(s)
        x2 = jnp.where(q4 == 3, 0.0, s * s)
        x2 = x2 + jnp.where((r8 & 1) == 0, pltpu.roll(x2, 7, 0), pltpu.roll(x2, 1, 0))
        x2 = x2 + jnp.where((r8 & 2) == 0, pltpu.roll(x2, 6, 0), pltpu.roll(x2, 2, 0))
        n1, n2, n3 = split3(x2)
        t1 = jnp.where(q4 == 0, n1, jnp.where(q4 == 1, n2, n3))
        T = jnp.concatenate([s1, s2, s3, s1, s2, s1, t1, one], 0).astype(BF16)
        t_ref[b, j, 0:64, 0:128] = T
        t_ref[b, j, 64:128, 128:256] = T
        m1, m2, m3 = split3(jnp.where(q4 == 3, s, s * halves(s, 3, 7)))
        s_ref[b, j] = jnp.concatenate([m1, m2, m3, zero8], 0).astype(BF16)

    def force(g, b, j):
        la, lb = leaves(g, j)
        lane = lax.broadcasted_iota(I32, (128, 128), 1)
        L = jnp.where(lane < 64, g_ref[la], g_ref[lb])
        inv = lax.rsqrt(jnp.dot(L, t_ref[b, j], preferred_element_type=F32))
        u = inv * inv * inv
        hi = u.astype(BF16)
        v_ref[b, j, 0:128, :] = hi
        v_ref[b, j, 128:256, :] = (u - hi.astype(F32)).astype(BF16)

    def sums(g, b, j):
        la, lb = leaves(g, j)
        h = 8 * (j % 2)
        r32 = lax.broadcasted_iota(I32, (32, 128), 0)
        gm = jnp.where((r32 & 7) < 4, gm_ref[la], gm_ref[lb])
        f = jnp.dot(jnp.concatenate([gm, gm], 1), v_ref[b, j], preferred_element_type=F32)
        t = sum_parts(f[0:24])
        t = jnp.where(low, t[:, :128], t[:, 128:])
        kick_ref[g * (G // 2) + j // 2, h : h + 8, :] = t - stars(g, j) * halves(t, 3, 7)
        S = s_ref[b, j]
        hi = v_ref[b, j, 0:128, :]
        lo = v_ref[b, j, 128:256, :]
        V = jnp.concatenate(
            [
                jnp.concatenate([hi[:, :128], lo[:, :128]], 1),
                jnp.concatenate([hi[:, 128:], lo[:, 128:]], 1),
            ],
            0,
        )
        f = lax.dot_general(jnp.concatenate([S, S], 1), V, NT, preferred_element_type=F32)
        return la, lb, sum_parts(f[0:24])

    def step(g, b, more, more2):
        done = []
        for j in range(G):
            done.append(sums(g, b, j))
            if more:
                force(g + 1, 1 - b, j)
            if more2:
                prep(g + 2, b, j)
        for la, lb, t in done:
            acc_ref[la] += jnp.where(low, t[:, :128], 0.0)
            acc_ref[lb] += jnp.where(low, 0.0, t[:, 128:])

    for j in range(G):
        prep(0, 0, j)
    for j in range(G):
        force(0, 0, j)
        prep(1, 1, j)

    def body(i, carry):
        step(2 * i, 0, True, True)
        step(2 * i + 1, 1, True, True)
        return carry

    lax.fori_loop(0, ng // 2 - 1, body, 0)
    step(ng - 2, 0, True, False)
    step(ng - 1, 1, False, False)

    def finish(l, carry):
        a = acc_ref[l]
        a = a[0:4] + a[4:8]
        for q in range(3):
            g = gpos_ref[q, pl.ds(l, 1), :]
            pull_ref[q, pl.ds(l, 1), :] = (a[q : q + 1] - g * a[3:4]) * scale
        return carry

    lax.fori_loop(0, nl, finish, 0, unroll=8)


def entry_terms(row, table, stars, g, gm, gpos, scale, G=4):
    nd = stars.shape[0]
    nl = g.shape[0]
    return pl.pallas_call(
        functools.partial(entry_kernel, G, scale),
        in_specs=[SMEM] * 2 + [VMEM] * 4,
        out_shape=(
            jax.ShapeDtypeStruct((3, nl, 128), F32),
            jax.ShapeDtypeStruct((nd, 16, 128), F32),
        ),
        scratch_shapes=[
            pltpu.VMEM((nl, 8, 128), F32),
            pltpu.VMEM((2, G, 128, 256), BF16),
            pltpu.VMEM((2, G, 32, 128), BF16),
            pltpu.VMEM((2, G, 256, 256), BF16),
        ],
    )(row, table, stars, g, gm, gpos)


def finish_kernel(block_ref, kick_ref, mid_ref, vel_ref):
    nb = mid_ref.shape[1]
    low = lax.broadcasted_iota(I32, (8, 128), 0) < 4

    def body(e, sums):
        sums = list(sums)
        for h in range(2):
            owner = jnp.where(low, block_ref[2 * h, e], block_ref[2 * h + 1, e])
            k = kick_ref[e, 8 * h : 8 * h + 8, :]
            for b in range(nb):
                sums[b] = sums[b] + jnp.where(owner == b, k, 0.0)
        return tuple(sums)

    start = tuple(jnp.zeros((8, 128), F32) for _ in range(nb))
    sums = lax.fori_loop(0, kick_ref.shape[0], body, start, unroll=8)
    for b in range(nb):
        total = sums[b][0:4] + sums[b][4:8]
        for q in range(3):
            vel_ref[q, b : b + 1, :] = mid_ref[q, b : b + 1, :] + STEP * total[q : q + 1]


def finish(block, kicks, mid):
    return pl.pallas_call(
        finish_kernel,
        in_specs=[SMEM] + [VMEM] * 2,
        out_shape=jax.ShapeDtypeStruct(mid.shape, F32),
    )(block, kicks, mid)


def local(
    star_pos,
    star_vel,
    star_acc,
    star_jerk,
    star_mass,
    active_index,
    send_block,
    send_leaf,
    galaxy_pos,
    galaxy_mass,
):
    rows = lax.axis_size("row")
    cols = lax.axis_size("col")
    nb = star_pos.shape[0]
    turn = lambda x: x.transpose(1, 0, 2)
    row = lax.axis_index("row").astype(I32).reshape(1)
    block = send_block[0].T
    leaf = send_leaf[0].T
    gpos = turn(galaxy_pos)
    planes, sent, start = prepare(
        turn(star_pos), turn(star_vel), turn(star_acc), turn(star_jerk),
        star_mass, active_index, leaf, cols,
    )
    stars = [planes]
    for k in range(1, rows):
        perm = [(i, (i + k) % rows) for i in range(rows)]
        stars.append(lax.ppermute(planes, "row", perm))
    active = lax.all_to_all(sent, "col", 0, 0, tiled=True)
    parts = pair_terms(row, active, stars)
    parts = lax.all_to_all(parts, "col", 0, 0, tiled=True)
    pos_new, mid, outgoing, table = correct(block, parts, start, planes, active_index, nb)
    arrived = lax.all_to_all(outgoing, ("row", "col"), 0, 0, tiled=True)
    g, gm = leaf_prep(gpos, galaxy_mass)
    scale = STAR_DEV * rows * cols / BLOCK
    pull, kick = entry_terms(row, table, arrived, g, gm, gpos, scale)
    returned = lax.all_to_all(kick, ("row", "col"), 0, 0, tiled=True)
    vel_new = finish(block, returned, mid)
    return turn(pos_new), turn(vel_new), turn(pull)


def solution(mesh):
    both = P(("row", "col"), None, None)
    flat = P(("row", "col"), None)
    return jax.shard_map(
        local,
        mesh=mesh,
        in_specs=(both, both, both, both, flat, flat, both, both, both, flat),
        out_specs=(both, both, both),
        check_vma=False,
    )
```

time: 326 us -> 135 us (0.41)
  other arithmetic: 216 us -> 0 us
  Pallas kernels: 0 us -> 58.4 us
  blocking collectives: 11 us -> 41.2 us
  waiting for transfers between devices: 39.1 us -> 15.2 us
  local copies, waits for them, and re-layouts: 19.3 us -> 1.65 us
  starting transfers between devices: 33 us -> 17.8 us
  matrix products: 3.58 us -> 0 us
    reduce_sum x81 -> x0, other arithmetic: 165 us -> none  [the longest x32 62.5 us: entry_one(): kick = jnp.sum(delta * (gmass[:, None, :] * cube)[:, None], -1)]
    pallas_call x0 -> x6, Pallas kernels: none -> 58.4 us  [the longest x1 25.6 us: entry_terms(): pl.pallas_call(functools.partial(entry_kernel, G, scale), in_specs=[SMEM]...]
    all_to_all x0 -> x2, blocking collectives: none -> 41.2 us  [the longest x1 24.6 us: local(): returned = lax.all_to_all(kick, ('row', 'col'), 0, 0, tiled=True)]
    mul x40 -> x0, other arithmetic: 28 us -> none  [the longest x8 15.5 us: pair_block(): jerks = jnp.sum((dvel - 3.0 * along[None] * delta) * weight[None], -1)]
    all_to_all x5 -> x2, waiting for transfers between devices: 39.1 us -> 11.6 us  [the longest x1 11.6 us: local(): arrived = lax.all_to_all(outgoing, ('row', 'col'), 0, 0, tiled=True)]
    dynamic_update_slice x40 -> x0, other arithmetic: 20.8 us -> none  [the longest x32 20.7 us: entry_terms(): pull, kick = lax.map(entry_one, shaped)]
    all_to_all x5 -> x2, starting transfers between devices: 33 us -> 13.2 us  [the longest x1 8.58 us: local(): active = lax.all_to_all(sent, 'col', 0, 0, tiled=True)]
    all_gather x1 -> x0, blocking collectives: 11 us -> none  [gather_turned(): out = lax.all_gather(both, axis, axis=0, tiled=True)]
  transfers between devices with their start and end apart: 5 -> 5, of which waited for: 4 -> 3; matrix products, arithmetic and copies ran while one was open for 4% -> 0% of each run, Pallas kernels for 0% -> 5%
where the time goes in v1:
time: 135 us
  Pallas kernels  58.4 us (43%)
  blocking collectives  41.2 us (31%)
  starting transfers between devices  17.8 us (13%)
  waiting for transfers between devices  15.2 us (11%)
  local copies, waits for them, and re-layouts  1.65 us (1%)
    pallas_call x1, Pallas kernels, entry_terms(): pl.pallas_call(functools.partial(entry_kernel, G, scale), in_specs=[SMEM]...  25.6 us
    all_to_all x1, blocking collectives, local(): returned = lax.all_to_all(kick, ('row', 'col'), 0, 0, tiled=True)  24.6 us
    pallas_call x1, Pallas kernels, pair_terms(): pl.pallas_call(functools.partial(pair_kernel, width), grid=(cols // group...  18.3 us
    all_to_all x1, blocking collectives, local(): parts = lax.all_to_all(parts, 'col', 0, 0, tiled=True)  16.6 us
    all_to_all x1, waiting for transfers between devices, local(): arrived = lax.all_to_all(outgoing, ('row', 'col'), 0, 0, tiled=True)  11.6 us
    all_to_all x1, starting transfers between devices, local(): active = lax.all_to_all(sent, 'col', 0, 0, tiled=True)  8.58 us
    pallas_call x1, Pallas kernels, leaf_prep(): pl.pallas_call(leaf_kernel, out_shape=(jax.ShapeDtypeStruct((nl, 128, 128...  7.16 us
    all_to_all x1, starting transfers between devices, local(): arrived = lax.all_to_all(outgoing, ('row', 'col'), 0, 0, tiled=True)  4.66 us
  transfers between devices with their start and end apart: 5, of which 3 were waited for; matrix products, arithmetic and copies ran while one was open for 0% of the time, Pallas kernels for 5%

profile of v1, /device:TPU:1, one launch (start us, length us, event | category | flops | bytes accessed | tf_op | source)
XLA Modules:
  0.0 134.9 jit_solution(2104420368951925812)
XLA Ops:
  0.6 1.6 %shard_map.121 = (f32[8,512]{1,0:T(8,128)}, f32[32,8,128]{2,1,0:T(8,128)}, f32[16,128]{1,0:T(8,128)}) custom-call(f32[3,4,128]{2,1,0:T(4,128)} %bitcast.20, f32[3,4,128]{2,1,0:T(4,128)} %bitcast.21, f32[3,4,128]{2,1,0:T(4,128)} %bitcast.22, f32[3,4,128]{2,1,0:T(4,128)} %bitcast.23, f32[4,128]{1,0:T(4,128)} %mass_ref.2, s32[1,128]{1,0:T(1,128)} %idx_ref.3, ...), custom_call_target="tpu_custom_call" | custom-call | tf_op jit(solution)/shard_map/pallas_call | solution.py:78
  2.2 8.6 %all-to-all-start = ((f32[32,8,128]{2,1,0:T(8,128)}), f32[32,8,128]{2,1,0:T(8,128)S(1)}, u32[]{:S(2)}, u32[]{:S(2)}) async-start(f32[32,8,128]{2,1,0:T(8,128)} %get-tuple-element.14), calls=%async_computation | async-start | bytes 262144 | tf_op jit(solution)/shard_map/all_to_all | solution.py:485
  10.8 3.8 %collective-permute-start.2 = (f32[8,512]{1,0:T(8,128)}, f32[8,512]{1,0:T(8,128)S(1)}, u32[]{:S(2)}, u32[]{:S(2)}) collective-permute-start(f32[8,512]{1,0:T(8,128)} %get-tuple-element.15.s0_ref.planes_ref), channel_id=1, source_target_pairs={{0,96},{32,0},{64,32},{96,64},{1,97},{33,1},{65,33},{97,65},{2,98}... | collective-permute-start | bytes 49160 | tf_op jit(solution)/shard_map/ppermute | solution.py:484
  14.7 0.0 collective-permute-start.1
  14.7 0.7 collective-permute-start
  15.4 0.4 collective-permute-done.2.s3_ref
  15.7 0.0 copy-start.2
  15.7 3.2 %collective-permute-done.1.s2_ref = f32[8,512]{1,0:T(8,128)S(1)} collective-permute-done((f32[8,512]{1,0:T(8,128)}, f32[8,512]{1,0:T(8,128)S(1)}, u32[]{:S(2)}, u32[]{:S(2)}) %collective-permute-start.1) | collective-permute-done | bytes 16416 | tf_op jit(solution)/shard_map/ppermute | solution.py:484
  19.0 0.0 copy-start.3
  19.0 0.0 collective-permute-done.s1_ref
  19.0 0.0 copy-start.4
  19.0 0.0 all-to-all-done.act_ref
  19.0 0.0 copy-start.1
  19.0 0.0 copy-done.2
  19.0 0.6 copy-done.3
  19.6 0.0 copy-done.4
  19.6 0.1 copy-done.1
  19.6 18.3 %shard_map.122 = f32[32,8,128]{2,1,0:T(8,128)} custom-call(s32[1]{0:T(128)} %bitcast.2.row_ref, f32[32,8,128]{2,1,0:T(8,128)} %copy-done.1, f32[8,512]{1,0:T(8,128)} %get-tuple-element.15.s0_ref.planes_ref, f32[8,512]{1,0:T(8,128)} %copy-done.4, f32[8,512]{1,0:T(8,128)} %copy-done.3, f32[8,512]{1,0:T(8,128)} %copy-done.2), custom_call_target="tpu_custom_call" | custom-call | tf_op jit(solution)/shard_map/pallas_call | solution.py:184
  37.9 16.6 %all_to_all.20.part_ref = f32[32,8,128]{2,1,0:T(8,128)} all-to-all(f32[32,8,128]{2,1,0:T(8,128)} %shard_map.122), channel_id=1, replica_groups=mesh['row'=4,'col'=32] {'col'}, dimensions={0} | all-to-all | bytes 262144 | tf_op jit(solution)/shard_map/all_to_all | solution.py:487
  54.5 3.2 %shard_map.123 = (f32[3,4,128]{2,1,0:T(4,128)}, f32[3,4,128]{2,1,0:T(4,128)}, f32[128,16,128]{2,1,0:T(8,128)}, s32[32,128]{1,0:T(8,128)}) custom-call(s32[4,128]{1,0:T(4,128)} %bitcast.17, f32[32,8,128]{2,1,0:T(8,128)} %all_to_all.20.part_ref, f32[16,128]{1,0:T(8,128)} %get-tuple-element.16.start_ref, f32[8,512]{1,0:T(8,128)} %get-tuple-element.15.s0_ref.planes_ref, ...), custom_call_target="tpu_custom_call" | custom-call | tf_op jit(solution)/shard_map/pallas_call | solution.py:244
  57.7 4.7 %all-to-all-start.2 = ((f32[128,16,128]{2,1,0:T(8,128)}), f32[128,16,128]{2,1,0:T(8,128)S(1)}, u32[]{:S(2)}, u32[]{:S(2)}) async-start(f32[128,16,128]{2,1,0:T(8,128)} %get-tuple-element.19), calls=%async_computation.2 | async-start | bytes 2097152 | tf_op jit(solution)/shard_map/all_to_all | solution.py:489
  62.4 7.2 %shard_map.124 = (bf16[128,128,128]{2,1,0:T(8,128)(2,1)}, bf16[128,32,128]{2,1,0:T(8,128)(2,1)}) custom-call(f32[3,128,128]{2,1,0:T(8,128)} %bitcast.15, f32[128,128]{1,0:T(8,128)} %mass_ref.3), custom_call_target="tpu_custom_call" | custom-call | flops 10000000 | bytes 5000000 | tf_op jit(solution)/shard_map/pallas_call | solution.py:280
  69.5 11.6 %all-to-all-done.2.st_ref = f32[128,16,128]{2,1,0:T(8,128)S(1)} async-done(((f32[128,16,128]{2,1,0:T(8,128)}), f32[128,16,128]{2,1,0:T(8,128)S(1)}, u32[]{:S(2)}, u32[]{:S(2)}) %all-to-all-start.2) | async-done | bytes 1048608 | tf_op jit(solution)/shard_map/all_to_all | solution.py:489
  81.2 0.0 copy-start
  81.2 1.0 copy-done
  82.2 25.6 %shard_map.125 = (f32[3,128,128]{2,1,0:T(8,128)}, f32[128,16,128]{2,1,0:T(8,128)}) custom-call(s32[1]{0:T(128)} %bitcast.2.row_ref, s32[32,128]{1,0:T(8,128)} %get-tuple-element.18.tab_ref, f32[128,16,128]{2,1,0:T(8,128)} %copy-done, bf16[128,128,128]{2,1,0:T(8,128)(2,1)} %get-tuple-element.20.g_ref, bf16[128,32,128]{2,1,0:T(8,128)(2,1)} %get-tuple-element.21.gm_ref, ...), custom_call_target="tpu_custom_call" | custom-call | tf_op jit(solution)/shard_map/pallas_call | solution.py:412
  107.8 24.6 %all_to_all.21.kick_ref = f32[128,16,128]{2,1,0:T(8,128)} all-to-all(f32[128,16,128]{2,1,0:T(8,128)} %get-tuple-element.22), channel_id=1, replica_groups=mesh['row'=4,'col'=32] {'row','col'}, dimensions={0} | all-to-all | bytes 2097152 | tf_op jit(solution)/shard_map/all_to_all | solution.py:493
  132.4 2.5 %shard_map.126 = f32[3,4,128]{2,1,0:T(4,128)} custom-call(s32[4,128]{1,0:T(4,128)} %bitcast.18, f32[128,16,128]{2,1,0:T(8,128)} %all_to_all.21.kick_ref, f32[3,4,128]{2,1,0:T(4,128)} %get-tuple-element.23.mid_ref), custom_call_target="tpu_custom_call" | custom-call | tf_op jit(solution)/shard_map/pallas_call | solution.py:450
Async XLA Ops:
  2.2 16.7 %all-to-all-start = ((f32[32,8,128]{2,1,0:T(8,128)}), f32[32,8,128]{2,1,0:T(8,128)S(1)}, u32[]{:S(2)}, u32[]{:S(2)}) async-start(f32[32,8,128]{2,1,0:T(8,128)} %get-tuple-element.14), calls=%async_computation | async-start | bytes 262144 | tf_op jit(solution)/shard_map/all_to_all | solution.py:485
  10.8 4.9 %collective-permute-start.2 = (f32[8,512]{1,0:T(8,128)}, f32[8,512]{1,0:T(8,128)S(1)}, u32[]{:S(2)}, u32[]{:S(2)}) collective-permute-start(f32[8,512]{1,0:T(8,128)} %get-tuple-element.15.s0_ref.planes_ref), channel_id=1, source_target_pairs={{0,96},{32,0},{64,32},{96,64},{1,97},{33,1},{65,33},{97,65},{2,98}... | collective-permute-start | bytes 49160 | tf_op jit(solution)/shard_map/ppermute | solution.py:484
  14.7 4.3 %collective-permute-start.1 = (f32[8,512]{1,0:T(8,128)}, f32[8,512]{1,0:T(8,128)S(1)}, u32[]{:S(2)}, u32[]{:S(2)}) collective-permute-start(f32[8,512]{1,0:T(8,128)} %get-tuple-element.15.s0_ref.planes_ref), channel_id=1, source_target_pairs={{0,64},{32,96},{64,0},{96,32},{1,65},{33,97},{65,1},{97,33},{2,66}... | collective-permute-start | bytes 49160 | tf_op jit(solution)/shard_map/ppermute | solution.py:484
  14.7 4.3 %collective-permute-start = (f32[8,512]{1,0:T(8,128)}, f32[8,512]{1,0:T(8,128)S(1)}, u32[]{:S(2)}, u32[]{:S(2)}) collective-permute-start(f32[8,512]{1,0:T(8,128)} %get-tuple-element.15.s0_ref.planes_ref), channel_id=1, source_target_pairs={{0,32},{32,64},{64,96},{96,0},{1,33},{33,65},{65,97},{97,1},{2,34}... | collective-permute-start | bytes 49160 | tf_op jit(solution)/shard_map/ppermute | solution.py:484
  15.7 3.3 %copy-start.2 = (f32[8,512]{1,0:T(8,128)}, f32[8,512]{1,0:T(8,128)S(1)}, u32[]{:S(2)}) copy-start(f32[8,512]{1,0:T(8,128)S(1)} %collective-permute-done.2.s3_ref) | copy-start | bytes 49156
  19.0 0.6 copy-start.3
  19.0 0.6 copy-start.4
  19.0 0.7 copy-start.1
  57.7 23.4 %all-to-all-start.2 = ((f32[128,16,128]{2,1,0:T(8,128)}), f32[128,16,128]{2,1,0:T(8,128)S(1)}, u32[]{:S(2)}, u32[]{:S(2)}) async-start(f32[128,16,128]{2,1,0:T(8,128)} %get-tuple-element.19), calls=%async_computation.2 | async-start | bytes 2097152 | tf_op jit(solution)/shard_map/all_to_all | solution.py:489
  81.2 1.0 copy-start

commit v2 on v1

v2 whole, which is shorter than its diff:
```python
import functools

import jax
import jax.numpy as jnp
from jax import lax
from jax.experimental import pallas as pl
from jax.experimental.pallas import tpu as pltpu
from jax.sharding import PartitionSpec as P


F32 = jnp.float32
BF16 = jnp.bfloat16
I32 = jnp.int32

STAR_DEV = 512
BLOCK = 128
STEP = 1.0
SOFT_STAR = 0.01
SOFT_GALAXY = 0.04

NT = (((1,), (1,)), ((), ()))
SMEM = pl.BlockSpec(memory_space=pltpu.SMEM)
VMEM = pl.BlockSpec(memory_space=pltpu.VMEM)


def grant(mib):
    return pltpu.CompilerParams(vmem_limit_bytes=mib * 2**20)


def split3(x):
    a = x.astype(BF16).astype(F32)
    r = x - a
    b = r.astype(BF16).astype(F32)
    c = (r - b).astype(BF16).astype(F32)
    return a, b, c


def predicted(pos, vel, acc, jerk):
    half = 0.5 * STEP**2
    sixth = STEP**3 / 6.0
    return (
        pos + STEP * vel + half * acc + sixth * jerk,
        vel + STEP * acc + half * jerk,
    )


def chosen_hot(active_row, stars):
    row = lax.broadcasted_iota(I32, (stars, active_row.shape[1]), 0)
    return jnp.where(row == active_row, 1.0, 0.0).astype(BF16)


def sum_parts(x):
    n = x.shape[0] // 3
    return x[:n] + x[n : 2 * n] + x[2 * n : 3 * n]


def pre_kernel(pos_ref, vel_ref, acc_ref, jerk_ref, mass_ref, idx_ref, leaf_ref, block_ref,
               planes_ref, act_ref, start_ref, hot_ref):
    nb = mass_ref.shape[0]
    lanes = lambda ref, q: jnp.concatenate([ref[q, b : b + 1, :] for b in range(nb)], 1)
    rows = lambda ref: jnp.concatenate([lanes(ref, q) for q in range(3)], 0)
    flat = lambda ref: jnp.concatenate([ref[b : b + 1, :] for b in range(ref.shape[0])], 1)
    pos, vel, acc, jerk = (rows(r) for r in (pos_ref, vel_ref, acc_ref, jerk_ref))
    x, v = predicted(pos, vel, acc, jerk)
    zero1 = jnp.zeros((1, pos.shape[1]), F32)
    planes_ref[0:8, :] = jnp.concatenate([x, v, flat(mass_ref), zero1], 0)
    lists = [flat(leaf_ref).astype(F32), flat(block_ref).astype(F32)]
    planes_ref[8:16, :] = jnp.concatenate(lists + [zero1] * 6, 0)
    hot = chosen_hot(idx_ref[...], pos.shape[1])
    hot_ref[...] = hot
    zero4 = jnp.zeros((4, pos.shape[1]), F32)
    parts = split3(jnp.concatenate([pos, vel, acc, jerk, zero4], 0))
    at = sum_parts(
        jnp.dot(jnp.concatenate(parts, 0).astype(BF16), hot, preferred_element_type=F32)
    )
    start_ref[...] = at
    ax, av = predicted(at[0:3], at[3:6], at[6:9], at[9:12])
    act_ref[...] = jnp.concatenate([ax, av, jnp.zeros((2, at.shape[1]), F32)], 0)


def prepare(pos, vel, acc, jerk, mass, idx, leaf, block):
    stars = mass.size
    acts = idx.shape[1]
    return pl.pallas_call(
        pre_kernel,
        out_shape=(
            jax.ShapeDtypeStruct((16, stars), F32),
            jax.ShapeDtypeStruct((8, acts), F32),
            jax.ShapeDtypeStruct((16, acts), F32),
            jax.ShapeDtypeStruct((stars, acts), BF16),
        ),
    )(pos, vel, acc, jerk, mass, idx, leaf, block)


def address_kernel(cols, row_ref, act_ref, s0_ref, s1_ref, s2_ref, s3_ref, out_ref):
    refs = (s0_ref, s1_ref, s2_ref, s3_ref)
    slots = s0_ref.shape[1] // 128
    table = [
        ref[q : q + 1, 128 * s : 128 * s + 128]
        for q in range(2)
        for ref in refs
        for s in range(slots)
    ]
    table.append(jnp.zeros((128 - len(table), 128), F32))
    shift = (128 - cols * row_ref[0]) & 127
    turned = pltpu.roll(jnp.concatenate(table, 0), shift, 1).T
    for c in range(cols):
        out_ref[c, 0:6, :] = act_ref[0:6, :]
        out_ref[c, 6:7, :] = turned[c : c + 1, :]
        out_ref[c, 7:8, :] = jnp.zeros((1, 128), F32)


def address(row, active, stars, cols):
    lists = pl.BlockSpec((8, stars[0].shape[1]), lambda i: (1, 0))
    whole = pl.BlockSpec(active.shape, lambda i: (0, 0))
    return pl.pallas_call(
        functools.partial(address_kernel, cols),
        grid=(1,),
        in_specs=[SMEM, whole] + [lists] * len(stars),
        out_specs=pl.BlockSpec((cols,) + active.shape, lambda i: (0, 0, 0)),
        out_shape=jax.ShapeDtypeStruct((cols,) + active.shape, F32),
        compiler_params=grant(8),
    )(row, active, *stars)


def pair_kernel(width, act_ref, s0_ref, s1_ref, s2_ref, s3_ref, out_ref,
                rs_ref, b_ref, ws_ref):
    own = s0_ref.shape[1]
    refs = (s0_ref, s1_ref, s2_ref, s3_ref)
    n = own * len(refs)
    acts = act_ref.shape[2]
    ic = act_ref.shape[0] * acts

    @pl.when(pl.program_id(0) == 0)
    def _():
        for k, ref in enumerate(refs):
            s = ref[...]
            row = lax.broadcasted_iota(I32, s.shape, 0)
            s1, s2, s3 = split3(s)
            x = s[0:3]
            v = s[3:6]
            n1, n2, n3 = split3(jnp.sum(x * x, 0, keepdims=True))
            d1, d2, d3 = split3(jnp.sum(x * v, 0, keepdims=True))
            one = jnp.ones_like(n1)
            zero7 = jnp.zeros((7, own), F32)
            tail = [one, one, one, n1, n2, n3, d1, d2, d3, zero7]
            big = jnp.concatenate([s1, s2, s3, s1, s2, s1] + tail, 0)
            rs_ref[k * own : (k + 1) * own, :] = big.T.astype(BF16)
            m = s[6:7]
            g1, g2, g3 = split3(jnp.where(row == 6, m, s * m))
            b_ref[:, k * own : (k + 1) * own] = jnp.concatenate(
                [g1, g2, g3, jnp.zeros_like(g1)], 0
            ).astype(BF16)

    a = jnp.concatenate([act_ref[q] for q in range(act_ref.shape[0])], 1)
    x = a[0:3]
    v = a[3:6]
    zero2 = jnp.zeros((2, ic), F32)
    one = jnp.ones((1, ic), F32)
    zero3 = jnp.zeros((3, ic), F32)
    one3 = jnp.ones((3, ic), F32)
    zero7 = jnp.zeros((7, ic), F32)

    def left(p, extra, tail):
        p1, p2, p3 = split3(p)
        return jnp.concatenate(
            [p1, p1, p1, p2, p2, p3] + list(split3(extra)) + tail + [zero7], 0
        )

    lr = left(
        jnp.concatenate([-2.0 * x, zero3, zero2], 0),
        jnp.sum(x * x, 0, keepdims=True) + SOFT_STAR,
        [one3, zero3],
    )
    lv = left(
        jnp.concatenate([-v, -x, zero2], 0),
        jnp.sum(x * v, 0, keepdims=True),
        [zero3, one3],
    )
    L = jnp.concatenate([lr, lv], 1).astype(BF16)
    f = None
    for j0 in range(0, n, width):
        p = jnp.dot(rs_ref[j0 : j0 + width, :], L, preferred_element_type=F32)
        inv = lax.rsqrt(p[:, :ic])
        i2 = inv * inv
        w = i2 * inv
        ws_ref[j0 : j0 + width, :ic] = w.astype(BF16)
        ws_ref[j0 : j0 + width, ic:] = ((w * i2) * p[:, ic:]).astype(BF16)
        d = jnp.dot(
            b_ref[:, j0 : j0 + width],
            ws_ref[j0 : j0 + width, :],
            preferred_element_type=F32,
        )
        f = d if f is None else f + d
    t = sum_parts(f[0:24])
    wt = t[:, :ic]
    st = t[:, ic:]
    mw = wt[6:7]
    ms = st[6:7]
    acc = wt[0:3] - x * mw
    jerk = wt[3:6] - v * mw - 3.0 * (st[0:3] - x * ms)
    for q in range(act_ref.shape[0]):
        cut = slice(q * acts, (q + 1) * acts)
        out_ref[q] = jnp.concatenate([acc[:, cut], jerk[:, cut], zero2[:, cut]], 0)


def pair_terms(active, stars, group=2, width=1024):
    cols, _, acts = active.shape
    own = stars[0].shape[1]
    n = own * len(stars)
    ic = group * acts
    block = pl.BlockSpec((group, 8, acts), lambda i: (i, 0, 0))
    whole = pl.BlockSpec((8, own), lambda i: (0, 0))
    return pl.pallas_call(
        functools.partial(pair_kernel, width),
        grid=(cols // group,),
        in_specs=[block] + [whole] * len(stars),
        out_specs=block,
        out_shape=jax.ShapeDtypeStruct((cols, 8, acts), F32),
        compiler_params=grant(16),
        scratch_shapes=[
            pltpu.VMEM((n, 64), BF16),
            pltpu.VMEM((32, n), BF16),
            pltpu.VMEM((n, 2 * ic), BF16),
        ],
        cost_estimate=pl.CostEstimate(
            flops=4 * 2 * 128 * cols * acts * n,
            transcendentals=cols * acts * n,
            bytes_accessed=4 * 2 * cols * 8 * acts,
        ),
    )(active, *stars)


def correct_kernel(part_ref, start_ref, planes_ref, hot_ref, pos_ref, mid_ref, send_ref):
    nb = pos_ref.shape[1]
    total = part_ref[0]
    for c in range(1, part_ref.shape[0]):
        total = total + part_ref[c]
    acc = total[0:3]
    jerk = total[3:6]
    x0, v0, a0, j0 = (start_ref[3 * q : 3 * q + 3, :] for q in range(4))
    v1 = v0 + (a0 + acc) * (0.5 * STEP) + (j0 - jerk) * (STEP**2 / 12.0)
    x1 = x0 + (v0 + v1) * (0.5 * STEP) + (a0 - acc) * (STEP**2 / 12.0)
    one = jnp.ones((2, x1.shape[1]), F32)
    parts = split3(jnp.concatenate([x1, v1, one], 0))
    planes = planes_ref[0:8, :]
    put = jnp.concatenate(parts + (jnp.zeros_like(parts[0]),), 0).astype(BF16)
    spread = sum_parts(
        lax.dot_general(put, hot_ref[...], NT, preferred_element_type=F32)[0:24]
    )
    new = jnp.where(spread[6:7] > 0.5, spread, planes)
    sent = []
    for b in range(nb):
        cut = slice(b * BLOCK, (b + 1) * BLOCK)
        for q in range(3):
            pos_ref[q, b : b + 1, :] = new[q : q + 1, cut]
            mid_ref[q, b : b + 1, :] = new[3 + q : 4 + q, cut]
        sent += [new[0:3, cut], planes[6:7, cut]]
    sent = jnp.concatenate(sent, 0)
    for e in range(send_ref.shape[0]):
        send_ref[e] = sent


def correct(part, start, planes, hot, nb, chips):
    return pl.pallas_call(
        correct_kernel,
        in_specs=[VMEM] * 4,
        out_shape=(
            jax.ShapeDtypeStruct((3, nb, BLOCK), F32),
            jax.ShapeDtypeStruct((3, nb, BLOCK), F32),
            jax.ShapeDtypeStruct((chips, 4 * nb, BLOCK), F32),
        ),
    )(part, start, planes, hot)


def target_terms(g):
    z1 = jnp.zeros((1, g.shape[1]), F32)
    z4 = jnp.zeros((4, g.shape[1]), F32)
    e = jnp.concatenate(split3(jnp.sum(g * g, 0, keepdims=True) + SOFT_GALAXY), 0)
    p1, p2, p3 = split3(-2.0 * g)
    low = []
    high = []
    for t in (p1, p1, p1, p2, p2, p3, jnp.ones_like(g), e):
        low += [t, z1, z4]
        high += [z4, t, z1]
    return jnp.concatenate(low + high, 0).T.astype(BF16)


def leaf_kernel(pos_ref, mass_ref, g_ref, lo_ref, hi_ref):
    nl = mass_ref.shape[0]
    z4 = jnp.zeros((4, 128), F32)

    def body(l, carry):
        g = jnp.concatenate([pos_ref[q, pl.ds(l, 1), :] for q in range(3)], 0)
        m = mass_ref[pl.ds(l, 1), :]
        g_ref[l] = target_terms(g)
        lo_ref[l] = jnp.concatenate([g, m, z4], 0)
        hi_ref[l] = jnp.concatenate([z4, g, m], 0)
        return carry

    lax.fori_loop(0, nl, body, 0, unroll=4)
    lo_ref[nl] = jnp.zeros((8, 128), F32)
    hi_ref[nl] = jnp.zeros((8, 128), F32)


def leaf_prep(pos, mass):
    nl = mass.shape[0]
    return pl.pallas_call(
        leaf_kernel,
        out_shape=(
            jax.ShapeDtypeStruct((nl, 128, 128), BF16),
            jax.ShapeDtypeStruct((nl + 1, 8, 128), F32),
            jax.ShapeDtypeStruct((nl + 1, 8, 128), F32),
        ),
        cost_estimate=pl.CostEstimate(
            flops=10**7, transcendentals=0, bytes_accessed=7 * 10**6
        ),
    )(pos, mass)


def listed(row, d):
    return d & 31, 4 * ((row - lax.shift_right_logical(d, 5)) & 3)


def fetch_kernel(row_ref, tab_ref, lo_ref, hi_ref, out_ref):
    nl = lo_ref.shape[0] - 1
    row = row_ref[0]

    def body(d, carry):
        c, k = listed(row, d)
        for h in range(2):
            a = tab_ref[c, k + 2 * h]
            b = tab_ref[c, k + 2 * h + 1]
            out_ref[d, 8 * h : 8 * h + 8, :] = (
                lo_ref[jnp.where(a < 0, nl, a)] + hi_ref[jnp.where(b < 0, nl, b)]
            )
        return carry

    lax.fori_loop(0, out_ref.shape[0], body, 0, unroll=8)


def fetch(row, table, lo, hi, sources):
    return pl.pallas_call(
        fetch_kernel,
        in_specs=[SMEM] * 2 + [VMEM] * 2,
        out_shape=jax.ShapeDtypeStruct((sources, 16, 128), F32),
    )(row, table, lo, hi)


def attract(G, ng, bodies, targets, g_ref, acc_ref, t_ref, s_ref, v_ref):
    acc_ref[...] = jnp.zeros_like(acc_ref)
    t_ref[...] = jnp.zeros_like(t_ref)
    r8 = lax.broadcasted_iota(I32, (8, 128), 0)
    low = r8 < 4
    q4 = r8 & 3
    one = jnp.ones((8, 128), F32)
    zero8 = jnp.zeros((8, 128), F32)

    def prep(g, b, j):
        s = bodies(g, j, low)
        s1, s2, s3 = split3(s)
        x2 = jnp.where(q4 == 3, 0.0, s * s)
        x2 = x2 + jnp.where((r8 & 1) == 0, pltpu.roll(x2, 7, 0), pltpu.roll(x2, 1, 0))
        x2 = x2 + jnp.where((r8 & 2) == 0, pltpu.roll(x2, 6, 0), pltpu.roll(x2, 2, 0))
        n1, n2, n3 = split3(x2)
        t1 = jnp.where(q4 == 0, n1, jnp.where(q4 == 1, n2, n3))
        T = jnp.concatenate([s1, s2, s3, s1, s2, s1, t1, one], 0).astype(BF16)
        t_ref[b, j, 0:64, 0:128] = T
        t_ref[b, j, 64:128, 128:256] = T
        m = jnp.where(
            low,
            jnp.broadcast_to(s[3:4], (8, 128)),
            jnp.broadcast_to(s[7:8], (8, 128)),
        )
        m1, m2, m3 = split3(jnp.where(q4 == 3, s, s * m))
        s_ref[b, j] = jnp.concatenate([m1, m2, m3, zero8], 0).astype(BF16)

    def force(g, b, j):
        la, lb = targets(g, j)
        lane = lax.broadcasted_iota(I32, (128, 128), 1)
        L = jnp.where(lane < 64, g_ref[la], g_ref[lb])
        inv = lax.rsqrt(jnp.dot(L, t_ref[b, j], preferred_element_type=F32))
        u = inv * inv * inv
        hi = u.astype(BF16)
        lo = (u - hi.astype(F32)).astype(BF16)
        v_ref[b, j, 0:128, 0:128] = hi[:, :128]
        v_ref[b, j, 0:128, 128:256] = lo[:, :128]
        v_ref[b, j, 128:256, 0:128] = hi[:, 128:]
        v_ref[b, j, 128:256, 128:256] = lo[:, 128:]

    def sums(g, b, j):
        S = s_ref[b, j]
        f = lax.dot_general(
            jnp.concatenate([S, S], 1), v_ref[b, j], NT, preferred_element_type=F32
        )
        return targets(g, j) + (sum_parts(f[0:24]),)

    def step(g, b, more, more2):
        done = []
        for j in range(G):
            done.append(sums(g, b, j))
            if more:
                force(g + 1, 1 - b, j)
            if more2:
                prep(g + 2, b, j)
        for la, lb, t in done:
            acc_ref[la] += jnp.where(low, t[:, :128], 0.0)
            acc_ref[lb] += jnp.where(low, 0.0, t[:, 128:])

    for j in range(G):
        prep(0, 0, j)
    for j in range(G):
        force(0, 0, j)
        prep(1, 1, j)

    def body(i, carry):
        step(2 * i, 0, True, True)
        step(2 * i + 1, 1, True, True)
        return carry

    lax.fori_loop(0, ng // 2 - 1, body, 0)
    step(ng - 2, 0, True, False)
    step(ng - 1, 1, False, False)


def attract_scratch(targets, G):
    return [
        pltpu.VMEM((targets, 8, 128), F32),
        pltpu.VMEM((2, G, 128, 256), BF16),
        pltpu.VMEM((2, G, 32, 128), BF16),
        pltpu.VMEM((2, G, 256, 256), BF16),
    ]


def attract_cost(entries):
    return pl.CostEstimate(
        flops=3 * 2 * entries * 128**3,
        transcendentals=entries * 128**2,
        bytes_accessed=entries * 4 * 512,
    )


def kick_kernel(G, block_ref, leaf_ref, pos_ref, mid_ref, vel_ref, g_ref, *scratch):
    nb = pos_ref.shape[1]
    acc_ref = scratch[0]
    place = [
        jnp.concatenate([pos_ref[q, b : b + 1, :] for q in range(3)], 0) for b in range(nb)
    ]
    for b in range(nb):
        g_ref[b] = target_terms(place[b])

    def where(g, j):
        e = g * (G // 2) + j // 2
        h = 2 * (j % 2)
        return jnp.maximum(block_ref[h, e], 0), jnp.maximum(block_ref[h + 1, e], 0)

    def bodies(g, j, low):
        h = 8 * (j % 2)
        return leaf_ref[g * (G // 2) + j // 2, h : h + 8, :]

    attract(G, 2 * leaf_ref.shape[0] // G, bodies, where, g_ref, *scratch)
    for b in range(nb):
        a = acc_ref[b]
        a = a[0:4] + a[4:8]
        kick = a[0:3] - place[b] * a[3:4]
        for q in range(3):
            vel_ref[q, b : b + 1, :] = mid_ref[q, b : b + 1, :] + STEP * kick[q : q + 1]


def kicks(block, leaves, pos, mid, G=4):
    nb = pos.shape[1]
    return pl.pallas_call(
        functools.partial(kick_kernel, G),
        in_specs=[SMEM] + [VMEM] * 3,
        out_shape=jax.ShapeDtypeStruct(mid.shape, F32),
        scratch_shapes=[pltpu.VMEM((nb, 128, 128), BF16)] + attract_scratch(nb, G),
        cost_estimate=attract_cost(4 * leaves.shape[0]),
    )(block, leaves, pos, mid)


def pull_kernel(G, scale, here_ref, tab_ref, own_ref, other_ref, g_ref, gpos_ref,
                pull_ref, *scratch):
    acc_ref = scratch[0]
    row = here_ref[0]
    core = here_ref[1]

    def source(g, j):
        i = g * (G // 4) + j // 4
        flip = (j // 2) % 2
        c, k = listed(row, 2 * i + (core ^ flip))
        return (own_ref, other_ref)[flip], i, c, k + 2 * (j % 2)

    def where(g, j):
        _, _, c, k = source(g, j)
        return jnp.maximum(tab_ref[c, k], 0), jnp.maximum(tab_ref[c, k + 1], 0)

    def bodies(g, j, low):
        ref, i, c, k = source(g, j)
        a = tab_ref[c, 16 + k]
        b = tab_ref[c, 16 + k + 1]
        ta = ref[i, lax.shift_right_logical(jnp.maximum(a, 0), 1)]
        tb = ref[i, lax.shift_right_logical(jnp.maximum(b, 0), 1)]
        ta = jnp.where((a & 1) == 1, pltpu.roll(ta, 4, 0), ta)
        tb = jnp.where((b & 1) == 1, tb, pltpu.roll(tb, 4, 0))
        return jnp.where(jnp.where(low, a, b) < 0, 0.0, jnp.where(low, ta, tb))

    ng = 4 * own_ref.shape[0] // G
    attract(G, ng, bodies, where, g_ref, *scratch)

    def finish(l, carry):
        a = acc_ref[l]
        a = a[0:4] + a[4:8]
        for q in range(3):
            g = gpos_ref[q, pl.ds(l, 1), :]
            pull_ref[q, pl.ds(l, 1), :] = (a[q : q + 1] - g * a[3:4]) * scale
        return carry

    lax.fori_loop(0, g_ref.shape[0], finish, 0, unroll=8)


def pulls(here, table, own, other, g, gpos, scale, G=4):
    nl = g.shape[0]
    return pl.pallas_call(
        functools.partial(pull_kernel, G, scale),
        in_specs=[SMEM] * 2 + [VMEM] * 4,
        out_shape=jax.ShapeDtypeStruct((3, nl, 128), F32),
        scratch_shapes=attract_scratch(nl, G),
        cost_estimate=attract_cost(8 * own.shape[0]),
    )(here, table, own, other, g, gpos)


def local(
    star_pos,
    star_vel,
    star_acc,
    star_jerk,
    star_mass,
    active_index,
    send_block,
    send_leaf,
    galaxy_pos,
    galaxy_mass,
):
    rows = lax.axis_size("row")
    cols = lax.axis_size("col")
    devices = rows * cols
    nb = star_pos.shape[0]
    both = ("row", "col")
    turn = lambda x: x.transpose(1, 0, 2)
    row = lax.axis_index("row").astype(I32).reshape(1)
    core = (lax.axis_index("col") & 1).astype(I32).reshape(1)
    here = jnp.concatenate([row, core])
    block = send_block[0].T
    gpos = turn(galaxy_pos)
    planes, active, start, hot = prepare(
        turn(star_pos), turn(star_vel), turn(star_acc), turn(star_jerk),
        star_mass, active_index, send_leaf[0].T, block,
    )
    stars = [planes]
    for k in range(1, rows):
        perm = [(i, (i + k) % rows) for i in range(rows)]
        stars.append(lax.ppermute(planes, "row", perm))
    sent = address(here, active, stars, cols)
    arrived = lax.all_to_all(sent, "col", 0, 0, tiled=True)
    table = arrived[:, 6, :].astype(I32)
    g, lo, hi = leaf_prep(gpos, galaxy_mass)
    leaves = fetch(here, table, lo, hi, devices)
    leaves = lax.all_to_all(leaves, both, 0, 0, tiled=True)
    parts = pair_terms(arrived, stars)
    parts = lax.all_to_all(parts, "col", 0, 0, tiled=True)
    pos_new, mid, outgoing = correct(parts, start, planes, hot, nb, devices // 2)
    same_core = [[d for d in range(devices) if d % 2 == c] for c in range(2)]
    own = lax.all_to_all(outgoing, both, 0, 0, tiled=True, axis_index_groups=same_core)
    other = lax.ppermute(own, "col", [(i, i ^ 1) for i in range(cols)])
    vel_new = kicks(block, leaves, pos_new, mid)
    tiles = lambda x: x.reshape(-1, 2, 8, BLOCK)
    scale = STAR_DEV * devices / BLOCK
    pull = pulls(here, table, tiles(own), tiles(other), g, gpos, scale)
    return turn(pos_new), turn(vel_new), turn(pull)


def solution(mesh):
    both = P(("row", "col"), None, None)
    flat = P(("row", "col"), None)
    return jax.shard_map(
        local,
        mesh=mesh,
        in_specs=(both, both, both, both, flat, flat, both, both, both, flat),
        out_specs=(both, both, both),
        check_vma=False,
    )
```

time: 135 us -> 151 us (1.12)
  Pallas kernels: 58.4 us -> 74.4 us
  blocking collectives: 41.2 us -> 28.2 us
  waiting for transfers between devices: 15.2 us -> 21.7 us
  starting transfers between devices: 17.8 us -> 21 us
  local copies, waits for them, and re-layouts: 1.65 us -> 4 us
    pallas_call x4 -> x6, Pallas kernels: 33 us -> 50.6 us  [the longest x1 22.1 us: pulls(): pl.pallas_call(functools.partial(pull_kernel, G, scale), in_specs=[SMEM]...]
    all_to_all x1, blocking collectives: 24.6 us -> 16.7 us  [local(): arrived = lax.all_to_all(sent, 'col', 0, 0, tiled=True)]
    all_to_all x2, waiting for transfers between devices: 11.6 us -> 18 us  [the longest x1 17.6 us: local(): leaves = lax.all_to_all(leaves, both, 0, 0, tiled=True)]
    all_to_all x1, blocking collectives: 16.6 us -> 11.5 us  [local(): parts = lax.all_to_all(parts, 'col', 0, 0, tiled=True)]
    unnamed x10 -> x14, local copies, waits for them, and re-layouts: 1.65 us -> 3.98 us
    pallas_call x1, Pallas kernels: 18.3 us -> 16.6 us  [pair_terms(): pl.pallas_call(functools.partial(pair_kernel, width), grid=(cols // group...]
  transfers between devices with their start and end apart: 5 -> 6, of which waited for: 3 -> 4; matrix products, arithmetic and copies ran while one was open for 0% -> 0% of each run, Pallas kernels for 5% -> 21%
where the time goes in v2:
time: 151 us
  Pallas kernels  74.4 us (49%)
  blocking collectives  28.2 us (19%)
  waiting for transfers between devices  21.7 us (14%)
  starting transfers between devices  21 us (14%)
  local copies, waits for them, and re-layouts  4 us (3%)
    pallas_call x1, Pallas kernels, pulls(): pl.pallas_call(functools.partial(pull_kernel, G, scale), in_specs=[SMEM]...  22.1 us
    pallas_call x1, Pallas kernels, kicks(): pl.pallas_call(functools.partial(kick_kernel, G), in_specs=[SMEM] + [VMEM...  20.3 us
    all_to_all x1, waiting for transfers between devices, local(): leaves = lax.all_to_all(leaves, both, 0, 0, tiled=True)  17.6 us
    all_to_all x1, blocking collectives, local(): arrived = lax.all_to_all(sent, 'col', 0, 0, tiled=True)  16.7 us
    pallas_call x1, Pallas kernels, pair_terms(): pl.pallas_call(functools.partial(pair_kernel, width), grid=(cols // group...  16.6 us
    all_to_all x1, blocking collectives, local(): parts = lax.all_to_all(parts, 'col', 0, 0, tiled=True)  11.5 us
    all_to_all x1, starting transfers between devices, local(): leaves = lax.all_to_all(leaves, both, 0, 0, tiled=True)  9.46 us
    pallas_call x1, Pallas kernels, leaf_prep(): pl.pallas_call(leaf_kernel, out_shape=(jax.ShapeDtypeStruct((nl, 128, 128...  7.16 us
  transfers between devices with their start and end apart: 6, of which 4 were waited for; matrix products, arithmetic and copies ran while one was open for 0% of the time, Pallas kernels for 21%

profile of v2, /device:TPU:1, one launch (start us, length us, event | category | flops | bytes accessed | tf_op | source)
XLA Modules:
  0.0 150.7 jit_solution(2791706749546989212)
XLA Ops:
  0.6 1.6 %shard_map.121 = (f32[16,512]{1,0:T(8,128)}, f32[8,128]{1,0:T(8,128)}, f32[16,128]{1,0:T(8,128)}, bf16[512,128]{1,0:T(8,128)(2,1)}) custom-call(f32[3,4,128]{2,1,0:T(4,128)} %bitcast.25, f32[3,4,128]{2,1,0:T(4,128)} %bitcast.26, f32[3,4,128]{2,1,0:T(4,128)} %bitcast.27, f32[3,4,128]{2,1,0:T(4,128)} %bitcast.28, f32[4,128]{1,0:T(4,128)} %mass_ref.2, ...), custom_call_target="tpu_custom_call" | custom-call | tf_op jit(solution)/shard_map/pallas_call | solution.py:84
  2.2 4.6 %collective-permute-start.2 = (f32[16,512]{1,0:T(8,128)}, f32[16,512]{1,0:T(8,128)S(1)}, u32[]{:S(2)}, u32[]{:S(2)}) collective-permute-start(f32[16,512]{1,0:T(8,128)} %get-tuple-element.14.s0_ref.planes_ref), channel_id=1, source_target_pairs={{0,96},{32,0},{64,32},{96,64},{1,97},{33,1},{65,33},{97,65},{2,98}... | collective-permute-start | bytes 98312 | tf_op jit(solution)/shard_map/ppermute | solution.py:562
  6.8 0.0 collective-permute-start.1
  6.8 0.7 collective-permute-start
  7.5 0.1 pad_add_fusion.row_ref.here_ref
  7.6 0.0 copy-start.3
  7.6 0.6 collective-permute-done.2.s3_ref
  8.1 3.2 %collective-permute-done.1.s2_ref = f32[16,512]{1,0:T(8,128)S(1)} collective-permute-done((f32[16,512]{1,0:T(8,128)}, f32[16,512]{1,0:T(8,128)S(1)}, u32[]{:S(2)}, u32[]{:S(2)}) %collective-permute-start.1) | collective-permute-done | bytes 32800 | tf_op jit(solution)/shard_map/ppermute | solution.py:562
  11.3 0.0 collective-permute-done.s1_ref
  11.3 0.0 copy-start
  11.3 0.8 copy-done
  12.1 0.0 copy-start.2
  12.1 0.7 copy-done.2
  12.8 0.7 shard_map.122
  13.5 16.7 %all_to_all.20.act_ref = f32[32,8,128]{2,1,0:T(8,128)S(1)} all-to-all(f32[32,8,128]{2,1,0:T(8,128)S(1)} %shard_map.122), channel_id=1, replica_groups=mesh['row'=4,'col'=32] {'col'}, dimensions={0} | all-to-all | bytes 262144 | tf_op jit(solution)/shard_map/all_to_all | solution.py:564
  30.1 0.0 copy-start.1
  30.1 0.8 copy-done.1
  30.9 16.6 %shard_map.123 = f32[32,8,128]{2,1,0:T(8,128)S(1)} custom-call(f32[32,8,128]{2,1,0:T(8,128)S(1)} %all_to_all.20.act_ref, f32[16,512]{1,0:T(8,128)S(1)} %copy-done.1, f32[16,512]{1,0:T(8,128)S(1)} %collective-permute-done.s1_ref, f32[16,512]{1,0:T(8,128)S(1)} %collective-permute-done.1.s2_ref, f32[16,512]{1,0:T(8,128)S(1)} %collective-permute-done.2.s3_ref), custom_call_target="tpu_custom_call" | custom-call | flops 8589934592 | bytes 262144 | tf_op jit(solution)/shard_map/pallas_call | solution.py:214
  47.5 0.0 copy-done.3
  47.5 11.5 %all_to_all.21.part_ref = f32[32,8,128]{2,1,0:T(8,128)} all-to-all(f32[32,8,128]{2,1,0:T(8,128)S(1)} %shard_map.123), channel_id=1, replica_groups=mesh['row'=4,'col'=32] {'col'}, dimensions={0} | all-to-all | bytes 262144 | tf_op jit(solution)/shard_map/all_to_all | solution.py:570
  59.0 2.0 %shard_map.124 = (f32[3,4,128]{2,1,0:T(4,128)}, f32[3,4,128]{2,1,0:T(4,128)}, f32[64,16,128]{2,1,0:T(8,128)}) custom-call(f32[32,8,128]{2,1,0:T(8,128)} %all_to_all.21.part_ref, f32[16,128]{1,0:T(8,128)} %get-tuple-element.15.start_ref, f32[16,512]{1,0:T(8,128)} %get-tuple-element.14.s0_ref.planes_ref, bf16[512,128]{1,0:T(8,128)(2,1)} %get-tuple-element.16.hot_ref), custom_call_target="tpu_custom_call" | custom-call | tf_op jit(solution)/shard_map/pallas_call | solution.py:265
  61.0 5.2 %all-to-all-start.3 = ((f32[64,16,128]{2,1,0:T(8,128)}), f32[64,16,128]{2,1,0:T(8,128)S(1)}, u32[]{:S(2)}, u32[]{:S(2)}) async-start(f32[64,16,128]{2,1,0:T(8,128)} %get-tuple-element.21), calls=%async_computation.3 | async-start | bytes 1048576 | tf_op jit(solution)/shard_map/all_to_all | solution.py:573
  66.2 7.2 %shard_map.125 = (bf16[128,128,128]{2,1,0:T(8,128)(2,1)}, f32[129,8,128]{2,1,0:T(8,128)}, f32[129,8,128]{2,1,0:T(8,128)}) custom-call(f32[3,128,128]{2,1,0:T(8,128)} %bitcast.22, f32[128,128]{1,0:T(8,128)} %mass_ref.3), custom_call_target="tpu_custom_call" | custom-call | flops 10000000 | bytes 7000000 | tf_op jit(solution)/shard_map/pallas_call | solution.py:308
  73.4 0.6 convert_bitcast_fusion.tab_ref
  74.0 4.0 %shard_map.126 = f32[128,16,128]{2,1,0:T(8,128)} custom-call(s32[2]{0:T(128)} %copy-done.3, s32[32,128]{1,0:T(8,128)} %convert_bitcast_fusion.tab_ref, f32[129,8,128]{2,1,0:T(8,128)} %get-tuple-element.18.lo_ref, f32[129,8,128]{2,1,0:T(8,128)} %get-tuple-element.19.hi_ref), custom_call_target="tpu_custom_call" | custom-call | tf_op jit(solution)/shard_map/pallas_call | solution.py:343
  77.9 0.3 all-to-all-done.3
  78.2 0.0 copy-start.5
  78.2 9.5 %all-to-all-start.2 = ((f32[128,16,128]{2,1,0:T(8,128)}), f32[128,16,128]{2,1,0:T(8,128)S(1)}, u32[]{:S(2)}, u32[]{:S(2)}) async-start(f32[128,16,128]{2,1,0:T(8,128)} %shard_map.126), calls=%async_computation.2 | async-start | bytes 2097152 | tf_op jit(solution)/shard_map/all_to_all | solution.py:568
  87.7 1.1 collective-permute-start.3
  88.9 17.6 %all-to-all-done.2.leaf_ref = f32[128,16,128]{2,1,0:T(8,128)S(1)} async-done(((f32[128,16,128]{2,1,0:T(8,128)}), f32[128,16,128]{2,1,0:T(8,128)S(1)}, u32[]{:S(2)}, u32[]{:S(2)}) %all-to-all-start.2) | async-done | bytes 1048608 | tf_op jit(solution)/shard_map/all_to_all | solution.py:568
  106.5 0.0 copy-start.4
  106.5 1.0 copy-done.4
  107.5 20.3 %shard_map.127 = f32[3,4,128]{2,1,0:T(4,128)} custom-call(s32[4,128]{1,0:T(4,128)} %bitcast.31, f32[128,16,128]{2,1,0:T(8,128)} %copy-done.4, f32[3,4,128]{2,1,0:T(4,128)} %get-tuple-element.17.pos_ref, f32[3,4,128]{2,1,0:T(4,128)} %get-tuple-element.20.mid_ref), custom_call_target="tpu_custom_call" | custom-call | flops 6442450944 | bytes 1048576 | tf_op jit(solution)/shard_map/pallas_call | solution.py:472
  127.8 0.0 copy-done.5
  127.8 0.0 collective-permute-done.3
  127.8 0.0 copy-start.6
  127.8 0.8 copy-done.6
  128.6 22.1 %shard_map.128 = f32[3,128,128]{2,1,0:T(8,128)} custom-call(s32[2]{0:T(128)} %copy-done.3, s32[32,128]{1,0:T(8,128)} %convert_bitcast_fusion.tab_ref, f32[64,2,8,128]{3,2,1,0:T(8,128)} %bitcast.21, f32[64,2,8,128]{3,2,1,0:T(8,128)} %bitcast.32, bf16[128,128,128]{2,1,0:T(8,128)(2,1)} %get-tuple-element.22.g_ref, f32[3,128,128]{2,1,0:T(8,128)} %bitcast.23), custom_call_target="tpu_custom_call" | custom-call | flops 6442450944 | bytes 1048576 | tf_op jit(solution)/shard_map/pallas_call | solution.py:523
  (1 shorter events, 0.0 us)
Async XLA Ops:
  2.2 5.9 %collective-permute-start.2 = (f32[16,512]{1,0:T(8,128)}, f32[16,512]{1,0:T(8,128)S(1)}, u32[]{:S(2)}, u32[]{:S(2)}) collective-permute-start(f32[16,512]{1,0:T(8,128)} %get-tuple-element.14.s0_ref.planes_ref), channel_id=1, source_target_pairs={{0,96},{32,0},{64,32},{96,64},{1,97},{33,1},{65,33},{97,65},{2,98}... | collective-permute-start | bytes 98312 | tf_op jit(solution)/shard_map/ppermute | solution.py:562
  6.8 4.5 %collective-permute-start.1 = (f32[16,512]{1,0:T(8,128)}, f32[16,512]{1,0:T(8,128)S(1)}, u32[]{:S(2)}, u32[]{:S(2)}) collective-permute-start(f32[16,512]{1,0:T(8,128)} %get-tuple-element.14.s0_ref.planes_ref), channel_id=1, source_target_pairs={{0,64},{32,96},{64,0},{96,32},{1,65},{33,97},{65,1},{97,33},{2,66}... | collective-permute-start | bytes 98312 | tf_op jit(solution)/shard_map/ppermute | solution.py:562
  6.8 4.5 %collective-permute-start = (f32[16,512]{1,0:T(8,128)}, f32[16,512]{1,0:T(8,128)S(1)}, u32[]{:S(2)}, u32[]{:S(2)}) collective-permute-start(f32[16,512]{1,0:T(8,128)} %get-tuple-element.14.s0_ref.planes_ref), channel_id=1, source_target_pairs={{0,32},{32,64},{64,96},{96,0},{1,33},{33,65},{65,97},{97,1},{2,34}... | collective-permute-start | bytes 98312 | tf_op jit(solution)/shard_map/ppermute | solution.py:562
  7.6 39.9 %copy-start.3 = (s32[2]{0:T(128)}, s32[2]{0:T(128)S(1)}, u32[]{:S(2)}) copy-start(s32[2]{0:T(128)S(1)} %pad_add_fusion.row_ref.here_ref) | copy-start | bytes 28
  11.3 0.8 copy-start
  12.1 0.7 copy-start.2
  30.1 0.8 copy-start.1
  61.0 17.2 %all-to-all-start.3 = ((f32[64,16,128]{2,1,0:T(8,128)}), f32[64,16,128]{2,1,0:T(8,128)S(1)}, u32[]{:S(2)}, u32[]{:S(2)}) async-start(f32[64,16,128]{2,1,0:T(8,128)} %get-tuple-element.21), calls=%async_computation.3 | async-start | bytes 1048576 | tf_op jit(solution)/shard_map/all_to_all | solution.py:573
  78.2 49.5 %copy-start.5 = (f32[64,16,128]{2,1,0:T(8,128)}, f32[64,16,128]{2,1,0:T(8,128)S(1)}, u32[]{:S(2)}) copy-start(f32[64,16,128]{2,1,0:T(8,128)S(1)} %all-to-all-done.3) | copy-start | bytes 1572868
  78.2 28.3 %all-to-all-start.2 = ((f32[128,16,128]{2,1,0:T(8,128)}), f32[128,16,128]{2,1,0:T(8,128)S(1)}, u32[]{:S(2)}, u32[]{:S(2)}) async-start(f32[128,16,128]{2,1,0:T(8,128)} %shard_map.126), calls=%async_computation.2 | async-start | bytes 2097152 | tf_op jit(solution)/shard_map/all_to_all | solution.py:568
  87.7 40.1 %collective-permute-start.3 = (f32[64,16,128]{2,1,0:T(8,128)S(1)}, f32[64,16,128]{2,1,0:T(8,128)S(1)}, u32[]{:S(2)}, u32[]{:S(2)}) collective-permute-start(f32[64,16,128]{2,1,0:T(8,128)S(1)} %all-to-all-done.3), channel_id=1, source_target_pairs={{0,1},{1,0},{2,3},{3,2},{4,5},{5,4},{6,7},{7,6},{8,9},{9,8},{10,11... | collective-permute-start | bytes 1572872 | tf_op jit(solution)/shard_map/ppermute | solution.py:574
  106.5 1.0 copy-start.4
  127.8 0.8 copy-start.6

commit v3 on v2

--- a/solution.py
+++ b/solution.py
@@ -21,6 +21,7 @@
 NT = (((1,), (1,)), ((), ()))
 SMEM = pl.BlockSpec(memory_space=pltpu.SMEM)
 VMEM = pl.BlockSpec(memory_space=pltpu.VMEM)
+HBM = pl.BlockSpec(memory_space=pltpu.HBM)
 
 
 def grant(mib):
@@ -55,7 +56,7 @@
 
 
 def pre_kernel(pos_ref, vel_ref, acc_ref, jerk_ref, mass_ref, idx_ref, leaf_ref, block_ref,
-               planes_ref, act_ref, start_ref, hot_ref):
+               planes_ref, start_ref, hot_ref):
     nb = mass_ref.shape[0]
     lanes = lambda ref, q: jnp.concatenate([ref[q, b : b + 1, :] for b in range(nb)], 1)
     rows = lambda ref: jnp.concatenate([lanes(ref, q) for q in range(3)], 0)
@@ -65,7 +66,7 @@
     zero1 = jnp.zeros((1, pos.shape[1]), F32)
     planes_ref[0:8, :] = jnp.concatenate([x, v, flat(mass_ref), zero1], 0)
     lists = [flat(leaf_ref).astype(F32), flat(block_ref).astype(F32)]
-    planes_ref[8:16, :] = jnp.concatenate(lists + [zero1] * 6, 0)
+    planes_ref[8:10, :] = jnp.concatenate(lists, 0)
     hot = chosen_hot(idx_ref[...], pos.shape[1])
     hot_ref[...] = hot
     zero4 = jnp.zeros((4, pos.shape[1]), F32)
@@ -75,7 +76,8 @@
     )
     start_ref[...] = at
     ax, av = predicted(at[0:3], at[3:6], at[6:9], at[9:12])
-    act_ref[...] = jnp.concatenate([ax, av, jnp.zeros((2, at.shape[1]), F32)], 0)
+    rest = jnp.zeros((6, pos.shape[1] - at.shape[1]), F32)
+    planes_ref[10:16, :] = jnp.concatenate([jnp.concatenate([ax, av], 0), rest], 1)
 
 
 def prepare(pos, vel, acc, jerk, mass, idx, leaf, block):
@@ -85,18 +87,18 @@
         pre_kernel,
         out_shape=(
             jax.ShapeDtypeStruct((16, stars), F32),
-            jax.ShapeDtypeStruct((8, acts), F32),
             jax.ShapeDtypeStruct((16, acts), F32),
             jax.ShapeDtypeStruct((stars, acts), BF16),
         ),
     )(pos, vel, acc, jerk, mass, idx, leaf, block)
 
 
-def address_kernel(cols, row_ref, act_ref, s0_ref, s1_ref, s2_ref, s3_ref, out_ref):
+def address_kernel(row_ref, s0_ref, s1_ref, s2_ref, s3_ref, out_ref):
+    cols = out_ref.shape[0]
     refs = (s0_ref, s1_ref, s2_ref, s3_ref)
     slots = s0_ref.shape[1] // 128
     table = [
-        ref[q : q + 1, 128 * s : 128 * s + 128]
+        ref[8 + q : 9 + q, 128 * s : 128 * s + 128]
         for q in range(2)
         for ref in refs
         for s in range(slots)
@@ -104,23 +106,20 @@
     table.append(jnp.zeros((128 - len(table), 128), F32))
     shift = (128 - cols * row_ref[0]) & 127
     turned = pltpu.roll(jnp.concatenate(table, 0), shift, 1).T
+    active = s0_ref[10:16, 0:128]
     for c in range(cols):
-        out_ref[c, 0:6, :] = act_ref[0:6, :]
+        out_ref[c, 0:6, :] = active
         out_ref[c, 6:7, :] = turned[c : c + 1, :]
         out_ref[c, 7:8, :] = jnp.zeros((1, 128), F32)
 
 
-def address(row, active, stars, cols):
-    lists = pl.BlockSpec((8, stars[0].shape[1]), lambda i: (1, 0))
-    whole = pl.BlockSpec(active.shape, lambda i: (0, 0))
-    return pl.pallas_call(
-        functools.partial(address_kernel, cols),
-        grid=(1,),
-        in_specs=[SMEM, whole] + [lists] * len(stars),
-        out_specs=pl.BlockSpec((cols,) + active.shape, lambda i: (0, 0, 0)),
-        out_shape=jax.ShapeDtypeStruct((cols,) + active.shape, F32),
+def address(row, stars, cols):
+    return pl.pallas_call(
+        address_kernel,
+        in_specs=[SMEM] + [VMEM] * len(stars),
+        out_shape=jax.ShapeDtypeStruct((cols, 8, 128), F32),
         compiler_params=grant(8),
-    )(row, active, *stars)
+    )(row, *stars)
 
 
 def pair_kernel(width, act_ref, s0_ref, s1_ref, s2_ref, s3_ref, out_ref,
@@ -286,75 +285,86 @@
     return jnp.concatenate(low + high, 0).T.astype(BF16)
 
 
-def leaf_kernel(pos_ref, mass_ref, g_ref, lo_ref, hi_ref):
-    nl = mass_ref.shape[0]
+def leaf_kernel(first, pos_ref, mass_ref, g_ref, lo_ref):
     z4 = jnp.zeros((4, 128), F32)
 
-    def body(l, carry):
+    def body(i, carry):
+        l = first + i
         g = jnp.concatenate([pos_ref[q, pl.ds(l, 1), :] for q in range(3)], 0)
-        m = mass_ref[pl.ds(l, 1), :]
-        g_ref[l] = target_terms(g)
-        lo_ref[l] = jnp.concatenate([g, m, z4], 0)
-        hi_ref[l] = jnp.concatenate([z4, g, m], 0)
+        g_ref[i] = target_terms(g)
+        lo_ref[i] = jnp.concatenate([g, mass_ref[pl.ds(l, 1), :], z4], 0)
         return carry
 
-    lax.fori_loop(0, nl, body, 0, unroll=4)
-    lo_ref[nl] = jnp.zeros((8, 128), F32)
-    hi_ref[nl] = jnp.zeros((8, 128), F32)
-
-
-def leaf_prep(pos, mass):
-    nl = mass.shape[0]
-    return pl.pallas_call(
-        leaf_kernel,
+    lax.fori_loop(0, g_ref.shape[0], body, 0, unroll=4)
+
+
+def leaf_prep(pos, mass, part, parts):
+    nl = mass.shape[0] // parts
+    return pl.pallas_call(
+        functools.partial(leaf_kernel, part * nl),
         out_shape=(
             jax.ShapeDtypeStruct((nl, 128, 128), BF16),
-            jax.ShapeDtypeStruct((nl + 1, 8, 128), F32),
-            jax.ShapeDtypeStruct((nl + 1, 8, 128), F32),
+            jax.ShapeDtypeStruct((nl, 8, 128), F32),
         ),
         cost_estimate=pl.CostEstimate(
-            flops=10**7, transcendentals=0, bytes_accessed=7 * 10**6
+            flops=10**7, transcendentals=0, bytes_accessed=3 * 10**6
         ),
     )(pos, mass)
 
 
-def listed(row, d):
-    return d & 31, 4 * ((row - lax.shift_right_logical(d, 5)) & 3)
-
-
-def fetch_kernel(row_ref, tab_ref, lo_ref, hi_ref, out_ref):
+def gathered(parts, into, sems):
+    n = parts[0].shape[0]
+    return [
+        pltpu.make_async_copy(p, into.at[i * n : (i + 1) * n], sems.at[i])
+        for i, p in enumerate(parts)
+    ]
+
+
+def fetch_kernel(rows, row_ref, tab_ref, *refs):
+    parts = refs[:-3]
+    out_ref, lo_ref, sems = refs[-3:]
     nl = lo_ref.shape[0] - 1
-    row = row_ref[0]
-
-    def body(d, carry):
-        c, k = listed(row, d)
-        for h in range(2):
-            a = tab_ref[c, k + 2 * h]
-            b = tab_ref[c, k + 2 * h + 1]
-            out_ref[d, 8 * h : 8 * h + 8, :] = (
-                lo_ref[jnp.where(a < 0, nl, a)] + hi_ref[jnp.where(b < 0, nl, b)]
-            )
-        return carry
-
-    lax.fori_loop(0, out_ref.shape[0], body, 0, unroll=8)
-
-
-def fetch(row, table, lo, hi, sources):
-    return pl.pallas_call(
-        fetch_kernel,
-        in_specs=[SMEM] * 2 + [VMEM] * 2,
+    copies = gathered(parts, lo_ref, sems)
+    for copy in copies:
+        copy.start()
+    lo_ref[nl] = jnp.zeros((8, 128), F32)
+    for copy in copies:
+        copy.wait()
+    cols = out_ref.shape[0] // rows
+    for r in range(rows):
+        k = 4 * ((row_ref[0] - r) & 3)
+
+        def body(c, carry):
+            for h in range(2):
+                a = lo_ref[tab_ref[c, k + 2 * h]]
+                b = lo_ref[tab_ref[c, k + 2 * h + 1]]
+                out_ref[r * cols + c, 8 * h : 8 * h + 8, :] = a + pltpu.roll(b, 4, 0)
+            return carry
+
+        lax.fori_loop(0, cols, body, 0, unroll=8)
+
+
+def fetch(row, table, parts, rows, sources):
+    nl = sum(p.shape[0] for p in parts)
+    return pl.pallas_call(
+        functools.partial(fetch_kernel, rows),
+        in_specs=[SMEM] * 2 + [HBM] * len(parts),
         out_shape=jax.ShapeDtypeStruct((sources, 16, 128), F32),
-    )(row, table, lo, hi)
-
-
-def attract(G, ng, bodies, targets, g_ref, acc_ref, t_ref, s_ref, v_ref):
+        scratch_shapes=[
+            pltpu.VMEM((nl + 1, 8, 128), F32),
+            pltpu.SemaphoreType.DMA((len(parts),)),
+        ],
+    )(row, table, *parts)
+
+
+def attract(G, ng, fine, bodies, targets, ready, g_ref, acc_ref, t_ref, s_ref, v_ref):
     acc_ref[...] = jnp.zeros_like(acc_ref)
-    t_ref[...] = jnp.zeros_like(t_ref)
     r8 = lax.broadcasted_iota(I32, (8, 128), 0)
     low = r8 < 4
     q4 = r8 & 3
     one = jnp.ones((8, 128), F32)
     zero8 = jnp.zeros((8, 128), F32)
+    zero64 = jnp.zeros((64, 128), BF16)
 
     def prep(g, b, j):
         s = bodies(g, j, low)
@@ -364,35 +374,40 @@
         x2 = x2 + jnp.where((r8 & 2) == 0, pltpu.roll(x2, 6, 0), pltpu.roll(x2, 2, 0))
         n1, n2, n3 = split3(x2)
         t1 = jnp.where(q4 == 0, n1, jnp.where(q4 == 1, n2, n3))
-        T = jnp.concatenate([s1, s2, s3, s1, s2, s1, t1, one], 0).astype(BF16)
-        t_ref[b, j, 0:64, 0:128] = T
-        t_ref[b, j, 64:128, 128:256] = T
         m = jnp.where(
             low,
             jnp.broadcast_to(s[3:4], (8, 128)),
             jnp.broadcast_to(s[7:8], (8, 128)),
         )
-        m1, m2, m3 = split3(jnp.where(q4 == 3, s, s * m))
-        s_ref[b, j] = jnp.concatenate([m1, m2, m3, zero8], 0).astype(BF16)
+        for q, t in enumerate((s1, s2, s3, t1)):
+            t_ref[b, j, 8 * q : 8 * q + 8, :] = t
+        for q, t in enumerate(split3(jnp.where(q4 == 3, s, s * m))):
+            s_ref[b, j, 8 * q : 8 * q + 8, :] = t
 
     def force(g, b, j):
         la, lb = targets(g, j)
         lane = lax.broadcasted_iota(I32, (128, 128), 1)
         L = jnp.where(lane < 64, g_ref[la], g_ref[lb])
-        inv = lax.rsqrt(jnp.dot(L, t_ref[b, j], preferred_element_type=F32))
-        u = inv * inv * inv
+        s1, s2, s3, t1 = (t_ref[b, j, 8 * q : 8 * q + 8, :] for q in range(4))
+        T = jnp.concatenate([s1, s2, s3, s1, s2, s1, t1, one], 0).astype(BF16)
+        W = jnp.concatenate(
+            [jnp.concatenate([T, zero64], 1), jnp.concatenate([zero64, T], 1)], 0
+        )
+        inv = lax.rsqrt(jnp.dot(L, W, preferred_element_type=F32))
+        v_ref[b, j] = inv * inv * inv
+
+    def sums(g, b, j):
+        S = jnp.concatenate([s_ref[b, j], zero8], 0).astype(BF16)
+        u = v_ref[b, j]
         hi = u.astype(BF16)
-        lo = (u - hi.astype(F32)).astype(BF16)
-        v_ref[b, j, 0:128, 0:128] = hi[:, :128]
-        v_ref[b, j, 0:128, 128:256] = lo[:, :128]
-        v_ref[b, j, 128:256, 0:128] = hi[:, 128:]
-        v_ref[b, j, 128:256, 128:256] = lo[:, 128:]
-
-    def sums(g, b, j):
-        S = s_ref[b, j]
-        f = lax.dot_general(
-            jnp.concatenate([S, S], 1), v_ref[b, j], NT, preferred_element_type=F32
-        )
+        if fine:
+            lo = (u - hi.astype(F32)).astype(BF16)
+            S = jnp.concatenate([S, S], 1)
+            V = [jnp.concatenate([t[:, :128] for t in (hi, lo)], 1)]
+            V.append(jnp.concatenate([t[:, 128:] for t in (hi, lo)], 1))
+        else:
+            V = [hi[:, :128], hi[:, 128:]]
+        f = lax.dot_general(S, jnp.concatenate(V, 0), NT, preferred_element_type=F32)
         return targets(g, j) + (sum_parts(f[0:24]),)
 
     def step(g, b, more, more2):
@@ -409,9 +424,10 @@
 
     for j in range(G):
         prep(0, 0, j)
+        prep(1, 1, j)
+    ready()
     for j in range(G):
         force(0, 0, j)
-        prep(1, 1, j)
 
     def body(i, carry):
         step(2 * i, 0, True, True)
@@ -426,9 +442,9 @@
 def attract_scratch(targets, G):
     return [
         pltpu.VMEM((targets, 8, 128), F32),
-        pltpu.VMEM((2, G, 128, 256), BF16),
-        pltpu.VMEM((2, G, 32, 128), BF16),
-        pltpu.VMEM((2, G, 256, 256), BF16),
+        pltpu.VMEM((2, G, 32, 128), F32),
+        pltpu.VMEM((2, G, 24, 128), F32),
+        pltpu.VMEM((2, G, 128, 256), F32),
     ]
 
 
@@ -458,7 +474,7 @@
         h = 8 * (j % 2)
         return leaf_ref[g * (G // 2) + j // 2, h : h + 8, :]
 
-    attract(G, 2 * leaf_ref.shape[0] // G, bodies, where, g_ref, *scratch)
+    attract(G, 2 * leaf_ref.shape[0] // G, False, bodies, where, lambda: None, g_ref, *scratch)
     for b in range(nb):
         a = acc_ref[b]
         a = a[0:4] + a[4:8]
@@ -467,7 +483,7 @@
             vel_ref[q, b : b + 1, :] = mid_ref[q, b : b + 1, :] + STEP * kick[q : q + 1]
 
 
-def kicks(block, leaves, pos, mid, G=4):
+def kicks(block, leaves, pos, mid, G=16):
     nb = pos.shape[1]
     return pl.pallas_call(
         functools.partial(kick_kernel, G),
@@ -478,11 +494,24 @@
     )(block, leaves, pos, mid)
 
 
-def pull_kernel(G, scale, here_ref, tab_ref, own_ref, other_ref, g_ref, gpos_ref,
-                pull_ref, *scratch):
+def pull_kernel(G, scale, nparts, here_ref, tab_ref, own_ref, other_ref, *refs):
+    parts = refs[:nparts]
+    far_ref, pull_ref, g_ref, gpos_ref, sems = refs[nparts : nparts + 5]
+    scratch = refs[nparts + 5 :]
     acc_ref = scratch[0]
     row = here_ref[0]
     core = here_ref[1]
+    copies = gathered(parts, g_ref, sems)
+    copies.append(pltpu.make_async_copy(far_ref, gpos_ref, sems.at[nparts]))
+    for copy in copies:
+        copy.start()
+
+    def ready():
+        for copy in copies:
+            copy.wait()
+
+    def listed(row, d):
+        return d & 31, 4 * ((row - lax.shift_right_logical(d, 5)) & 3)
 
     def source(g, j):
         i = g * (G // 4) + j // 4
@@ -492,20 +521,21 @@
 
     def where(g, j):
         _, _, c, k = source(g, j)
-        return jnp.maximum(tab_ref[c, k], 0), jnp.maximum(tab_ref[c, k + 1], 0)
+        last = g_ref.shape[0] - 1
+        return jnp.minimum(tab_ref[c, k], last), jnp.minimum(tab_ref[c, k + 1], last)
 
     def bodies(g, j, low):
         ref, i, c, k = source(g, j)
         a = tab_ref[c, 16 + k]
         b = tab_ref[c, 16 + k + 1]
-        ta = ref[i, lax.shift_right_logical(jnp.maximum(a, 0), 1)]
-        tb = ref[i, lax.shift_right_logical(jnp.maximum(b, 0), 1)]
+        ta = ref[i, lax.shift_right_logical(a, 1) & 1]
+        tb = ref[i, lax.shift_right_logical(b, 1) & 1]
         ta = jnp.where((a & 1) == 1, pltpu.roll(ta, 4, 0), ta)
         tb = jnp.where((b & 1) == 1, tb, pltpu.roll(tb, 4, 0))
-        return jnp.where(jnp.where(low, a, b) < 0, 0.0, jnp.where(low, ta, tb))
+        return jnp.where(jnp.where(low, a, b) > 3, 0.0, jnp.where(low, ta, tb))
 
     ng = 4 * own_ref.shape[0] // G
-    attract(G, ng, bodies, where, g_ref, *scratch)
+    attract(G, ng, True, bodies, where, ready, g_ref, *scratch)
 
     def finish(l, carry):
         a = acc_ref[l]
@@ -518,15 +548,21 @@
     lax.fori_loop(0, g_ref.shape[0], finish, 0, unroll=8)
 
 
-def pulls(here, table, own, other, g, gpos, scale, G=4):
-    nl = g.shape[0]
-    return pl.pallas_call(
-        functools.partial(pull_kernel, G, scale),
-        in_specs=[SMEM] * 2 + [VMEM] * 4,
+def pulls(here, table, own, other, parts, gpos, scale, G=16):
+    nl = gpos.shape[1]
+    return pl.pallas_call(
+        functools.partial(pull_kernel, G, scale, len(parts)),
+        in_specs=[SMEM] * 2 + [VMEM] * 2 + [HBM] * (len(parts) + 1),
         out_shape=jax.ShapeDtypeStruct((3, nl, 128), F32),
-        scratch_shapes=attract_scratch(nl, G),
+        compiler_params=grant(51),
+        scratch_shapes=[
+            pltpu.VMEM((nl, 128, 128), BF16),
+            pltpu.VMEM(gpos.shape, F32),
+            pltpu.SemaphoreType.DMA((len(parts) + 1,)),
+        ]
+        + attract_scratch(nl, G),
         cost_estimate=attract_cost(8 * own.shape[0]),
-    )(here, table, own, other, g, gpos)
+    )(here, table, own, other, *parts, gpos)
 
 
 def local(
@@ -552,7 +588,7 @@
     here = jnp.concatenate([row, core])
     block = send_block[0].T
     gpos = turn(galaxy_pos)
-    planes, active, start, hot = prepare(
+    planes, start, hot = prepare(
         turn(star_pos), turn(star_vel), turn(star_acc), turn(star_jerk),
         star_mass, active_index, send_leaf[0].T, block,
     )
@@ -560,11 +596,14 @@
     for k in range(1, rows):
         perm = [(i, (i + k) % rows) for i in range(rows)]
         stars.append(lax.ppermute(planes, "row", perm))
-    sent = address(here, active, stars, cols)
+    sent = address(here, stars, cols)
     arrived = lax.all_to_all(sent, "col", 0, 0, tiled=True)
     table = arrived[:, 6, :].astype(I32)
-    g, lo, hi = leaf_prep(gpos, galaxy_mass)
-    leaves = fetch(here, table, lo, hi, devices)
+    table = jnp.where(table < 0, galaxy_pos.shape[0], table)
+    halves = []
+    for q in range(2):
+        halves.append(leaf_prep(gpos, galaxy_mass, q, 2))
+    leaves = fetch(here, table, [t[1] for t in halves], rows, devices)
     leaves = lax.all_to_all(leaves, both, 0, 0, tiled=True)
     parts = pair_terms(arrived, stars)
     parts = lax.all_to_all(parts, "col", 0, 0, tiled=True)
@@ -575,7 +614,9 @@
     vel_new = kicks(block, leaves, pos_new, mid)
     tiles = lambda x: x.reshape(-1, 2, 8, BLOCK)
     scale = STAR_DEV * devices / BLOCK
-    pull = pulls(here, table, tiles(own), tiles(other), g, gpos, scale)
+    pull = pulls(
+        here, table, tiles(own), tiles(other), [t[0] for t in halves], gpos, scale
+    )
     return turn(pos_new), turn(vel_new), turn(pull)
 
 

time: 151 us -> 137 us (0.907)
  Pallas kernels: 74.4 us -> 61.8 us
    pallas_call x1, Pallas kernels: 20.3 us -> 10.8 us  [kicks(): pl.pallas_call(functools.partial(kick_kernel, G), in_specs=[SMEM] + [VMEM...]
    pallas_call x4 -> x5, Pallas kernels: 33.9 us -> 30.8 us  [the longest x1 17.8 us: pulls(): pl.pallas_call(functools.partial(pull_kernel, G, scale, len(parts)), in_s...]
  transfers between devices with their start and end apart: 6 -> 6, of which waited for: 4 -> 3; matrix products, arithmetic and copies ran while one was open for 0% -> 1% of each run, Pallas kernels for 21% -> 17%
where the time goes in v3:
time: 137 us
  Pallas kernels  61.8 us (45%)
  blocking collectives  28.2 us (21%)
  starting transfers between devices  21.4 us (16%)
  waiting for transfers between devices  21.4 us (16%)
  local copies, waits for them, and re-layouts  2.52 us (2%)
    pallas_call x1, Pallas kernels, pulls(): pl.pallas_call(functools.partial(pull_kernel, G, scale, len(parts)), in_s...  17.8 us
    all_to_all x1, waiting for transfers between devices, local(): leaves = lax.all_to_all(leaves, both, 0, 0, tiled=True)  17.6 us
    all_to_all x1, blocking collectives, local(): arrived = lax.all_to_all(sent, 'col', 0, 0, tiled=True)  16.7 us
    pallas_call x1, Pallas kernels, pair_terms(): pl.pallas_call(functools.partial(pair_kernel, width), grid=(cols // group...  16.6 us
    all_to_all x1, blocking collectives, local(): parts = lax.all_to_all(parts, 'col', 0, 0, tiled=True)  11.5 us
    pallas_call x1, Pallas kernels, kicks(): pl.pallas_call(functools.partial(kick_kernel, G), in_specs=[SMEM] + [VMEM...  10.8 us
    all_to_all x1, starting transfers between devices, local(): leaves = lax.all_to_all(leaves, both, 0, 0, tiled=True)  9.79 us
    pallas_call x2, Pallas kernels, leaf_prep(): pl.pallas_call(functools.partial(leaf_kernel, part * nl), out_shape=(jax....  8.39 us
  transfers between devices with their start and end apart: 6, of which 3 were waited for; matrix products, arithmetic and copies ran while one was open for 1% of the time, Pallas kernels for 17%

profile of v3, /device:TPU:1, one launch (start us, length us, event | category | flops | bytes accessed | tf_op | source)
XLA Modules:
  0.0 136.7 jit_solution(3401329587847302388)
XLA Ops:
  0.6 1.6 %shard_map.121 = (f32[16,512]{1,0:T(8,128)}, f32[16,128]{1,0:T(8,128)}, bf16[512,128]{1,0:T(8,128)(2,1)}) custom-call(f32[3,4,128]{2,1,0:T(4,128)} %bitcast.27, f32[3,4,128]{2,1,0:T(4,128)} %bitcast.28, f32[3,4,128]{2,1,0:T(4,128)} %bitcast.29, f32[3,4,128]{2,1,0:T(4,128)} %bitcast.30, f32[4,128]{1,0:T(4,128)} %mass_ref.3, s32[1,128]{1,0:T(1,128)} %idx_ref.1, ...), custom_call_target="tpu_custom_call" | custom-call | tf_op jit(solution)/shard_map/pallas_call | solution.py:86
  2.3 4.6 %collective-permute-start.2 = (f32[16,512]{1,0:T(8,128)}, f32[16,512]{1,0:T(8,128)S(1)}, u32[]{:S(2)}, u32[]{:S(2)}) collective-permute-start(f32[16,512]{1,0:T(8,128)} %get-tuple-element.13.s0_ref.planes_ref), channel_id=1, source_target_pairs={{0,96},{32,0},{64,32},{96,64},{1,97},{33,1},{65,33},{97,65},{2,98}... | collective-permute-start | bytes 98312 | tf_op jit(solution)/shard_map/ppermute | solution.py:598
  6.8 0.0 collective-permute-start.1
  6.9 0.7 collective-permute-start
  7.5 0.1 pad_add_fusion.row_ref.here_ref
  7.6 0.0 copy-start.4
  7.6 0.6 collective-permute-done.2.s3_ref
  8.2 3.2 %collective-permute-done.1.s2_ref = f32[16,512]{1,0:T(8,128)S(1)} collective-permute-done((f32[16,512]{1,0:T(8,128)}, f32[16,512]{1,0:T(8,128)S(1)}, u32[]{:S(2)}, u32[]{:S(2)}) %collective-permute-start.1) | collective-permute-done | bytes 32800 | tf_op jit(solution)/shard_map/ppermute | solution.py:598
  11.4 0.0 collective-permute-done.s1_ref
  11.4 0.0 copy-start.1
  11.4 0.8 copy-done.1
  12.2 0.7 shard_map.122
  12.8 16.7 %all_to_all.20.act_ref = f32[32,8,128]{2,1,0:T(8,128)S(1)} all-to-all(f32[32,8,128]{2,1,0:T(8,128)S(1)} %shard_map.122), channel_id=1, replica_groups=mesh['row'=4,'col'=32] {'col'}, dimensions={0} | all-to-all | bytes 262144 | tf_op jit(solution)/shard_map/all_to_all | solution.py:600
  29.5 0.0 copy-start.2
  29.5 0.8 copy-done.2
  30.3 16.6 %shard_map.123 = f32[32,8,128]{2,1,0:T(8,128)S(1)} custom-call(f32[32,8,128]{2,1,0:T(8,128)S(1)} %all_to_all.20.act_ref, f32[16,512]{1,0:T(8,128)S(1)} %copy-done.2, f32[16,512]{1,0:T(8,128)S(1)} %collective-permute-done.s1_ref, f32[16,512]{1,0:T(8,128)S(1)} %collective-permute-done.1.s2_ref, f32[16,512]{1,0:T(8,128)S(1)} %collective-permute-done.2.s3_ref), custom_call_target="tpu_custom_call" | custom-call | flops 8589934592 | bytes 262144 | tf_op jit(solution)/shard_map/pallas_call | solution.py:213
  46.9 0.0 copy-done.4
  46.9 11.5 %all_to_all.21.part_ref = f32[32,8,128]{2,1,0:T(8,128)} all-to-all(f32[32,8,128]{2,1,0:T(8,128)S(1)} %shard_map.123), channel_id=1, replica_groups=mesh['row'=4,'col'=32] {'col'}, dimensions={0} | all-to-all | bytes 262144 | tf_op jit(solution)/shard_map/all_to_all | solution.py:609
  58.4 2.0 %shard_map.124 = (f32[3,4,128]{2,1,0:T(4,128)}, f32[3,4,128]{2,1,0:T(4,128)}, f32[64,16,128]{2,1,0:T(8,128)}) custom-call(f32[32,8,128]{2,1,0:T(8,128)} %all_to_all.21.part_ref, f32[16,128]{1,0:T(8,128)} %get-tuple-element.14.start_ref, f32[16,512]{1,0:T(8,128)} %get-tuple-element.13.s0_ref.planes_ref, bf16[512,128]{1,0:T(8,128)(2,1)} %get-tuple-element.15.hot_ref), custom_call_target="tpu_custom_call" | custom-call | tf_op jit(solution)/shard_map/pallas_call | solution.py:264
  60.4 5.2 %all-to-all-start.3 = ((f32[64,16,128]{2,1,0:T(8,128)}), f32[64,16,128]{2,1,0:T(8,128)S(1)}, u32[]{:S(2)}, u32[]{:S(2)}) async-start(f32[64,16,128]{2,1,0:T(8,128)} %get-tuple-element.20), calls=%async_computation.3 | async-start | bytes 1048576 | tf_op jit(solution)/shard_map/all_to_all | solution.py:612
  65.6 4.2 %shard_map.126 = (bf16[64,128,128]{2,1,0:T(8,128)(2,1)}, f32[64,8,128]{2,1,0:T(8,128)}) custom-call(f32[3,128,128]{2,1,0:T(8,128)} %bitcast.21, f32[128,128]{1,0:T(8,128)} %mass_ref.5), custom_call_target="tpu_custom_call" | custom-call | flops 10000000 | bytes 3000000 | tf_op jit(solution)/shard_map/pallas_call | solution.py:303
  69.8 4.2 %shard_map.125 = (bf16[64,128,128]{2,1,0:T(8,128)(2,1)}, f32[64,8,128]{2,1,0:T(8,128)}) custom-call(f32[3,128,128]{2,1,0:T(8,128)} %bitcast.22, f32[128,128]{1,0:T(8,128)} %mass_ref.5), custom_call_target="tpu_custom_call" | custom-call | flops 10000000 | bytes 3000000 | tf_op jit(solution)/shard_map/pallas_call | solution.py:303
  74.0 0.6 compare_select_fusion.tab_ref
  74.6 3.9 %shard_map.127 = f32[128,16,128]{2,1,0:T(8,128)} custom-call(s32[2]{0:T(128)} %copy-done.4, s32[32,128]{1,0:T(8,128)} %compare_select_fusion.tab_ref, f32[64,8,128]{2,1,0:T(8,128)} %get-tuple-element.17.refs_0_, f32[64,8,128]{2,1,0:T(8,128)} %get-tuple-element.18.refs_1_), custom_call_target="tpu_custom_call" | custom-call | tf_op jit(solution)/shard_map/pallas_call | solution.py:349
  78.5 0.0 all-to-all-done.3
  78.5 9.8 %all-to-all-start.2 = ((f32[128,16,128]{2,1,0:T(8,128)}), f32[128,16,128]{2,1,0:T(8,128)S(1)}, u32[]{:S(2)}, u32[]{:S(2)}) async-start(f32[128,16,128]{2,1,0:T(8,128)} %shard_map.127), calls=%async_computation.2 | async-start | bytes 2097152 | tf_op jit(solution)/shard_map/all_to_all | solution.py:607
  88.3 1.1 collective-permute-start.3
  89.5 17.6 %all-to-all-done.2.leaf_ref = f32[128,16,128]{2,1,0:T(8,128)S(1)} async-done(((f32[128,16,128]{2,1,0:T(8,128)}), f32[128,16,128]{2,1,0:T(8,128)S(1)}, u32[]{:S(2)}, u32[]{:S(2)}) %all-to-all-start.2) | async-done | bytes 1048608 | tf_op jit(solution)/shard_map/all_to_all | solution.py:607
  107.1 0.0 copy-start.6
  107.1 1.0 copy-done.6
  108.1 0.0 copy-start
  108.1 0.0 copy-start.3
  108.1 0.0 copy-start.5
  108.1 10.8 %shard_map.128 = f32[3,4,128]{2,1,0:T(4,128)} custom-call(s32[4,128]{1,0:T(4,128)} %bitcast.33, f32[128,16,128]{2,1,0:T(8,128)} %copy-done.6, f32[3,4,128]{2,1,0:T(4,128)} %get-tuple-element.16.pos_ref, f32[3,4,128]{2,1,0:T(4,128)} %get-tuple-element.19.mid_ref), custom_call_target="tpu_custom_call" | custom-call | flops 6442450944 | bytes 1048576 | tf_op jit(solution)/shard_map/pallas_call | solution.py:488
  118.9 0.0 collective-permute-done.3
  118.9 0.0 copy-done
  118.9 0.0 copy-done.3
  118.9 0.0 copy-done.5
  118.9 17.8 %shard_map.129 = f32[3,128,128]{2,1,0:T(8,128)} custom-call(s32[2]{0:T(128)S(1)} %copy-done.5, s32[32,128]{1,0:T(8,128)S(1)} %copy-done.3, f32[64,2,8,128]{3,2,1,0:T(8,128)S(1)} %bitcast.24, f32[64,2,8,128]{3,2,1,0:T(8,128)S(1)} %bitcast.25, bf16[64,128,128]{2,1,0:T(8,128)(2,1)} %get-tuple-element.21.refs_0_, ...), custom_call_target="tpu_custom_call" | custom-call | flops 6442450944 | bytes 1048576 | tf_op jit(solution)/shard_map/pallas_call | solution.py:553
  (1 shorter events, 0.0 us)
Async XLA Ops:
  2.3 5.9 %collective-permute-start.2 = (f32[16,512]{1,0:T(8,128)}, f32[16,512]{1,0:T(8,128)S(1)}, u32[]{:S(2)}, u32[]{:S(2)}) collective-permute-start(f32[16,512]{1,0:T(8,128)} %get-tuple-element.13.s0_ref.planes_ref), channel_id=1, source_target_pairs={{0,96},{32,0},{64,32},{96,64},{1,97},{33,1},{65,33},{97,65},{2,98}... | collective-permute-start | bytes 98312 | tf_op jit(solution)/shard_map/ppermute | solution.py:598
  6.8 4.5 %collective-permute-start.1 = (f32[16,512]{1,0:T(8,128)}, f32[16,512]{1,0:T(8,128)S(1)}, u32[]{:S(2)}, u32[]{:S(2)}) collective-permute-start(f32[16,512]{1,0:T(8,128)} %get-tuple-element.13.s0_ref.planes_ref), channel_id=1, source_target_pairs={{0,64},{32,96},{64,0},{96,32},{1,65},{33,97},{65,1},{97,33},{2,66}... | collective-permute-start | bytes 98312 | tf_op jit(solution)/shard_map/ppermute | solution.py:598
  6.9 4.5 %collective-permute-start = (f32[16,512]{1,0:T(8,128)}, f32[16,512]{1,0:T(8,128)S(1)}, u32[]{:S(2)}, u32[]{:S(2)}) collective-permute-start(f32[16,512]{1,0:T(8,128)} %get-tuple-element.13.s0_ref.planes_ref), channel_id=1, source_target_pairs={{0,32},{32,64},{64,96},{96,0},{1,33},{33,65},{65,97},{97,1},{2,34}... | collective-permute-start | bytes 98312 | tf_op jit(solution)/shard_map/ppermute | solution.py:598
  7.6 39.2 %copy-start.4 = (s32[2]{0:T(128)}, s32[2]{0:T(128)S(1)}, u32[]{:S(2)}) copy-start(s32[2]{0:T(128)S(1)} %pad_add_fusion.row_ref.here_ref) | copy-start | bytes 28
  11.4 0.8 copy-start.1
  29.5 0.8 copy-start.2
  60.4 18.1 %all-to-all-start.3 = ((f32[64,16,128]{2,1,0:T(8,128)}), f32[64,16,128]{2,1,0:T(8,128)S(1)}, u32[]{:S(2)}, u32[]{:S(2)}) async-start(f32[64,16,128]{2,1,0:T(8,128)} %get-tuple-element.20), calls=%async_computation.3 | async-start | bytes 1048576 | tf_op jit(solution)/shard_map/all_to_all | solution.py:612
  78.5 28.6 %all-to-all-start.2 = ((f32[128,16,128]{2,1,0:T(8,128)}), f32[128,16,128]{2,1,0:T(8,128)S(1)}, u32[]{:S(2)}, u32[]{:S(2)}) async-start(f32[128,16,128]{2,1,0:T(8,128)} %shard_map.127), calls=%async_computation.2 | async-start | bytes 2097152 | tf_op jit(solution)/shard_map/all_to_all | solution.py:607
  88.3 30.5 %collective-permute-start.3 = (f32[64,16,128]{2,1,0:T(8,128)S(1)}, f32[64,16,128]{2,1,0:T(8,128)S(1)}, u32[]{:S(2)}, u32[]{:S(2)}) collective-permute-start(f32[64,16,128]{2,1,0:T(8,128)S(1)} %all-to-all-done.3), channel_id=1, source_target_pairs={{0,1},{1,0},{2,3},{3,2},{4,5},{5,4},{6,7},{7,6},{8,9},{9,8},{10,11... | collective-permute-start | bytes 1572872 | tf_op jit(solution)/shard_map/ppermute | solution.py:613
  107.1 1.0 copy-start.6
  108.1 10.8 %copy-start = (f32[128,3,128]{2,0,1:T(8,128)S(1)}, f32[128,3,128]{2,0,1:T(8,128)}, u32[]{:S(2)}) copy-start(f32[128,3,128]{2,0,1:T(8,128)} %param.18) | copy-start | bytes 589828
  108.1 10.8 %copy-start.3 = (s32[32,128]{1,0:T(8,128)S(1)}, s32[32,128]{1,0:T(8,128)}, u32[]{:S(2)}) copy-start(s32[32,128]{1,0:T(8,128)} %compare_select_fusion.tab_ref) | copy-start | bytes 49156
  108.1 10.8 %copy-start.5 = (s32[2]{0:T(128)S(1)}, s32[2]{0:T(128)}, u32[]{:S(2)}) copy-start(s32[2]{0:T(128)} %copy-done.4) | copy-start | bytes 28

commit v4 on v3

--- a/solution.py
+++ b/solution.py
@@ -32,8 +32,7 @@
     a = x.astype(BF16).astype(F32)
     r = x - a
     b = r.astype(BF16).astype(F32)
-    c = (r - b).astype(BF16).astype(F32)
-    return a, b, c
+    return a, b, r - b
 
 
 def predicted(pos, vel, acc, jerk):
@@ -56,7 +55,7 @@
 
 
 def pre_kernel(pos_ref, vel_ref, acc_ref, jerk_ref, mass_ref, idx_ref, leaf_ref, block_ref,
-               planes_ref, start_ref, hot_ref):
+               planes_ref, sent_ref, start_ref, hot_ref):
     nb = mass_ref.shape[0]
     lanes = lambda ref, q: jnp.concatenate([ref[q, b : b + 1, :] for b in range(nb)], 1)
     rows = lambda ref: jnp.concatenate([lanes(ref, q) for q in range(3)], 0)
@@ -64,9 +63,7 @@
     pos, vel, acc, jerk = (rows(r) for r in (pos_ref, vel_ref, acc_ref, jerk_ref))
     x, v = predicted(pos, vel, acc, jerk)
     zero1 = jnp.zeros((1, pos.shape[1]), F32)
-    planes_ref[0:8, :] = jnp.concatenate([x, v, flat(mass_ref), zero1], 0)
-    lists = [flat(leaf_ref).astype(F32), flat(block_ref).astype(F32)]
-    planes_ref[8:10, :] = jnp.concatenate(lists, 0)
+    planes_ref[...] = jnp.concatenate([x, v, flat(mass_ref), zero1], 0)
     hot = chosen_hot(idx_ref[...], pos.shape[1])
     hot_ref[...] = hot
     zero4 = jnp.zeros((4, pos.shape[1]), F32)
@@ -76,8 +73,14 @@
     )
     start_ref[...] = at
     ax, av = predicted(at[0:3], at[3:6], at[6:9], at[9:12])
-    rest = jnp.zeros((6, pos.shape[1] - at.shape[1]), F32)
-    planes_ref[10:16, :] = jnp.concatenate([jnp.concatenate([ax, av], 0), rest], 1)
+    lists = [leaf_ref[...].astype(F32), block_ref[...].astype(F32)]
+    targets = sent_ref.shape[0]
+    lists.append(jnp.zeros((targets - 8, targets), F32))
+    lists = jnp.concatenate(lists, 0).T
+    active = jnp.concatenate([ax, av], 0)
+    blank = jnp.zeros((1, active.shape[1]), F32)
+    for e in range(targets):
+        sent_ref[e] = jnp.concatenate([active, lists[e : e + 1, :], blank], 0)
 
 
 def prepare(pos, vel, acc, jerk, mass, idx, leaf, block):
@@ -86,43 +89,15 @@
     return pl.pallas_call(
         pre_kernel,
         out_shape=(
-            jax.ShapeDtypeStruct((16, stars), F32),
+            jax.ShapeDtypeStruct((8, stars), F32),
+            jax.ShapeDtypeStruct((block.shape[1], 8, acts), F32),
             jax.ShapeDtypeStruct((16, acts), F32),
             jax.ShapeDtypeStruct((stars, acts), BF16),
         ),
     )(pos, vel, acc, jerk, mass, idx, leaf, block)
 
 
-def address_kernel(row_ref, s0_ref, s1_ref, s2_ref, s3_ref, out_ref):
-    cols = out_ref.shape[0]
-    refs = (s0_ref, s1_ref, s2_ref, s3_ref)
-    slots = s0_ref.shape[1] // 128
-    table = [
-        ref[8 + q : 9 + q, 128 * s : 128 * s + 128]
-        for q in range(2)
-        for ref in refs
-        for s in range(slots)
-    ]
-    table.append(jnp.zeros((128 - len(table), 128), F32))
-    shift = (128 - cols * row_ref[0]) & 127
-    turned = pltpu.roll(jnp.concatenate(table, 0), shift, 1).T
-    active = s0_ref[10:16, 0:128]
-    for c in range(cols):
-        out_ref[c, 0:6, :] = active
-        out_ref[c, 6:7, :] = turned[c : c + 1, :]
-        out_ref[c, 7:8, :] = jnp.zeros((1, 128), F32)
-
-
-def address(row, stars, cols):
-    return pl.pallas_call(
-        address_kernel,
-        in_specs=[SMEM] + [VMEM] * len(stars),
-        out_shape=jax.ShapeDtypeStruct((cols, 8, 128), F32),
-        compiler_params=grant(8),
-    )(row, *stars)
-
-
-def pair_kernel(width, act_ref, s0_ref, s1_ref, s2_ref, s3_ref, out_ref,
+def pair_kernel(width, row_ref, act_ref, s0_ref, s1_ref, s2_ref, s3_ref, out_ref,
                 rs_ref, b_ref, ws_ref):
     own = s0_ref.shape[1]
     refs = (s0_ref, s1_ref, s2_ref, s3_ref)
@@ -203,31 +178,37 @@
         out_ref[q] = jnp.concatenate([acc[:, cut], jerk[:, cut], zero2[:, cut]], 0)
 
 
-def pair_terms(active, stars, group=2, width=1024):
-    cols, _, acts = active.shape
+def pair_terms(row, active, stars, cols, group=2, width=1024):
+    acts = active.shape[2]
     own = stars[0].shape[1]
     n = own * len(stars)
     ic = group * acts
-    block = pl.BlockSpec((group, 8, acts), lambda i: (i, 0, 0))
-    whole = pl.BlockSpec((8, own), lambda i: (0, 0))
+    steps = cols // group
+    whole = pl.BlockSpec((8, own), lambda i, row: (0, 0))
     return pl.pallas_call(
         functools.partial(pair_kernel, width),
-        grid=(cols // group,),
-        in_specs=[block] + [whole] * len(stars),
-        out_specs=block,
+        grid_spec=pltpu.PrefetchScalarGridSpec(
+            num_scalar_prefetch=1,
+            grid=(steps,),
+            in_specs=[
+                pl.BlockSpec((group, 8, acts), lambda i, row: (row[0] * steps + i, 0, 0))
+            ]
+            + [whole] * len(stars),
+            out_specs=pl.BlockSpec((group, 8, acts), lambda i, row: (i, 0, 0)),
+            scratch_shapes=[
+                pltpu.VMEM((n, 64), BF16),
+                pltpu.VMEM((32, n), BF16),
+                pltpu.VMEM((n, 2 * ic), BF16),
+            ],
+        ),
         out_shape=jax.ShapeDtypeStruct((cols, 8, acts), F32),
         compiler_params=grant(16),
-        scratch_shapes=[
-            pltpu.VMEM((n, 64), BF16),
-            pltpu.VMEM((32, n), BF16),
-            pltpu.VMEM((n, 2 * ic), BF16),
-        ],
         cost_estimate=pl.CostEstimate(
             flops=4 * 2 * 128 * cols * acts * n,
             transcendentals=cols * acts * n,
             bytes_accessed=4 * 2 * cols * 8 * acts,
         ),
-    )(active, *stars)
+    )(row, active, *stars)
 
 
 def correct_kernel(part_ref, start_ref, planes_ref, hot_ref, pos_ref, mid_ref, send_ref):
@@ -242,7 +223,7 @@
     x1 = x0 + (v0 + v1) * (0.5 * STEP) + (a0 - acc) * (STEP**2 / 12.0)
     one = jnp.ones((2, x1.shape[1]), F32)
     parts = split3(jnp.concatenate([x1, v1, one], 0))
-    planes = planes_ref[0:8, :]
+    planes = planes_ref[...]
     put = jnp.concatenate(parts + (jnp.zeros_like(parts[0]),), 0).astype(BF16)
     spread = sum_parts(
         lax.dot_general(put, hot_ref[...], NT, preferred_element_type=F32)[0:24]
@@ -320,41 +301,56 @@
     ]
 
 
-def fetch_kernel(rows, row_ref, tab_ref, *refs):
-    parts = refs[:-3]
-    out_ref, lo_ref, sems = refs[-3:]
-    nl = lo_ref.shape[0] - 1
-    copies = gathered(parts, lo_ref, sems)
-    for copy in copies:
-        copy.start()
-    lo_ref[nl] = jnp.zeros((8, 128), F32)
-    for copy in copies:
-        copy.wait()
-    cols = out_ref.shape[0] // rows
-    for r in range(rows):
-        k = 4 * ((row_ref[0] - r) & 3)
-
-        def body(c, carry):
-            for h in range(2):
-                a = lo_ref[tab_ref[c, k + 2 * h]]
-                b = lo_ref[tab_ref[c, k + 2 * h + 1]]
-                out_ref[r * cols + c, 8 * h : 8 * h + 8, :] = a + pltpu.roll(b, 4, 0)
-            return carry
-
-        lax.fori_loop(0, cols, body, 0, unroll=8)
-
-
-def fetch(row, table, parts, rows, sources):
-    nl = sum(p.shape[0] for p in parts)
+def fetch_kernel(arrived_ref, far_ref, out_ref, table_ref, lo_ref, tab_ref, sems):
+    nl = far_ref.shape[0]
+    n = out_ref.shape[0]
+    first = pl.program_id(0) * n
+
+    @pl.when(pl.program_id(0) == 0)
+    def _():
+        leaves = pltpu.make_async_copy(far_ref, lo_ref.at[0:nl], sems.at[0])
+        leaves.start()
+        t = arrived_ref[:, 6, :].T[0:8, :].astype(I32)
+        table_ref[...] = jnp.where(t < 0, nl, t)
+        numbers = pltpu.make_async_copy(table_ref, tab_ref, sems.at[1])
+        numbers.start()
+        lo_ref[nl] = jnp.zeros((8, 128), F32)
+        numbers.wait()
+        leaves.wait()
+
+    def body(d, carry):
+        for h in range(2):
+            a = lo_ref[tab_ref[2 * h, first + d]]
+            b = lo_ref[tab_ref[2 * h + 1, first + d]]
+            out_ref[d, 8 * h : 8 * h + 8, :] = a + pltpu.roll(b, 4, 0)
+        return carry
+
+    lax.fori_loop(0, n, body, 0, unroll=8)
+
+
+def fetch(arrived, lo, steps=4):
+    nl = lo.shape[0]
+    devices = arrived.shape[0]
+    n = devices // steps
     return pl.pallas_call(
-        functools.partial(fetch_kernel, rows),
-        in_specs=[SMEM] * 2 + [HBM] * len(parts),
-        out_shape=jax.ShapeDtypeStruct((sources, 16, 128), F32),
+        fetch_kernel,
+        grid=(steps,),
+        in_specs=[pl.BlockSpec(arrived.shape, lambda i: (0, 0, 0)), HBM],
+        out_specs=(
+            pl.BlockSpec((n, 16, 128), lambda i: (i, 0, 0)),
+            pl.BlockSpec((8, devices), lambda i: (0, 0)),
+        ),
+        out_shape=(
+            jax.ShapeDtypeStruct((devices, 16, 128), F32),
+            jax.ShapeDtypeStruct((8, devices), I32),
+        ),
+        compiler_params=grant(53),
         scratch_shapes=[
             pltpu.VMEM((nl + 1, 8, 128), F32),
-            pltpu.SemaphoreType.DMA((len(parts),)),
+            pltpu.SMEM((8, devices), I32),
+            pltpu.SemaphoreType.DMA((2,)),
         ],
-    )(row, table, *parts)
+    )(arrived, lo)
 
 
 def attract(G, ng, fine, bodies, targets, ready, g_ref, acc_ref, t_ref, s_ref, v_ref):
@@ -494,13 +490,12 @@
     )(block, leaves, pos, mid)
 
 
-def pull_kernel(G, scale, nparts, here_ref, tab_ref, own_ref, other_ref, *refs):
+def pull_kernel(G, scale, nparts, core_ref, tab_ref, own_ref, other_ref, *refs):
     parts = refs[:nparts]
     far_ref, pull_ref, g_ref, gpos_ref, sems = refs[nparts : nparts + 5]
     scratch = refs[nparts + 5 :]
     acc_ref = scratch[0]
-    row = here_ref[0]
-    core = here_ref[1]
+    core = core_ref[0]
     copies = gathered(parts, g_ref, sems)
     copies.append(pltpu.make_async_copy(far_ref, gpos_ref, sems.at[nparts]))
     for copy in copies:
@@ -510,24 +505,20 @@
         for copy in copies:
             copy.wait()
 
-    def listed(row, d):
-        return d & 31, 4 * ((row - lax.shift_right_logical(d, 5)) & 3)
-
     def source(g, j):
         i = g * (G // 4) + j // 4
         flip = (j // 2) % 2
-        c, k = listed(row, 2 * i + (core ^ flip))
-        return (own_ref, other_ref)[flip], i, c, k + 2 * (j % 2)
+        return (own_ref, other_ref)[flip], i, 2 * i + (core ^ flip), 2 * (j % 2)
 
     def where(g, j):
-        _, _, c, k = source(g, j)
+        _, _, d, h = source(g, j)
         last = g_ref.shape[0] - 1
-        return jnp.minimum(tab_ref[c, k], last), jnp.minimum(tab_ref[c, k + 1], last)
+        return jnp.minimum(tab_ref[h, d], last), jnp.minimum(tab_ref[h + 1, d], last)
 
     def bodies(g, j, low):
-        ref, i, c, k = source(g, j)
-        a = tab_ref[c, 16 + k]
-        b = tab_ref[c, 16 + k + 1]
+        ref, i, d, h = source(g, j)
+        a = tab_ref[4 + h, d]
+        b = tab_ref[5 + h, d]
         ta = ref[i, lax.shift_right_logical(a, 1) & 1]
         tb = ref[i, lax.shift_right_logical(b, 1) & 1]
         ta = jnp.where((a & 1) == 1, pltpu.roll(ta, 4, 0), ta)
@@ -548,7 +539,7 @@
     lax.fori_loop(0, g_ref.shape[0], finish, 0, unroll=8)
 
 
-def pulls(here, table, own, other, parts, gpos, scale, G=16):
+def pulls(core, table, own, other, parts, gpos, scale, G=16):
     nl = gpos.shape[1]
     return pl.pallas_call(
         functools.partial(pull_kernel, G, scale, len(parts)),
@@ -562,7 +553,7 @@
         ]
         + attract_scratch(nl, G),
         cost_estimate=attract_cost(8 * own.shape[0]),
-    )(here, table, own, other, *parts, gpos)
+    )(core, table, own, other, *parts, gpos)
 
 
 def local(
@@ -585,27 +576,21 @@
     turn = lambda x: x.transpose(1, 0, 2)
     row = lax.axis_index("row").astype(I32).reshape(1)
     core = (lax.axis_index("col") & 1).astype(I32).reshape(1)
-    here = jnp.concatenate([row, core])
     block = send_block[0].T
     gpos = turn(galaxy_pos)
-    planes, start, hot = prepare(
+    planes, sent, start, hot = prepare(
         turn(star_pos), turn(star_vel), turn(star_acc), turn(star_jerk),
         star_mass, active_index, send_leaf[0].T, block,
     )
+    arrived = lax.all_to_all(sent, both, 0, 0, tiled=True)
     stars = [planes]
     for k in range(1, rows):
         perm = [(i, (i + k) % rows) for i in range(rows)]
         stars.append(lax.ppermute(planes, "row", perm))
-    sent = address(here, stars, cols)
-    arrived = lax.all_to_all(sent, "col", 0, 0, tiled=True)
-    table = arrived[:, 6, :].astype(I32)
-    table = jnp.where(table < 0, galaxy_pos.shape[0], table)
-    halves = []
-    for q in range(2):
-        halves.append(leaf_prep(gpos, galaxy_mass, q, 2))
-    leaves = fetch(here, table, [t[1] for t in halves], rows, devices)
+    g, lo = leaf_prep(gpos, galaxy_mass, 0, 1)
+    leaves, table = fetch(arrived, lo)
     leaves = lax.all_to_all(leaves, both, 0, 0, tiled=True)
-    parts = pair_terms(arrived, stars)
+    parts = pair_terms(row, arrived, stars, cols)
     parts = lax.all_to_all(parts, "col", 0, 0, tiled=True)
     pos_new, mid, outgoing = correct(parts, start, planes, hot, nb, devices // 2)
     same_core = [[d for d in range(devices) if d % 2 == c] for c in range(2)]
@@ -615,7 +600,7 @@
     tiles = lambda x: x.reshape(-1, 2, 8, BLOCK)
     scale = STAR_DEV * devices / BLOCK
     pull = pulls(
-        here, table, tiles(own), tiles(other), [t[0] for t in halves], gpos, scale
+        core, table, tiles(own), tiles(other), [g], gpos, scale
     )
     return turn(pos_new), turn(vel_new), turn(pull)
 

time: 137 us -> 132 us (0.964)
  blocking collectives: 28.2 us -> 12.1 us
  starting transfers between devices: 21.4 us -> 29.7 us
  waiting for transfers between devices: 21.4 us -> 28.3 us
  Pallas kernels: 61.8 us -> 59.2 us
    all_to_all x1 -> x0, blocking collectives: 16.7 us -> none  [local(): arrived = lax.all_to_all(sent, 'col', 0, 0, tiled=True)]
    all_to_all x0 -> x1, starting transfers between devices: none -> 11.5 us  [local(): arrived = lax.all_to_all(sent, both, 0, 0, tiled=True)]
    all_to_all x0 -> x1, waiting for transfers between devices: none -> 5.07 us  [local(): arrived = lax.all_to_all(sent, both, 0, 0, tiled=True)]
    all_to_all x1, starting transfers between devices: 9.79 us -> 7 us  [local(): leaves = lax.all_to_all(leaves, both, 0, 0, tiled=True)]
    all_to_all x1, waiting for transfers between devices: 0.01 us -> 2.48 us  [local(): lax.all_to_all(outgoing, both, 0, 0, tiled=True, axis_index_groups=same_c...]
    pallas_call x2 -> x1, Pallas kernels: 8.39 us -> 6.71 us  [leaf_prep(): pl.pallas_call(functools.partial(leaf_kernel, part * nl), out_shape=(jax....]
    pallas_call x4 -> x3, Pallas kernels: 22.8 us -> 21.7 us  [the longest x1 16.6 us: pair_terms(): pl.pallas_call(functools.partial(pair_kernel, width), grid_spec=pltpu.Pre...]
  transfers between devices with their start and end apart: 6 -> 7, of which waited for: 3 -> 5; matrix products, arithmetic and copies ran while one was open for 1% -> 0% of each run, Pallas kernels for 17% -> 16%
where the time goes in v4:
time: 132 us
  Pallas kernels  59.2 us (45%)
  starting transfers between devices  29.7 us (22%)
  waiting for transfers between devices  28.3 us (21%)
  blocking collectives  12.1 us (9%)
  local copies, waits for them, and re-layouts  1.71 us (1%)
    all_to_all x1, waiting for transfers between devices, local(): leaves = lax.all_to_all(leaves, both, 0, 0, tiled=True)  17.6 us
    pallas_call x1, Pallas kernels, pulls(): pl.pallas_call(functools.partial(pull_kernel, G, scale, len(parts)), in_s...  17.4 us
    pallas_call x1, Pallas kernels, pair_terms(): pl.pallas_call(functools.partial(pair_kernel, width), grid_spec=pltpu.Pre...  16.6 us
    all_to_all x1, blocking collectives, local(): parts = lax.all_to_all(parts, 'col', 0, 0, tiled=True)  12.1 us
    all_to_all x1, starting transfers between devices, local(): arrived = lax.all_to_all(sent, both, 0, 0, tiled=True)  11.5 us
    pallas_call x1, Pallas kernels, kicks(): pl.pallas_call(functools.partial(kick_kernel, G), in_specs=[SMEM] + [VMEM...  11.3 us
    all_to_all x1, starting transfers between devices, local(): leaves = lax.all_to_all(leaves, both, 0, 0, tiled=True)  7 us
    pallas_call x1, Pallas kernels, leaf_prep(): pl.pallas_call(functools.partial(leaf_kernel, part * nl), out_shape=(jax....  6.71 us
  transfers between devices with their start and end apart: 7, of which 5 were waited for; matrix products, arithmetic and copies ran while one was open for 0% of the time, Pallas kernels for 16%

profile of v4, /device:TPU:1, one launch (start us, length us, event | category | flops | bytes accessed | tf_op | source)
XLA Modules:
  0.0 131.6 jit_solution(11366285879595800985)
XLA Ops:
  0.6 1.8 %shard_map.121 = (f32[8,512]{1,0:T(8,128)}, f32[128,8,128]{2,1,0:T(8,128)}, f32[16,128]{1,0:T(8,128)}, bf16[512,128]{1,0:T(8,128)(2,1)}) custom-call(f32[3,4,128]{2,1,0:T(4,128)} %bitcast.22, f32[3,4,128]{2,1,0:T(4,128)} %bitcast.23, f32[3,4,128]{2,1,0:T(4,128)} %bitcast.24, f32[3,4,128]{2,1,0:T(4,128)} %bitcast.25, f32[4,128]{1,0:T(4,128)} %mass_ref.2, ...), custom_call_target="tpu_custom_call" | custom-call | tf_op jit(solution)/shard_map/pallas_call | solution.py:89
  2.5 11.5 %all-to-all-start = ((f32[128,8,128]{2,1,0:T(8,128)}), f32[128,8,128]{2,1,0:T(8,128)S(1)}, u32[]{:S(2)}, u32[]{:S(2)}) async-start(f32[128,8,128]{2,1,0:T(8,128)} %get-tuple-element.14), calls=%async_computation | async-start | bytes 1048576 | tf_op jit(solution)/shard_map/all_to_all | solution.py:585
  14.0 1.6 %collective-permute-start = (f32[8,512]{1,0:T(8,128)}, f32[8,512]{1,0:T(8,128)S(1)}, u32[]{:S(2)}, u32[]{:S(2)}) collective-permute-start(f32[8,512]{1,0:T(8,128)} %get-tuple-element.15.s0_ref.planes_ref), channel_id=1, source_target_pairs={{0,32},{32,64},{64,96},{96,0},{1,33},{33,65},{65,97},{97,1},{2,34}... | collective-permute-start | bytes 49160 | tf_op jit(solution)/shard_map/ppermute | solution.py:589
  15.5 2.9 %collective-permute-start.1 = (f32[8,512]{1,0:T(8,128)}, f32[8,512]{1,0:T(8,128)S(1)}, u32[]{:S(2)}, u32[]{:S(2)}) collective-permute-start(f32[8,512]{1,0:T(8,128)} %get-tuple-element.15.s0_ref.planes_ref), channel_id=1, source_target_pairs={{0,64},{32,96},{64,0},{96,32},{1,65},{33,97},{65,1},{97,33},{2,66}... | collective-permute-start | bytes 49160 | tf_op jit(solution)/shard_map/ppermute | solution.py:589
  18.4 0.9 collective-permute-start.2
  19.4 0.0 collective-permute-done.s1_ref
  19.4 1.3 %collective-permute-done.1.s2_ref = f32[8,512]{1,0:T(8,128)S(1)} collective-permute-done((f32[8,512]{1,0:T(8,128)}, f32[8,512]{1,0:T(8,128)S(1)}, u32[]{:S(2)}, u32[]{:S(2)}) %collective-permute-start.1) | collective-permute-done | bytes 16416 | tf_op jit(solution)/shard_map/ppermute | solution.py:589
  20.7 1.7 %collective-permute-done.2.s3_ref = f32[8,512]{1,0:T(8,128)S(1)} collective-permute-done((f32[8,512]{1,0:T(8,128)}, f32[8,512]{1,0:T(8,128)S(1)}, u32[]{:S(2)}, u32[]{:S(2)}) %collective-permute-start.2) | collective-permute-done | bytes 16416 | tf_op jit(solution)/shard_map/ppermute | solution.py:589
  22.4 5.1 %all-to-all-done.act_ref.arrived_ref = f32[128,8,128]{2,1,0:T(8,128)S(1)} async-done(((f32[128,8,128]{2,1,0:T(8,128)}), f32[128,8,128]{2,1,0:T(8,128)S(1)}, u32[]{:S(2)}, u32[]{:S(2)}) %all-to-all-start) | async-done | bytes 524320 | tf_op jit(solution)/shard_map/all_to_all | solution.py:585
  27.5 0.0 copy-start.1
  27.5 0.7 copy-done.1
  28.2 16.6 %shard_map.122 = f32[32,8,128]{2,1,0:T(8,128)S(1)} custom-call(s32[1]{0:T(128)} %bitcast.row_ref, f32[128,8,128]{2,1,0:T(8,128)S(1)} %all-to-all-done.act_ref.arrived_ref, f32[8,512]{1,0:T(8,128)S(1)} %copy-done.1, f32[8,512]{1,0:T(8,128)S(1)} %collective-permute-done.s1_ref, f32[8,512]{1,0:T(8,128)S(1)} %collective-permute-done.1.s2_ref, ...), custom_call_target="tpu_custom_call" | custom-call | flops 8589934592 | bytes 262144 | tf_op jit(solution)/shard_map/pallas_call | solution.py:188
  44.9 12.1 %all_to_all.20.part_ref = f32[32,8,128]{2,1,0:T(8,128)} all-to-all(f32[32,8,128]{2,1,0:T(8,128)S(1)} %shard_map.122), channel_id=1, replica_groups=mesh['row'=4,'col'=32] {'col'}, dimensions={0} | all-to-all | bytes 262144 | tf_op jit(solution)/shard_map/all_to_all | solution.py:594
  57.0 2.0 %shard_map.123 = (f32[3,4,128]{2,1,0:T(4,128)}, f32[3,4,128]{2,1,0:T(4,128)}, f32[64,16,128]{2,1,0:T(8,128)}) custom-call(f32[32,8,128]{2,1,0:T(8,128)} %all_to_all.20.part_ref, f32[16,128]{1,0:T(8,128)} %get-tuple-element.16.start_ref, f32[8,512]{1,0:T(8,128)} %get-tuple-element.15.s0_ref.planes_ref, bf16[512,128]{1,0:T(8,128)(2,1)} %get-tuple-element.17.hot_ref), custom_call_target="tpu_custom_call" | custom-call | tf_op jit(solution)/shard_map/pallas_call | solution.py:245
  59.0 4.6 %all-to-all-start.3 = ((f32[64,16,128]{2,1,0:T(8,128)}), f32[64,16,128]{2,1,0:T(8,128)S(1)}, u32[]{:S(2)}, u32[]{:S(2)}) async-start(f32[64,16,128]{2,1,0:T(8,128)} %get-tuple-element.23), calls=%async_computation.3 | async-start | bytes 1048576 | tf_op jit(solution)/shard_map/all_to_all | solution.py:597
  63.7 6.7 %shard_map.124 = (bf16[128,128,128]{2,1,0:T(8,128)(2,1)}, f32[128,8,128]{2,1,0:T(8,128)}) custom-call(f32[3,128,128]{2,1,0:T(8,128)} %bitcast.19, f32[128,128]{1,0:T(8,128)} %mass_ref.3), custom_call_target="tpu_custom_call" | custom-call | flops 10000000 | bytes 3000000 | tf_op jit(solution)/shard_map/pallas_call | solution.py:284
  70.4 3.2 %shard_map.125 = (f32[128,16,128]{2,1,0:T(8,128)}, s32[8,128]{1,0:T(8,128)S(1)}) custom-call(f32[128,8,128]{2,1,0:T(8,128)S(1)} %all-to-all-done.act_ref.arrived_ref, f32[128,8,128]{2,1,0:T(8,128)} %get-tuple-element.19.far_ref), custom_call_target="tpu_custom_call" | custom-call | tf_op jit(solution)/shard_map/pallas_call | solution.py:335
  73.6 2.5 %all-to-all-done.3 = f32[64,16,128]{2,1,0:T(8,128)S(1)} async-done(((f32[64,16,128]{2,1,0:T(8,128)}), f32[64,16,128]{2,1,0:T(8,128)S(1)}, u32[]{:S(2)}, u32[]{:S(2)}) %all-to-all-start.3) | async-done | bytes 524320 | tf_op jit(solution)/shard_map/all_to_all | solution.py:597
  76.0 7.0 %all-to-all-start.2 = ((f32[128,16,128]{2,1,0:T(8,128)}), f32[128,16,128]{2,1,0:T(8,128)S(1)}, u32[]{:S(2)}, u32[]{:S(2)}) async-start(f32[128,16,128]{2,1,0:T(8,128)} %get-tuple-element.20), calls=%async_computation.2 | async-start | bytes 2097152 | tf_op jit(solution)/shard_map/all_to_all | solution.py:592
  83.1 1.1 collective-permute-start.3
  84.2 17.6 %all-to-all-done.2.leaf_ref = f32[128,16,128]{2,1,0:T(8,128)S(1)} async-done(((f32[128,16,128]{2,1,0:T(8,128)}), f32[128,16,128]{2,1,0:T(8,128)S(1)}, u32[]{:S(2)}, u32[]{:S(2)}) %all-to-all-start.2) | async-done | bytes 1048608 | tf_op jit(solution)/shard_map/all_to_all | solution.py:592
  101.8 0.0 copy-start.2
  101.8 1.0 copy-done.2
  102.8 0.0 copy-start
  102.8 11.3 %shard_map.126 = f32[3,4,128]{2,1,0:T(4,128)} custom-call(s32[4,128]{1,0:T(4,128)} %bitcast.28, f32[128,16,128]{2,1,0:T(8,128)} %copy-done.2, f32[3,4,128]{2,1,0:T(4,128)} %get-tuple-element.18.pos_ref, f32[3,4,128]{2,1,0:T(4,128)} %get-tuple-element.21.mid_ref), custom_call_target="tpu_custom_call" | custom-call | flops 6442450944 | bytes 1048576 | tf_op jit(solution)/shard_map/pallas_call | solution.py:484
  114.2 0.0 collective-permute-done.3
  114.2 0.0 copy-done
  114.2 17.4 %shard_map.127 = f32[3,128,128]{2,1,0:T(8,128)} custom-call(s32[1]{0:T(128)} %bitcast.13.core_ref, s32[8,128]{1,0:T(8,128)S(1)} %get-tuple-element.22.tab_ref, f32[64,2,8,128]{3,2,1,0:T(8,128)S(1)} %bitcast.18, f32[64,2,8,128]{3,2,1,0:T(8,128)S(1)} %bitcast.21, bf16[128,128,128]{2,1,0:T(8,128)(2,1)} %get-tuple-element.24.refs_0_, f32[3,128,128]{2,1,0:T(8,128)S(1)} %bitcast.20), custom_call_target="tpu_custom_call" | custom-call | flops 6442450944 | bytes 1048576 | tf_op jit(solution)/shard_map/pallas_call | solution.py:544
Async XLA Ops:
  2.5 25.0 %all-to-all-start = ((f32[128,8,128]{2,1,0:T(8,128)}), f32[128,8,128]{2,1,0:T(8,128)S(1)}, u32[]{:S(2)}, u32[]{:S(2)}) async-start(f32[128,8,128]{2,1,0:T(8,128)} %get-tuple-element.14), calls=%async_computation | async-start | bytes 1048576 | tf_op jit(solution)/shard_map/all_to_all | solution.py:585
  14.0 5.4 %collective-permute-start = (f32[8,512]{1,0:T(8,128)}, f32[8,512]{1,0:T(8,128)S(1)}, u32[]{:S(2)}, u32[]{:S(2)}) collective-permute-start(f32[8,512]{1,0:T(8,128)} %get-tuple-element.15.s0_ref.planes_ref), channel_id=1, source_target_pairs={{0,32},{32,64},{64,96},{96,0},{1,33},{33,65},{65,97},{97,1},{2,34}... | collective-permute-start | bytes 49160 | tf_op jit(solution)/shard_map/ppermute | solution.py:589
  15.5 5.2 %collective-permute-start.1 = (f32[8,512]{1,0:T(8,128)}, f32[8,512]{1,0:T(8,128)S(1)}, u32[]{:S(2)}, u32[]{:S(2)}) collective-permute-start(f32[8,512]{1,0:T(8,128)} %get-tuple-element.15.s0_ref.planes_ref), channel_id=1, source_target_pairs={{0,64},{32,96},{64,0},{96,32},{1,65},{33,97},{65,1},{97,33},{2,66}... | collective-permute-start | bytes 49160 | tf_op jit(solution)/shard_map/ppermute | solution.py:589
  18.4 4.0 %collective-permute-start.2 = (f32[8,512]{1,0:T(8,128)}, f32[8,512]{1,0:T(8,128)S(1)}, u32[]{:S(2)}, u32[]{:S(2)}) collective-permute-start(f32[8,512]{1,0:T(8,128)} %get-tuple-element.15.s0_ref.planes_ref), channel_id=1, source_target_pairs={{0,96},{32,0},{64,32},{96,64},{1,97},{33,1},{65,33},{97,65},{2,98}... | collective-permute-start | bytes 49160 | tf_op jit(solution)/shard_map/ppermute | solution.py:589
  27.5 0.7 copy-start.1
  59.0 17.0 %all-to-all-start.3 = ((f32[64,16,128]{2,1,0:T(8,128)}), f32[64,16,128]{2,1,0:T(8,128)S(1)}, u32[]{:S(2)}, u32[]{:S(2)}) async-start(f32[64,16,128]{2,1,0:T(8,128)} %get-tuple-element.23), calls=%async_computation.3 | async-start | bytes 1048576 | tf_op jit(solution)/shard_map/all_to_all | solution.py:597
  76.0 25.8 %all-to-all-start.2 = ((f32[128,16,128]{2,1,0:T(8,128)}), f32[128,16,128]{2,1,0:T(8,128)S(1)}, u32[]{:S(2)}, u32[]{:S(2)}) async-start(f32[128,16,128]{2,1,0:T(8,128)} %get-tuple-element.20), calls=%async_computation.2 | async-start | bytes 2097152 | tf_op jit(solution)/shard_map/all_to_all | solution.py:592
  83.1 31.1 %collective-permute-start.3 = (f32[64,16,128]{2,1,0:T(8,128)S(1)}, f32[64,16,128]{2,1,0:T(8,128)S(1)}, u32[]{:S(2)}, u32[]{:S(2)}) collective-permute-start(f32[64,16,128]{2,1,0:T(8,128)S(1)} %all-to-all-done.3), channel_id=1, source_target_pairs={{0,1},{1,0},{2,3},{3,2},{4,5},{5,4},{6,7},{7,6},{8,9},{9,8},{10,11... | collective-permute-start | bytes 1572872 | tf_op jit(solution)/shard_map/ppermute | solution.py:598
  101.8 1.0 copy-start.2
  102.8 11.4 %copy-start = (f32[128,3,128]{2,0,1:T(8,128)S(1)}, f32[128,3,128]{2,0,1:T(8,128)}, u32[]{:S(2)}) copy-start(f32[128,3,128]{2,0,1:T(8,128)} %param.18) | copy-start | bytes 589828

commit v5 on v4

--- a/solution.py
+++ b/solution.py
@@ -33,6 +33,12 @@
     r = x - a
     b = r.astype(BF16).astype(F32)
     return a, b, r - b
+
+
+def spread_scales(shape):
+    lane = lax.broadcasted_iota(I32, shape, 1) & 63
+    c = 1.0 + lane.astype(F32) * (1.0 / 128.0)
+    return c, c * c * lax.rsqrt(c)
 
 
 def predicted(pos, vel, acc, jerk):
@@ -110,18 +116,19 @@
         for k, ref in enumerate(refs):
             s = ref[...]
             row = lax.broadcasted_iota(I32, s.shape, 0)
-            s1, s2, s3 = split3(s)
+            scale, back = spread_scales(s.shape)
+            s1, s2, s3 = split3(s * scale)
             x = s[0:3]
             v = s[3:6]
-            n1, n2, n3 = split3(jnp.sum(x * x, 0, keepdims=True))
-            d1, d2, d3 = split3(jnp.sum(x * v, 0, keepdims=True))
-            one = jnp.ones_like(n1)
+            one = scale[0:1]
+            n1, n2, n3 = split3(jnp.sum(x * x, 0, keepdims=True) * one)
+            d1, d2, d3 = split3(jnp.sum(x * v, 0, keepdims=True) * one)
             zero7 = jnp.zeros((7, own), F32)
             tail = [one, one, one, n1, n2, n3, d1, d2, d3, zero7]
             big = jnp.concatenate([s1, s2, s3, s1, s2, s1] + tail, 0)
             rs_ref[k * own : (k + 1) * own, :] = big.T.astype(BF16)
             m = s[6:7]
-            g1, g2, g3 = split3(jnp.where(row == 6, m, s * m))
+            g1, g2, g3 = split3(jnp.where(row == 6, m, s * m) * back)
             b_ref[:, k * own : (k + 1) * own] = jnp.concatenate(
                 [g1, g2, g3, jnp.zeros_like(g1)], 0
             ).astype(BF16)
@@ -328,7 +335,7 @@
     lax.fori_loop(0, n, body, 0, unroll=8)
 
 
-def fetch(arrived, lo, steps=4):
+def fetch(arrived, lo, steps=2):
     nl = lo.shape[0]
     devices = arrived.shape[0]
     n = devices // steps
@@ -358,17 +365,17 @@
     r8 = lax.broadcasted_iota(I32, (8, 128), 0)
     low = r8 < 4
     q4 = r8 & 3
-    one = jnp.ones((8, 128), F32)
+    one, back = (jnp.ones((8, 128), F32),) * 2 if fine else spread_scales((8, 128))
     zero8 = jnp.zeros((8, 128), F32)
     zero64 = jnp.zeros((64, 128), BF16)
 
     def prep(g, b, j):
         s = bodies(g, j, low)
-        s1, s2, s3 = split3(s)
+        s1, s2, s3 = split3(s if fine else s * one)
         x2 = jnp.where(q4 == 3, 0.0, s * s)
         x2 = x2 + jnp.where((r8 & 1) == 0, pltpu.roll(x2, 7, 0), pltpu.roll(x2, 1, 0))
         x2 = x2 + jnp.where((r8 & 2) == 0, pltpu.roll(x2, 6, 0), pltpu.roll(x2, 2, 0))
-        n1, n2, n3 = split3(x2)
+        n1, n2, n3 = split3(x2 if fine else x2 * one)
         t1 = jnp.where(q4 == 0, n1, jnp.where(q4 == 1, n2, n3))
         m = jnp.where(
             low,
@@ -377,7 +384,8 @@
         )
         for q, t in enumerate((s1, s2, s3, t1)):
             t_ref[b, j, 8 * q : 8 * q + 8, :] = t
-        for q, t in enumerate(split3(jnp.where(q4 == 3, s, s * m))):
+        weighted = jnp.where(q4 == 3, s, s * m)
+        for q, t in enumerate(split3(weighted if fine else weighted * back)):
             s_ref[b, j, 8 * q : 8 * q + 8, :] = t
 
     def force(g, b, j):

time: 132 us -> 132 us (level)
  no operation moved by 1% of the time
where the time goes in v5:
time: 132 us; the launch traced here: 131 us
  Pallas kernels  58.9 us (45%)
  starting transfers between devices  29.3 us (22%)
  waiting for transfers between devices  28.7 us (22%)
  blocking collectives  12.1 us (9%)
  local copies, waits for them, and re-layouts  1.71 us (1%)
    all_to_all x1, waiting for transfers between devices, local(): leaves = lax.all_to_all(leaves, both, 0, 0, tiled=True)  17.6 us
    pallas_call x1, Pallas kernels, pulls(): pl.pallas_call(functools.partial(pull_kernel, G, scale, len(parts)), in_s...  17.4 us
    pallas_call x1, Pallas kernels, pair_terms(): pl.pallas_call(functools.partial(pair_kernel, width), grid_spec=pltpu.Pre...  16.6 us
    all_to_all x1, blocking collectives, local(): parts = lax.all_to_all(parts, 'col', 0, 0, tiled=True)  12.1 us
    all_to_all x1, starting transfers between devices, local(): arrived = lax.all_to_all(sent, both, 0, 0, tiled=True)  11.5 us
    pallas_call x1, Pallas kernels, kicks(): pl.pallas_call(functools.partial(kick_kernel, G), in_specs=[SMEM] + [VMEM...  11.5 us
    pallas_call x1, Pallas kernels, leaf_prep(): pl.pallas_call(functools.partial(leaf_kernel, part * nl), out_shape=(jax....  6.71 us
    all_to_all x1, starting transfers between devices, local(): leaves = lax.all_to_all(leaves, both, 0, 0, tiled=True)  6.61 us
  transfers between devices with their start and end apart: 7, of which 5 were waited for; matrix products, arithmetic and copies ran while one was open for 0% of the time, Pallas kernels for 16%

profile of v5, /device:TPU:1, one launch (start us, length us, event | category | flops | bytes accessed | tf_op | source)
XLA Modules:
  0.0 131.3 jit_solution(5009407393205143598)
XLA Ops:
  0.6 1.8 %shard_map.121 = (f32[8,512]{1,0:T(8,128)}, f32[128,8,128]{2,1,0:T(8,128)}, f32[16,128]{1,0:T(8,128)}, bf16[512,128]{1,0:T(8,128)(2,1)}) custom-call(f32[3,4,128]{2,1,0:T(4,128)} %bitcast.22, f32[3,4,128]{2,1,0:T(4,128)} %bitcast.23, f32[3,4,128]{2,1,0:T(4,128)} %bitcast.24, f32[3,4,128]{2,1,0:T(4,128)} %bitcast.25, f32[4,128]{1,0:T(4,128)} %mass_ref.2, ...), custom_call_target="tpu_custom_call" | custom-call | tf_op jit(solution)/shard_map/pallas_call | solution.py:95
  2.5 11.5 %all-to-all-start = ((f32[128,8,128]{2,1,0:T(8,128)}), f32[128,8,128]{2,1,0:T(8,128)S(1)}, u32[]{:S(2)}, u32[]{:S(2)}) async-start(f32[128,8,128]{2,1,0:T(8,128)} %get-tuple-element.14), calls=%async_computation | async-start | bytes 1048576 | tf_op jit(solution)/shard_map/all_to_all | solution.py:593
  14.0 1.6 %collective-permute-start = (f32[8,512]{1,0:T(8,128)}, f32[8,512]{1,0:T(8,128)S(1)}, u32[]{:S(2)}, u32[]{:S(2)}) collective-permute-start(f32[8,512]{1,0:T(8,128)} %get-tuple-element.15.s0_ref.planes_ref), channel_id=1, source_target_pairs={{0,32},{32,64},{64,96},{96,0},{1,33},{33,65},{65,97},{97,1},{2,34}... | collective-permute-start | bytes 49160 | tf_op jit(solution)/shard_map/ppermute | solution.py:597
  15.5 2.9 %collective-permute-start.1 = (f32[8,512]{1,0:T(8,128)}, f32[8,512]{1,0:T(8,128)S(1)}, u32[]{:S(2)}, u32[]{:S(2)}) collective-permute-start(f32[8,512]{1,0:T(8,128)} %get-tuple-element.15.s0_ref.planes_ref), channel_id=1, source_target_pairs={{0,64},{32,96},{64,0},{96,32},{1,65},{33,97},{65,1},{97,33},{2,66}... | collective-permute-start | bytes 49160 | tf_op jit(solution)/shard_map/ppermute | solution.py:597
  18.4 0.9 collective-permute-start.2
  19.4 0.0 collective-permute-done.s1_ref
  19.4 1.3 %collective-permute-done.1.s2_ref = f32[8,512]{1,0:T(8,128)S(1)} collective-permute-done((f32[8,512]{1,0:T(8,128)}, f32[8,512]{1,0:T(8,128)S(1)}, u32[]{:S(2)}, u32[]{:S(2)}) %collective-permute-start.1) | collective-permute-done | bytes 16416 | tf_op jit(solution)/shard_map/ppermute | solution.py:597
  20.7 1.7 %collective-permute-done.2.s3_ref = f32[8,512]{1,0:T(8,128)S(1)} collective-permute-done((f32[8,512]{1,0:T(8,128)}, f32[8,512]{1,0:T(8,128)S(1)}, u32[]{:S(2)}, u32[]{:S(2)}) %collective-permute-start.2) | collective-permute-done | bytes 16416 | tf_op jit(solution)/shard_map/ppermute | solution.py:597
  22.4 5.1 %all-to-all-done.act_ref.arrived_ref = f32[128,8,128]{2,1,0:T(8,128)S(1)} async-done(((f32[128,8,128]{2,1,0:T(8,128)}), f32[128,8,128]{2,1,0:T(8,128)S(1)}, u32[]{:S(2)}, u32[]{:S(2)}) %all-to-all-start) | async-done | bytes 524320 | tf_op jit(solution)/shard_map/all_to_all | solution.py:593
  27.5 0.0 copy-start.1
  27.5 0.7 copy-done.1
  28.2 16.6 %shard_map.122 = f32[32,8,128]{2,1,0:T(8,128)S(1)} custom-call(s32[1]{0:T(128)} %bitcast.row_ref, f32[128,8,128]{2,1,0:T(8,128)S(1)} %all-to-all-done.act_ref.arrived_ref, f32[8,512]{1,0:T(8,128)S(1)} %copy-done.1, f32[8,512]{1,0:T(8,128)S(1)} %collective-permute-done.s1_ref, f32[8,512]{1,0:T(8,128)S(1)} %collective-permute-done.1.s2_ref, ...), custom_call_target="tpu_custom_call" | custom-call | flops 8589934592 | bytes 262144 | tf_op jit(solution)/shard_map/pallas_call | solution.py:195
  44.9 12.1 %all_to_all.20.part_ref = f32[32,8,128]{2,1,0:T(8,128)} all-to-all(f32[32,8,128]{2,1,0:T(8,128)S(1)} %shard_map.122), channel_id=1, replica_groups=mesh['row'=4,'col'=32] {'col'}, dimensions={0} | all-to-all | bytes 262144 | tf_op jit(solution)/shard_map/all_to_all | solution.py:602
  57.0 2.0 %shard_map.123 = (f32[3,4,128]{2,1,0:T(4,128)}, f32[3,4,128]{2,1,0:T(4,128)}, f32[64,16,128]{2,1,0:T(8,128)}) custom-call(f32[32,8,128]{2,1,0:T(8,128)} %all_to_all.20.part_ref, f32[16,128]{1,0:T(8,128)} %get-tuple-element.16.start_ref, f32[8,512]{1,0:T(8,128)} %get-tuple-element.15.s0_ref.planes_ref, bf16[512,128]{1,0:T(8,128)(2,1)} %get-tuple-element.17.hot_ref), custom_call_target="tpu_custom_call" | custom-call | tf_op jit(solution)/shard_map/pallas_call | solution.py:252
  59.0 4.6 %all-to-all-start.3 = ((f32[64,16,128]{2,1,0:T(8,128)}), f32[64,16,128]{2,1,0:T(8,128)S(1)}, u32[]{:S(2)}, u32[]{:S(2)}) async-start(f32[64,16,128]{2,1,0:T(8,128)} %get-tuple-element.23), calls=%async_computation.3 | async-start | bytes 1048576 | tf_op jit(solution)/shard_map/all_to_all | solution.py:605
  63.7 6.7 %shard_map.124 = (bf16[128,128,128]{2,1,0:T(8,128)(2,1)}, f32[128,8,128]{2,1,0:T(8,128)}) custom-call(f32[3,128,128]{2,1,0:T(8,128)} %bitcast.19, f32[128,128]{1,0:T(8,128)} %mass_ref.3), custom_call_target="tpu_custom_call" | custom-call | flops 10000000 | bytes 3000000 | tf_op jit(solution)/shard_map/pallas_call | solution.py:291
  70.4 2.8 %shard_map.125 = (f32[128,16,128]{2,1,0:T(8,128)}, s32[8,128]{1,0:T(8,128)S(1)}) custom-call(f32[128,8,128]{2,1,0:T(8,128)S(1)} %all-to-all-done.act_ref.arrived_ref, f32[128,8,128]{2,1,0:T(8,128)} %get-tuple-element.19.far_ref), custom_call_target="tpu_custom_call" | custom-call | tf_op jit(solution)/shard_map/pallas_call | solution.py:342
  73.2 2.9 %all-to-all-done.3 = f32[64,16,128]{2,1,0:T(8,128)S(1)} async-done(((f32[64,16,128]{2,1,0:T(8,128)}), f32[64,16,128]{2,1,0:T(8,128)S(1)}, u32[]{:S(2)}, u32[]{:S(2)}) %all-to-all-start.3) | async-done | bytes 524320 | tf_op jit(solution)/shard_map/all_to_all | solution.py:605
  76.1 6.6 %all-to-all-start.2 = ((f32[128,16,128]{2,1,0:T(8,128)}), f32[128,16,128]{2,1,0:T(8,128)S(1)}, u32[]{:S(2)}, u32[]{:S(2)}) async-start(f32[128,16,128]{2,1,0:T(8,128)} %get-tuple-element.20), calls=%async_computation.2 | async-start | bytes 2097152 | tf_op jit(solution)/shard_map/all_to_all | solution.py:600
  82.7 1.1 collective-permute-start.3
  83.8 17.6 %all-to-all-done.2.leaf_ref = f32[128,16,128]{2,1,0:T(8,128)S(1)} async-done(((f32[128,16,128]{2,1,0:T(8,128)}), f32[128,16,128]{2,1,0:T(8,128)S(1)}, u32[]{:S(2)}, u32[]{:S(2)}) %all-to-all-start.2) | async-done | bytes 1048608 | tf_op jit(solution)/shard_map/all_to_all | solution.py:600
  101.5 0.0 copy-start.2
  101.5 1.0 copy-done.2
  102.4 0.0 copy-start
  102.4 11.5 %shard_map.126 = f32[3,4,128]{2,1,0:T(4,128)} custom-call(s32[4,128]{1,0:T(4,128)} %bitcast.28, f32[128,16,128]{2,1,0:T(8,128)} %copy-done.2, f32[3,4,128]{2,1,0:T(4,128)} %get-tuple-element.18.pos_ref, f32[3,4,128]{2,1,0:T(4,128)} %get-tuple-element.21.mid_ref), custom_call_target="tpu_custom_call" | custom-call | flops 6442450944 | bytes 1048576 | tf_op jit(solution)/shard_map/pallas_call | solution.py:492
  113.9 0.0 collective-permute-done.3
  113.9 0.0 copy-done
  113.9 17.4 %shard_map.127 = f32[3,128,128]{2,1,0:T(8,128)} custom-call(s32[1]{0:T(128)} %bitcast.13.core_ref, s32[8,128]{1,0:T(8,128)S(1)} %get-tuple-element.22.tab_ref, f32[64,2,8,128]{3,2,1,0:T(8,128)S(1)} %bitcast.18, f32[64,2,8,128]{3,2,1,0:T(8,128)S(1)} %bitcast.21, bf16[128,128,128]{2,1,0:T(8,128)(2,1)} %get-tuple-element.24.refs_0_, f32[3,128,128]{2,1,0:T(8,128)S(1)} %bitcast.20), custom_call_target="tpu_custom_call" | custom-call | flops 6442450944 | bytes 1048576 | tf_op jit(solution)/shard_map/pallas_call | solution.py:552
Async XLA Ops:
  2.5 25.0 %all-to-all-start = ((f32[128,8,128]{2,1,0:T(8,128)}), f32[128,8,128]{2,1,0:T(8,128)S(1)}, u32[]{:S(2)}, u32[]{:S(2)}) async-start(f32[128,8,128]{2,1,0:T(8,128)} %get-tuple-element.14), calls=%async_computation | async-start | bytes 1048576 | tf_op jit(solution)/shard_map/all_to_all | solution.py:593
  14.0 5.4 %collective-permute-start = (f32[8,512]{1,0:T(8,128)}, f32[8,512]{1,0:T(8,128)S(1)}, u32[]{:S(2)}, u32[]{:S(2)}) collective-permute-start(f32[8,512]{1,0:T(8,128)} %get-tuple-element.15.s0_ref.planes_ref), channel_id=1, source_target_pairs={{0,32},{32,64},{64,96},{96,0},{1,33},{33,65},{65,97},{97,1},{2,34}... | collective-permute-start | bytes 49160 | tf_op jit(solution)/shard_map/ppermute | solution.py:597
  15.5 5.2 %collective-permute-start.1 = (f32[8,512]{1,0:T(8,128)}, f32[8,512]{1,0:T(8,128)S(1)}, u32[]{:S(2)}, u32[]{:S(2)}) collective-permute-start(f32[8,512]{1,0:T(8,128)} %get-tuple-element.15.s0_ref.planes_ref), channel_id=1, source_target_pairs={{0,64},{32,96},{64,0},{96,32},{1,65},{33,97},{65,1},{97,33},{2,66}... | collective-permute-start | bytes 49160 | tf_op jit(solution)/shard_map/ppermute | solution.py:597
  18.4 4.0 %collective-permute-start.2 = (f32[8,512]{1,0:T(8,128)}, f32[8,512]{1,0:T(8,128)S(1)}, u32[]{:S(2)}, u32[]{:S(2)}) collective-permute-start(f32[8,512]{1,0:T(8,128)} %get-tuple-element.15.s0_ref.planes_ref), channel_id=1, source_target_pairs={{0,96},{32,0},{64,32},{96,64},{1,97},{33,1},{65,33},{97,65},{2,98}... | collective-permute-start | bytes 49160 | tf_op jit(solution)/shard_map/ppermute | solution.py:597
  27.5 0.7 copy-start.1
  59.0 17.0 %all-to-all-start.3 = ((f32[64,16,128]{2,1,0:T(8,128)}), f32[64,16,128]{2,1,0:T(8,128)S(1)}, u32[]{:S(2)}, u32[]{:S(2)}) async-start(f32[64,16,128]{2,1,0:T(8,128)} %get-tuple-element.23), calls=%async_computation.3 | async-start | bytes 1048576 | tf_op jit(solution)/shard_map/all_to_all | solution.py:605
  76.1 25.4 %all-to-all-start.2 = ((f32[128,16,128]{2,1,0:T(8,128)}), f32[128,16,128]{2,1,0:T(8,128)S(1)}, u32[]{:S(2)}, u32[]{:S(2)}) async-start(f32[128,16,128]{2,1,0:T(8,128)} %get-tuple-element.20), calls=%async_computation.2 | async-start | bytes 2097152 | tf_op jit(solution)/shard_map/all_to_all | solution.py:600
  82.7 31.3 %collective-permute-start.3 = (f32[64,16,128]{2,1,0:T(8,128)S(1)}, f32[64,16,128]{2,1,0:T(8,128)S(1)}, u32[]{:S(2)}, u32[]{:S(2)}) collective-permute-start(f32[64,16,128]{2,1,0:T(8,128)S(1)} %all-to-all-done.3), channel_id=1, source_target_pairs={{0,1},{1,0},{2,3},{3,2},{4,5},{5,4},{6,7},{7,6},{8,9},{9,8},{10,11... | collective-permute-start | bytes 1572872 | tf_op jit(solution)/shard_map/ppermute | solution.py:606
  101.5 1.0 copy-start.2
  102.4 11.5 %copy-start = (f32[128,3,128]{2,0,1:T(8,128)S(1)}, f32[128,3,128]{2,0,1:T(8,128)}, u32[]{:S(2)}) copy-start(f32[128,3,128]{2,0,1:T(8,128)} %param.18) | copy-start | bytes 589828

commit v6 on v5

--- a/solution.py
+++ b/solution.py
@@ -536,18 +536,13 @@
     ng = 4 * own_ref.shape[0] // G
     attract(G, ng, True, bodies, where, ready, g_ref, *scratch)
 
-    def finish(l, carry):
-        a = acc_ref[l]
-        a = a[0:4] + a[4:8]
-        for q in range(3):
-            g = gpos_ref[q, pl.ds(l, 1), :]
-            pull_ref[q, pl.ds(l, 1), :] = (a[q : q + 1] - g * a[3:4]) * scale
-        return carry
-
-    lax.fori_loop(0, g_ref.shape[0], finish, 0, unroll=8)
-
-
-def pulls(core, table, own, other, parts, gpos, scale, G=16):
+    weight = acc_ref[:, 3, :] + acc_ref[:, 7, :]
+    for q in range(3):
+        total = acc_ref[:, q, :] + acc_ref[:, 4 + q, :]
+        pull_ref[q] = (total - gpos_ref[q] * weight) * scale
+
+
+def pulls(core, table, own, other, parts, gpos, scale, G=32):
     nl = gpos.shape[1]
     return pl.pallas_call(
         functools.partial(pull_kernel, G, scale, len(parts)),

time: 132 us -> 132 us (level)
  no operation moved by 1% of the time
where the time goes in v6:
time: 132 us; the launch traced here: 131 us
  Pallas kernels  58.5 us (44%)
  starting transfers between devices  29.4 us (22%)
  waiting for transfers between devices  28.5 us (22%)
  blocking collectives  12.1 us (9%)
  local copies, waits for them, and re-layouts  1.71 us (1%)
    all_to_all x1, waiting for transfers between devices, local(): leaves = lax.all_to_all(leaves, both, 0, 0, tiled=True)  17.5 us
    pallas_call x1, Pallas kernels, pulls(): pl.pallas_call(functools.partial(pull_kernel, G, scale, len(parts)), in_s...  17 us
    pallas_call x1, Pallas kernels, pair_terms(): pl.pallas_call(functools.partial(pair_kernel, width), grid_spec=pltpu.Pre...  16.6 us
    all_to_all x1, blocking collectives, local(): parts = lax.all_to_all(parts, 'col', 0, 0, tiled=True)  12.1 us
    all_to_all x1, starting transfers between devices, local(): arrived = lax.all_to_all(sent, both, 0, 0, tiled=True)  11.5 us
    pallas_call x1, Pallas kernels, kicks(): pl.pallas_call(functools.partial(kick_kernel, G), in_specs=[SMEM] + [VMEM...  11.5 us
    pallas_call x1, Pallas kernels, leaf_prep(): pl.pallas_call(functools.partial(leaf_kernel, part * nl), out_shape=(jax....  6.71 us
    all_to_all x1, starting transfers between devices, local(): leaves = lax.all_to_all(leaves, both, 0, 0, tiled=True)  6.61 us
  transfers between devices with their start and end apart: 7, of which 5 were waited for; matrix products, arithmetic and copies ran while one was open for 0% of the time, Pallas kernels for 16%

profile of v6, /device:TPU:1, one launch (start us, length us, event | category | flops | bytes accessed | tf_op | source)
XLA Modules:
  0.0 131.1 jit_solution(8598767525947950826)
XLA Ops:
  0.6 1.8 %shard_map.121 = (f32[8,512]{1,0:T(8,128)}, f32[128,8,128]{2,1,0:T(8,128)}, f32[16,128]{1,0:T(8,128)}, bf16[512,128]{1,0:T(8,128)(2,1)}) custom-call(f32[3,4,128]{2,1,0:T(4,128)} %bitcast.22, f32[3,4,128]{2,1,0:T(4,128)} %bitcast.23, f32[3,4,128]{2,1,0:T(4,128)} %bitcast.24, f32[3,4,128]{2,1,0:T(4,128)} %bitcast.25, f32[4,128]{1,0:T(4,128)} %mass_ref.2, ...), custom_call_target="tpu_custom_call" | custom-call | tf_op jit(solution)/shard_map/pallas_call | solution.py:95
  2.5 11.5 %all-to-all-start = ((f32[128,8,128]{2,1,0:T(8,128)}), f32[128,8,128]{2,1,0:T(8,128)S(1)}, u32[]{:S(2)}, u32[]{:S(2)}) async-start(f32[128,8,128]{2,1,0:T(8,128)} %get-tuple-element.14), calls=%async_computation | async-start | bytes 1048576 | tf_op jit(solution)/shard_map/all_to_all | solution.py:588
  14.0 1.6 %collective-permute-start = (f32[8,512]{1,0:T(8,128)}, f32[8,512]{1,0:T(8,128)S(1)}, u32[]{:S(2)}, u32[]{:S(2)}) collective-permute-start(f32[8,512]{1,0:T(8,128)} %get-tuple-element.15.s0_ref.planes_ref), channel_id=1, source_target_pairs={{0,32},{32,64},{64,96},{96,0},{1,33},{33,65},{65,97},{97,1},{2,34}... | collective-permute-start | bytes 49160 | tf_op jit(solution)/shard_map/ppermute | solution.py:592
  15.5 2.9 %collective-permute-start.1 = (f32[8,512]{1,0:T(8,128)}, f32[8,512]{1,0:T(8,128)S(1)}, u32[]{:S(2)}, u32[]{:S(2)}) collective-permute-start(f32[8,512]{1,0:T(8,128)} %get-tuple-element.15.s0_ref.planes_ref), channel_id=1, source_target_pairs={{0,64},{32,96},{64,0},{96,32},{1,65},{33,97},{65,1},{97,33},{2,66}... | collective-permute-start | bytes 49160 | tf_op jit(solution)/shard_map/ppermute | solution.py:592
  18.4 0.9 collective-permute-start.2
  19.4 0.0 collective-permute-done.s1_ref
  19.4 1.3 %collective-permute-done.1.s2_ref = f32[8,512]{1,0:T(8,128)S(1)} collective-permute-done((f32[8,512]{1,0:T(8,128)}, f32[8,512]{1,0:T(8,128)S(1)}, u32[]{:S(2)}, u32[]{:S(2)}) %collective-permute-start.1) | collective-permute-done | bytes 16416 | tf_op jit(solution)/shard_map/ppermute | solution.py:592
  20.7 1.7 %collective-permute-done.2.s3_ref = f32[8,512]{1,0:T(8,128)S(1)} collective-permute-done((f32[8,512]{1,0:T(8,128)}, f32[8,512]{1,0:T(8,128)S(1)}, u32[]{:S(2)}, u32[]{:S(2)}) %collective-permute-start.2) | collective-permute-done | bytes 16416 | tf_op jit(solution)/shard_map/ppermute | solution.py:592
  22.4 5.1 %all-to-all-done.act_ref.arrived_ref = f32[128,8,128]{2,1,0:T(8,128)S(1)} async-done(((f32[128,8,128]{2,1,0:T(8,128)}), f32[128,8,128]{2,1,0:T(8,128)S(1)}, u32[]{:S(2)}, u32[]{:S(2)}) %all-to-all-start) | async-done | bytes 524320 | tf_op jit(solution)/shard_map/all_to_all | solution.py:588
  27.5 0.0 copy-start.1
  27.5 0.7 copy-done.1
  28.2 16.6 %shard_map.122 = f32[32,8,128]{2,1,0:T(8,128)S(1)} custom-call(s32[1]{0:T(128)} %bitcast.row_ref, f32[128,8,128]{2,1,0:T(8,128)S(1)} %all-to-all-done.act_ref.arrived_ref, f32[8,512]{1,0:T(8,128)S(1)} %copy-done.1, f32[8,512]{1,0:T(8,128)S(1)} %collective-permute-done.s1_ref, f32[8,512]{1,0:T(8,128)S(1)} %collective-permute-done.1.s2_ref, ...), custom_call_target="tpu_custom_call" | custom-call | flops 8589934592 | bytes 262144 | tf_op jit(solution)/shard_map/pallas_call | solution.py:195
  44.9 12.1 %all_to_all.20.part_ref = f32[32,8,128]{2,1,0:T(8,128)} all-to-all(f32[32,8,128]{2,1,0:T(8,128)S(1)} %shard_map.122), channel_id=1, replica_groups=mesh['row'=4,'col'=32] {'col'}, dimensions={0} | all-to-all | bytes 262144 | tf_op jit(solution)/shard_map/all_to_all | solution.py:597
  57.0 2.0 %shard_map.123 = (f32[3,4,128]{2,1,0:T(4,128)}, f32[3,4,128]{2,1,0:T(4,128)}, f32[64,16,128]{2,1,0:T(8,128)}) custom-call(f32[32,8,128]{2,1,0:T(8,128)} %all_to_all.20.part_ref, f32[16,128]{1,0:T(8,128)} %get-tuple-element.16.start_ref, f32[8,512]{1,0:T(8,128)} %get-tuple-element.15.s0_ref.planes_ref, bf16[512,128]{1,0:T(8,128)(2,1)} %get-tuple-element.17.hot_ref), custom_call_target="tpu_custom_call" | custom-call | tf_op jit(solution)/shard_map/pallas_call | solution.py:252
  59.0 4.6 %all-to-all-start.3 = ((f32[64,16,128]{2,1,0:T(8,128)}), f32[64,16,128]{2,1,0:T(8,128)S(1)}, u32[]{:S(2)}, u32[]{:S(2)}) async-start(f32[64,16,128]{2,1,0:T(8,128)} %get-tuple-element.23), calls=%async_computation.3 | async-start | bytes 1048576 | tf_op jit(solution)/shard_map/all_to_all | solution.py:600
  63.7 6.7 %shard_map.124 = (bf16[128,128,128]{2,1,0:T(8,128)(2,1)}, f32[128,8,128]{2,1,0:T(8,128)}) custom-call(f32[3,128,128]{2,1,0:T(8,128)} %bitcast.19, f32[128,128]{1,0:T(8,128)} %mass_ref.3), custom_call_target="tpu_custom_call" | custom-call | flops 10000000 | bytes 3000000 | tf_op jit(solution)/shard_map/pallas_call | solution.py:291
  70.4 2.8 %shard_map.125 = (f32[128,16,128]{2,1,0:T(8,128)}, s32[8,128]{1,0:T(8,128)S(1)}) custom-call(f32[128,8,128]{2,1,0:T(8,128)S(1)} %all-to-all-done.act_ref.arrived_ref, f32[128,8,128]{2,1,0:T(8,128)} %get-tuple-element.19.far_ref), custom_call_target="tpu_custom_call" | custom-call | tf_op jit(solution)/shard_map/pallas_call | solution.py:342
  73.2 2.9 %all-to-all-done.3 = f32[64,16,128]{2,1,0:T(8,128)S(1)} async-done(((f32[64,16,128]{2,1,0:T(8,128)}), f32[64,16,128]{2,1,0:T(8,128)S(1)}, u32[]{:S(2)}, u32[]{:S(2)}) %all-to-all-start.3) | async-done | bytes 524320 | tf_op jit(solution)/shard_map/all_to_all | solution.py:600
  76.1 6.6 %all-to-all-start.2 = ((f32[128,16,128]{2,1,0:T(8,128)}), f32[128,16,128]{2,1,0:T(8,128)S(1)}, u32[]{:S(2)}, u32[]{:S(2)}) async-start(f32[128,16,128]{2,1,0:T(8,128)} %get-tuple-element.20), calls=%async_computation.2 | async-start | bytes 2097152 | tf_op jit(solution)/shard_map/all_to_all | solution.py:595
  82.7 1.3 %collective-permute-start.3 = (f32[64,16,128]{2,1,0:T(8,128)S(1)}, f32[64,16,128]{2,1,0:T(8,128)S(1)}, u32[]{:S(2)}, u32[]{:S(2)}) collective-permute-start(f32[64,16,128]{2,1,0:T(8,128)S(1)} %all-to-all-done.3), channel_id=1, source_target_pairs={{0,1},{1,0},{2,3},{3,2},{4,5},{5,4},{6,7},{7,6},{8,9},{9,8},{10,11... | collective-permute-start | bytes 1572872 | tf_op jit(solution)/shard_map/ppermute | solution.py:601
  84.0 17.5 %all-to-all-done.2.leaf_ref = f32[128,16,128]{2,1,0:T(8,128)S(1)} async-done(((f32[128,16,128]{2,1,0:T(8,128)}), f32[128,16,128]{2,1,0:T(8,128)S(1)}, u32[]{:S(2)}, u32[]{:S(2)}) %all-to-all-start.2) | async-done | bytes 1048608 | tf_op jit(solution)/shard_map/all_to_all | solution.py:595
  101.5 0.0 copy-start.2
  101.5 1.0 copy-done.2
  102.4 0.0 copy-start
  102.4 11.5 %shard_map.126 = f32[3,4,128]{2,1,0:T(4,128)} custom-call(s32[4,128]{1,0:T(4,128)} %bitcast.28, f32[128,16,128]{2,1,0:T(8,128)} %copy-done.2, f32[3,4,128]{2,1,0:T(4,128)} %get-tuple-element.18.pos_ref, f32[3,4,128]{2,1,0:T(4,128)} %get-tuple-element.21.mid_ref), custom_call_target="tpu_custom_call" | custom-call | flops 6442450944 | bytes 1048576 | tf_op jit(solution)/shard_map/pallas_call | solution.py:492
  113.9 0.0 collective-permute-done.3
  113.9 0.0 copy-done
  113.9 17.0 %shard_map.127 = f32[3,128,128]{2,1,0:T(8,128)} custom-call(s32[1]{0:T(128)} %bitcast.13.core_ref, s32[8,128]{1,0:T(8,128)S(1)} %get-tuple-element.22.tab_ref, f32[64,2,8,128]{3,2,1,0:T(8,128)S(1)} %bitcast.18, f32[64,2,8,128]{3,2,1,0:T(8,128)S(1)} %bitcast.21, bf16[128,128,128]{2,1,0:T(8,128)(2,1)} %get-tuple-element.24.refs_0_, f32[3,128,128]{2,1,0:T(8,128)S(1)} %bitcast.20), custom_call_target="tpu_custom_call" | custom-call | flops 6442450944 | bytes 1048576 | tf_op jit(solution)/shard_map/pallas_call | solution.py:547
Async XLA Ops:
  2.5 25.0 %all-to-all-start = ((f32[128,8,128]{2,1,0:T(8,128)}), f32[128,8,128]{2,1,0:T(8,128)S(1)}, u32[]{:S(2)}, u32[]{:S(2)}) async-start(f32[128,8,128]{2,1,0:T(8,128)} %get-tuple-element.14), calls=%async_computation | async-start | bytes 1048576 | tf_op jit(solution)/shard_map/all_to_all | solution.py:588
  14.0 5.4 %collective-permute-start = (f32[8,512]{1,0:T(8,128)}, f32[8,512]{1,0:T(8,128)S(1)}, u32[]{:S(2)}, u32[]{:S(2)}) collective-permute-start(f32[8,512]{1,0:T(8,128)} %get-tuple-element.15.s0_ref.planes_ref), channel_id=1, source_target_pairs={{0,32},{32,64},{64,96},{96,0},{1,33},{33,65},{65,97},{97,1},{2,34}... | collective-permute-start | bytes 49160 | tf_op jit(solution)/shard_map/ppermute | solution.py:592
  15.5 5.2 %collective-permute-start.1 = (f32[8,512]{1,0:T(8,128)}, f32[8,512]{1,0:T(8,128)S(1)}, u32[]{:S(2)}, u32[]{:S(2)}) collective-permute-start(f32[8,512]{1,0:T(8,128)} %get-tuple-element.15.s0_ref.planes_ref), channel_id=1, source_target_pairs={{0,64},{32,96},{64,0},{96,32},{1,65},{33,97},{65,1},{97,33},{2,66}... | collective-permute-start | bytes 49160 | tf_op jit(solution)/shard_map/ppermute | solution.py:592
  18.4 4.0 %collective-permute-start.2 = (f32[8,512]{1,0:T(8,128)}, f32[8,512]{1,0:T(8,128)S(1)}, u32[]{:S(2)}, u32[]{:S(2)}) collective-permute-start(f32[8,512]{1,0:T(8,128)} %get-tuple-element.15.s0_ref.planes_ref), channel_id=1, source_target_pairs={{0,96},{32,0},{64,32},{96,64},{1,97},{33,1},{65,33},{97,65},{2,98}... | collective-permute-start | bytes 49160 | tf_op jit(solution)/shard_map/ppermute | solution.py:592
  27.5 0.7 copy-start.1
  59.0 17.0 %all-to-all-start.3 = ((f32[64,16,128]{2,1,0:T(8,128)}), f32[64,16,128]{2,1,0:T(8,128)S(1)}, u32[]{:S(2)}, u32[]{:S(2)}) async-start(f32[64,16,128]{2,1,0:T(8,128)} %get-tuple-element.23), calls=%async_computation.3 | async-start | bytes 1048576 | tf_op jit(solution)/shard_map/all_to_all | solution.py:600
  76.1 25.4 %all-to-all-start.2 = ((f32[128,16,128]{2,1,0:T(8,128)}), f32[128,16,128]{2,1,0:T(8,128)S(1)}, u32[]{:S(2)}, u32[]{:S(2)}) async-start(f32[128,16,128]{2,1,0:T(8,128)} %get-tuple-element.20), calls=%async_computation.2 | async-start | bytes 2097152 | tf_op jit(solution)/shard_map/all_to_all | solution.py:595
  82.7 31.3 %collective-permute-start.3 = (f32[64,16,128]{2,1,0:T(8,128)S(1)}, f32[64,16,128]{2,1,0:T(8,128)S(1)}, u32[]{:S(2)}, u32[]{:S(2)}) collective-permute-start(f32[64,16,128]{2,1,0:T(8,128)S(1)} %all-to-all-done.3), channel_id=1, source_target_pairs={{0,1},{1,0},{2,3},{3,2},{4,5},{5,4},{6,7},{7,6},{8,9},{9,8},{10,11... | collective-permute-start | bytes 1572872 | tf_op jit(solution)/shard_map/ppermute | solution.py:601
  101.5 1.0 copy-start.2
  102.4 11.5 %copy-start = (f32[128,3,128]{2,0,1:T(8,128)S(1)}, f32[128,3,128]{2,0,1:T(8,128)}, u32[]{:S(2)}) copy-start(f32[128,3,128]{2,0,1:T(8,128)} %param.18) | copy-start | bytes 589828
